TPU v7x, 128 devices: a whole 4x4x4 slice. The times are simulated.
128 devices in a mesh: row: 16 (over x, y), col: 8 (over z, core).
Axes of the slice: x: 4, y: 4, z: 4, core: 2. Of those that a mesh axis runs over, the one named last changes fastest.
Arguments:
- density: bfloat16 [16384, 16384], P('row', 'col'), as said below
- block_mask: int32 [128, 128], P('row', 'col'), may hold values from 0 to 1, as said below
Outputs:
- purified_slab: float32 [1024, 16384], P('col', 'row')
Inputs may be any that keep to these rules, and one draw needn't show every extreme that they name: density is exactly symmetric. block_mask is symmetric and its diagonal is all ones.
All inputs are finite; a program needn't handle non-finite values.
Results may differ from a plain program's by a relative error of at most 0.0018.
Values may be sent and summed in bfloat16 or wider, within the bound.
No kernel may reach another device: no remote copies, remote signals or barrier semaphores. Data moves between devices by JAX's collectives and lax.ppermute only.
A program may use at most 128 MiB of HBM per device.

v0:
```python
import functools

import jax
import jax.numpy as jnp
from jax import lax
from jax.experimental import pallas as pl
from jax.experimental.pallas import tpu as pltpu
from jax.sharding import Mesh
from jax.sharding import PartitionSpec as P

BLOCK = 128
SLAB = 1024
WIDE = 2048
LANES = 128
QUARTER = SLAB // 4
PIECE = SLAB // 16
AXES = ("x", "y", "z", "core")
F32, BF16, I16, I32 = jnp.float32, jnp.bfloat16, jnp.int16, jnp.int32

DEVICES = [(x, y, z, c) for x in range(4) for y in range(4) for z in range(4) for c in range(2)]


def turns(x, y):
    late = {(x + 2) % 4, (y + 2) % 4}
    return [q for q in range(4) if q not in late] + sorted(late)


def facts(x, y, z, core):
    first, second = (y, x) if core else (x, y)
    own = first + z
    quarters = [(own + d) % 4 for d in range(4)]
    chosen = [(first - q) % 4 for q in turns(x, y)]
    row = x * 4 + y
    source = 0 if z == 0 else 1 if z == 1 + 2 * core else 3 if z == 2 else 2
    own_square = int(z * 2 + core == row // 2)
    return [*quarters, *chosen, second, core, own_square, row % 2, source, 0, 0, 0]


QUARTERS, CHOSEN, SECOND, CORE, OWNER, HALF, SOURCE = 0, 4, 8, 9, 10, 11, 12


def shape(rows, columns, dtype):
    return jax.ShapeDtypeStruct((rows, columns), dtype)


def call(kernel, out, s, *args, flops=1 << 22, scratch=()):
    in_vmem = pl.BlockSpec(memory_space=pltpu.VMEM)
    return pl.pallas_call(
        kernel,
        out_shape=out,
        in_specs=[pl.BlockSpec(memory_space=pltpu.SMEM)] * len(s) + [in_vmem] * len(args),
        out_specs=jax.tree.map(lambda _: in_vmem, out),
        scratch_shapes=list(scratch),
        compiler_params=pltpu.CompilerParams(vmem_limit_bytes=16 << 20),
        cost_estimate=pl.CostEstimate(flops=flops, bytes_accessed=4 << 20, transcendentals=0),
    )(*s, *args)


def encode(v):
    top = jnp.max(jnp.abs(v), axis=1, keepdims=True)
    e = jnp.clip(jnp.floor(jnp.log2(top)) + 1.0, -100.0, 128.0)
    q = jnp.clip(jnp.round(v * jnp.exp2(15.0 - e)), -32767.0, 32767.0)
    tail = jnp.broadcast_to(e, (v.shape[0], LANES))
    return q.astype(I32).astype(I16), tail.astype(I32).astype(I16)


def put(ref, v):
    q, tail = encode(v)
    width = v.shape[1]
    ref[:, :width] = q
    ref[:, width:] = tail


def take(ref, rows=slice(None)):
    width = ref.shape[1] - LANES
    e = ref[rows, width:].astype(I32).astype(F32)
    scale = jnp.exp2(e - 15.0)[:, :1]
    return ref[rows, :width].astype(I32).astype(F32) * scale


def at(i, size):
    return pl.ds(pl.multiple_of(i * size, size), size)


def masked_block(m, density, i, j):
    block = density[i * BLOCK : (i + 1) * BLOCK, j * BLOCK : (j + 1) * BLOCK]
    return jnp.where(m[i, j] != 0, block, jnp.zeros_like(block))


def column_kernel(m, hbm, *refs):
    *outs, density, sem = refs
    copies = []
    for i in range(4):
        rows = slice(i * 256, (i + 1) * 256)
        copies.append(pltpu.make_async_copy(hbm.at[rows, :SLAB], density.at[rows], sem.at[i]))
        copies[i].start()
    for i in range(8):
        if i % 2 == 0:
            copies[i // 2].wait()
        rows = slice(i % 4 * BLOCK, (i % 4 + 1) * BLOCK)
        for j in range(8):
            out = outs[i // 4 + j // 4 * 2]
            out[rows, j % 4 * BLOCK : (j % 4 + 1) * BLOCK] = masked_block(m, density, i, j)


def mask_kernel(m, density, out):
    for i in range(8):
        for j in range(16):
            out[i * BLOCK : (i + 1) * BLOCK, j * BLOCK : (j + 1) * BLOCK] = masked_block(m, density, i, j)


def first_kernel(d, s, own_a, other_a, own_b, other_b, masked, *refs):
    *outs, left, acc = refs
    quarter = s[QUARTERS + d]
    for half, (own, other) in enumerate(((own_a, other_a), (own_b, other_b))):

        @pl.when(quarter // 2 == half)
        def _(own=own, other=other):
            left[:512] = own[:, at(quarter % 2, QUARTER)]
            left[512:] = other[:, at(quarter % 2, QUARTER)]

    dims = (((0,), (0,)), ((), ()))
    to = acc if d == 2 else outs[0]
    for n in range(4):
        columns = slice(n * 512, (n + 1) * 512)
        to[:, columns] = lax.dot_general(
            left[:512], masked[at(s[CORE], 512), columns], dims, preferred_element_type=F32
        ) + lax.dot_general(
            left[512:], masked[at(1 - s[CORE], 512), columns], dims, preferred_element_type=F32
        )
    if d == 2:
        put(outs[0], acc[:128])
        put(outs[1], acc[128:])


def first_product(d, s, parts, masked):
    out = [shape(128, WIDE + LANES, I16)] * 2 if d == 2 else shape(QUARTER, WIDE, F32)
    return call(
        functools.partial(first_kernel, d),
        out,
        [s],
        *parts,
        masked,
        flops=2 * QUARTER * SLAB * WIDE,
        scratch=[pltpu.VMEM((SLAB, QUARTER), BF16), pltpu.VMEM((QUARTER, WIDE), F32)],
    )


def push_kernel(start, mine, came, out):
    add = slice(start, start + 128)
    rest = slice(128 - start, 256 - start)
    put(out.at[add], mine[add, :] + take(came))
    put(out.at[rest], mine[rest, :])


def spread_kernel(s, own, a, b, *outs):
    for d, out in enumerate(outs):
        rows = at((s[SECOND] + d) % 4, PIECE)
        v = own[rows, :] + take(a, rows) + take(b, rows)
        if d == 0:
            out[...] = v
        else:
            put(out, v)


def gather_kernel(own, a, b, c, out):
    put(out, own[...] + take(a) + take(b) + take(c))


def join_kernel(*refs):
    *parts, out = refs
    for i, part in enumerate(parts):
        out[i * PIECE : (i + 1) * PIECE] = part[...]


def second_kernel(i, s, *refs):
    *quarters, masked, mine, theirs, left, triple = refs
    own, back, ahead, *far = quarters
    d = s[CHOSEN + i]
    starts = []
    for j in range(4):
        sub = (s[SECOND] + 4 - j) % 4
        starts.append(((sub // 2) ^ s[CORE]) * 128 + (sub % 2) * 64)

    def unpack(refs):
        for j, start in enumerate(starts):
            size = refs[0].shape[0]
            ref, first = refs[j * PIECE // size], j * PIECE % size
            v = take(ref, slice(first, first + PIECE))
            rows = pl.ds(pl.multiple_of(start, 64), PIECE)
            left[rows, :] = v.astype(BF16)
            for half in range(2):

                @pl.when((s[OWNER] == 1) & (s[HALF] == half))
                def _(v=v, rows=rows, half=half):
                    triple[rows, :] = 3.0 * v[:, half * SLAB : (half + 1) * SLAB]

    for shift, refs in ((0, [own]), (1, [back]), (3, [ahead]), (2, far)):
        if refs:
            pl.when(d == shift)(functools.partial(unpack, refs))
    for n in range(4):
        columns = slice(n * 256, (n + 1) * 256)
        t = -2.0 * lax.dot_general(
            left[...],
            masked[columns, :],
            (((1,), (1,)), ((), ())),
            preferred_element_type=F32,
        )
        mine[:, columns] = t[:128]
        theirs[:, columns] = t[128:]

    @pl.when(s[OWNER] == 1)
    def _():
        mine[...] += triple[:128]
        theirs[...] += triple[128:]


def second_product(i, s, quarters, masked):
    return call(
        functools.partial(second_kernel, i),
        [shape(128, SLAB, F32)] * 2,
        [s],
        *quarters,
        masked,
        flops=2 * QUARTER * SLAB * WIDE,
        scratch=[pltpu.VMEM((QUARTER, WIDE), BF16), pltpu.VMEM((QUARTER, SLAB), F32)],
    )


def pair_kernel(mine, came, out):
    put(out, mine[...] + came[...])


def finish_kernel(a, b, c, d, out):
    out[...] = take(a) + take(b) + take(c) + take(d)


def place(x, y, z, core):
    return ((x % 4 * 4 + y % 4) * 4 + z % 4) * 2 + core


def send(v, to):
    return lax.ppermute(v, AXES, [(place(*d), place(*to(*d))) for d in DEVICES])


def along(v, d):
    return send(v, lambda x, y, z, core: (x, y + d, z, core) if core else (x + d, y, z, core))


def across(v, d):
    return send(v, lambda x, y, z, core: (x + d, y, z, core) if core else (x, y + d, z, core))


def swap(v):
    return lax.ppermute(v, "core", [(0, 1), (1, 0)])


def pick_kernel(key, s, *refs):
    *parts, out = refs
    for i, part in enumerate(parts):

        @pl.when(s[key] == i)
        def _(part=part):
            out[...] = part[...]


def pick(key, s, *parts):
    out = shape(*parts[0].shape, parts[0].dtype)
    return call(functools.partial(pick_kernel, key), out, [s], *parts)


def spread_column(s, top, low):
    half = pick(CORE, s, top, lax.ppermute(low, "core", [(0, 1), (1, 0)]))
    axes = ("z", "core")
    one = lax.ppermute(half, axes, [(0, 2), (1, 7)])
    two = lax.ppermute(half, axes, [(0, 6), (1, 3)])
    three = lax.ppermute(one, axes, [(2, 4), (7, 5)])
    half = pick(SOURCE, s, half, one, two, three)
    return half, swap(half)


def local(density, block_mask):
    table = jnp.asarray([facts(*d) for d in DEVICES], I32)
    s = lax.dynamic_index_in_dim(table, lax.axis_index(AXES), 0, False)
    top_a, low_a, top_b, low_b = pl.pallas_call(
        column_kernel,
        out_shape=[shape(512, 512, BF16)] * 4,
        in_specs=[pl.BlockSpec(memory_space=pltpu.SMEM), pl.BlockSpec(memory_space=pltpu.HBM)],
        out_specs=[pl.BlockSpec(memory_space=pltpu.VMEM)] * 4,
        scratch_shapes=[pltpu.VMEM((SLAB, SLAB), BF16), pltpu.SemaphoreType.DMA((4,))],
        compiler_params=pltpu.CompilerParams(vmem_limit_bytes=60 << 20),
        name="column",
    )(block_mask, density)
    masked = call(mask_kernel, shape(SLAB, WIDE, BF16), [block_mask], density)
    parts = spread_column(s, top_a, low_a)
    parts += spread_column(s, top_b, low_b)

    wide = shape(QUARTER, WIDE + LANES, I16)
    top, low = first_product(2, s, parts, masked)
    top = along(top, 1)
    low = along(low, -1)
    ahead, back, mine = (first_product(d, s, parts, masked) for d in (1, 3, 0))
    ahead = call(functools.partial(push_kernel, 0), wide, [], ahead, top)
    ahead = along(ahead, 1)
    back = call(functools.partial(push_kernel, 128), wide, [], back, low)
    back = along(back, -1)
    coded = shape(PIECE, WIDE + LANES, I16)
    outs = [shape(PIECE, WIDE, F32), coded, coded, coded]
    mine, *pieces = call(spread_kernel, outs, [s], mine, ahead, back)
    came = [across(pieces[d - 1], d) for d in (2, 1, 3)]
    v = call(gather_kernel, coded, [], mine, *came)

    pieces = [across(v, d) for d in (1, 2, 3)]
    own = call(join_kernel, wide, [], v, *pieces)
    back, ahead = along(own, 1), along(own, -1)
    top = along(back[:128], 1)
    low = along(ahead[128:], -1)
    came = []
    for i in range(4):
        quarters = [own, back, ahead] + [top, low] * (i >= 2)
        mine, theirs = second_product(i, s, quarters, masked)
        theirs = swap(theirs)
        v = call(pair_kernel, shape(128, SLAB + LANES, I16), [], mine, theirs)
        came.append(send(v, lambda x, y, z, core: (x, y, z + turns(x, y)[i], core)))
    return call(finish_kernel, shape(128, SLAB, F32), [], *came)


def solution(mesh):
    torus = Mesh(mesh.devices.reshape(4, 4, 4, 2), AXES)
    in_specs = (P(("x", "y"), ("z", "core")),) * 2
    out_specs = P(("z", "core"), ("x", "y"))
    return jax.shard_map(local, mesh=torus, in_specs=in_specs, out_specs=out_specs, check_vma=False)
```

profile of v0, /device:TPU:0, one launch (start us, length us, event | category | flops | bytes accessed | tf_op | source)
XLA Modules:
  0.0 167.2 jit_solution(1954815068314281343)
XLA Ops:
  0.0 3.7 %column.1 = (bf16[512,512]{1,0:T(8,128)(2,1)}, bf16[512,512]{1,0:T(8,128)(2,1)}, bf16[512,512]{1,0:T(8,128)(2,1)}, bf16[512,512]{1,0:T(8,128)(2,1)}) custom-call(s32[8,16]{1,0:T(8,128)} %m.3, bf16[1024,2048]{1,0:T(8,128)(2,1)} %density.1), custom_call_target="tpu_custom_call" | custom-call | tf_op jit(solution)/shard_map/column/pallas_call | solution.py:285
  4.3 0.7 dynamic-slice_bitcast_fusion.s
  5.0 0.9 collective-permute-done.refs_1_
  5.9 1.0 copy-done.2
  7.6 4.0 %collective-permute-start.1 = (bf16[512,512]{1,0:T(8,128)(2,1)S(1)}, bf16[512,512]{1,0:T(8,128)(2,1)S(1)}, u32[]{:S(2)}, u32[]{:S(2)}) collective-permute-start(bf16[512,512]{1,0:T(8,128)(2,1)S(1)} %shard_map.37.refs_0_), channel_id=1, source_target_pairs={{0,2},{1,7},{8,10},{9,15},{16,18},{17,23},{24,26},{25,31},{32,34},... | collective-permute-start | bytes 1572872 | tf_op jit(solution)/shard_map/ppermute | solution.py:275
  12.2 1.3 collective-permute-start.6
  13.5 2.2 %collective-permute-start.2 = (bf16[512,512]{1,0:T(8,128)(2,1)S(1)}, bf16[512,512]{1,0:T(8,128)(2,1)S(1)}, u32[]{:S(2)}, u32[]{:S(2)}) collective-permute-start(bf16[512,512]{1,0:T(8,128)(2,1)S(1)} %shard_map.37.refs_0_), channel_id=1, source_target_pairs={{0,6},{1,3},{8,14},{9,11},{16,22},{17,19},{24,30},{25,27},{32,38},... | collective-permute-start | bytes 1572872 | tf_op jit(solution)/shard_map/ppermute | solution.py:276
  15.7 3.6 %collective-permute-done.1.refs_1_ = bf16[512,512]{1,0:T(8,128)(2,1)S(1)} collective-permute-done((bf16[512,512]{1,0:T(8,128)(2,1)S(1)}, bf16[512,512]{1,0:T(8,128)(2,1)S(1)}, u32[]{:S(2)}, u32[]{:S(2)}) %collective-permute-start.1) | collective-permute-done | bytes 524320 | tf_op jit(solution)/shard_map/ppermute | solution.py:275
  19.9 1.3 collective-permute-start.7
  21.3 9.2 %collective-permute-done.6.refs_1_ = bf16[512,512]{1,0:T(8,128)(2,1)S(1)} collective-permute-done((bf16[512,512]{1,0:T(8,128)(2,1)S(1)}, bf16[512,512]{1,0:T(8,128)(2,1)S(1)}, u32[]{:S(2)}, u32[]{:S(2)}) %collective-permute-start.6) | collective-permute-done | bytes 524320 | tf_op jit(solution)/shard_map/ppermute | solution.py:275
  30.5 0.7 collective-permute-start.8
  31.8 3.2 %collective-permute-start.4 = (bf16[512,512]{1,0:T(8,128)(2,1)S(1)}, bf16[512,512]{1,0:T(8,128)(2,1)S(1)}, u32[]{:S(2)}, u32[]{:S(2)}) collective-permute-start(bf16[512,512]{1,0:T(8,128)(2,1)S(1)} %shard_map.38.own_a), channel_id=1, source_target_pairs={{0,1},{1,0},{2,3},{3,2},{4,5},{5,4},{6,7},{7,6},{8,9},{9,8},{10,11... | collective-permute-start | bytes 1572872 | tf_op jit(solution)/shard_map/ppermute | solution.py:255
  35.0 1.3 collective-permute-done.7.refs_2_
  37.1 1.8 %shard_map.41.masked.refs_3_.refs_5_ = bf16[1024,2048]{1,0:T(8,128)(2,1)S(1)} custom-call(s32[8,16]{1,0:T(8,128)S(1)} %copy-done.3, bf16[1024,2048]{1,0:T(8,128)(2,1)S(1)} %copy-done), custom_call_target="tpu_custom_call" | custom-call | flops 4194304 | bytes 4194304 | tf_op jit(solution)/shard_map/pallas_call | solution.py:48
  38.9 2.2 %shard_map.44 = (s16[128,2176]{1,0:T(8,128)(2,1)S(1)}, s16[128,2176]{1,0:T(8,128)(2,1)S(1)}) custom-call(s32[16]{0:T(128)S(1)} %dynamic-slice_bitcast_fusion.s, bf16[512,512]{1,0:T(8,128)(2,1)S(1)} %shard_map.38.own_a, bf16[512,512]{1,0:T(8,128)(2,1)S(1)} %collective-permute-done.4.other_a, bf16[512,512]{1,0:T(8,128)(2,1)S(1)} %shard_map.40.own_b, ...), custom_call_target="tpu_custom_call" | custom-call | flops 1073741824 | bytes 4194304 | tf_op jit(solution)/shard_map/pallas_call | solution.py:48
  41.1 2.8 %collective-permute-start.12 = (s16[128,2176]{1,0:T(8,128)(2,1)S(1)}, s16[128,2176]{1,0:T(8,128)(2,1)S(1)}, u32[]{:S(2)}, u32[]{:S(2)}) collective-permute-start(s16[128,2176]{1,0:T(8,128)(2,1)S(1)} %get-tuple-element.28), channel_id=1, source_target_pairs={{0,96},{1,25},{2,98},{3,27},{4,100},{5,29},{6,102},{7,31},{8,104},... | collective-permute-start | bytes 1671176 | tf_op jit(solution)/shard_map/ppermute | solution.py:243
  44.0 1.9 %shard_map.46.mine = f32[256,2048]{1,0:T(8,128)S(1)} custom-call(s32[16]{0:T(128)S(1)} %dynamic-slice_bitcast_fusion.s, bf16[512,512]{1,0:T(8,128)(2,1)S(1)} %shard_map.38.own_a, bf16[512,512]{1,0:T(8,128)(2,1)S(1)} %collective-permute-done.4.other_a, bf16[512,512]{1,0:T(8,128)(2,1)S(1)} %shard_map.40.own_b, ...), custom_call_target="tpu_custom_call" | custom-call | flops 1073741824 | bytes 4194304 | tf_op jit(solution)/shard_map/pallas_call | solution.py:48
  45.9 1.9 %shard_map.43.mine = f32[256,2048]{1,0:T(8,128)S(1)} custom-call(s32[16]{0:T(128)S(1)} %dynamic-slice_bitcast_fusion.s, bf16[512,512]{1,0:T(8,128)(2,1)S(1)} %shard_map.38.own_a, bf16[512,512]{1,0:T(8,128)(2,1)S(1)} %collective-permute-done.4.other_a, bf16[512,512]{1,0:T(8,128)(2,1)S(1)} %shard_map.40.own_b, ...), custom_call_target="tpu_custom_call" | custom-call | flops 1073741824 | bytes 4194304 | tf_op jit(solution)/shard_map/pallas_call | solution.py:48
  47.8 3.3 %collective-permute-done.12.came = s16[128,2176]{1,0:T(8,128)(2,1)S(1)} collective-permute-done((s16[128,2176]{1,0:T(8,128)(2,1)S(1)}, s16[128,2176]{1,0:T(8,128)(2,1)S(1)}, u32[]{:S(2)}, u32[]{:S(2)}) %collective-permute-start.12) | collective-permute-done | bytes 557088 | tf_op jit(solution)/shard_map/ppermute | solution.py:243
  51.6 3.8 %collective-permute-start.13 = (s16[256,2176]{1,0:T(8,128)(2,1)S(1)}, s16[256,2176]{1,0:T(8,128)(2,1)S(1)}, u32[]{:S(2)}, u32[]{:S(2)}) collective-permute-start(s16[256,2176]{1,0:T(8,128)(2,1)S(1)} %shard_map.47), channel_id=1, source_target_pairs={{0,96},{1,25},{2,98},{3,27},{4,100},{5,29},{6,102},{7,31},{8,104},... | collective-permute-start | bytes 3342344 | tf_op jit(solution)/shard_map/ppermute | solution.py:243
  55.9 2.1 %shard_map.42.own = f32[256,2048]{1,0:T(8,128)S(1)} custom-call(s32[16]{0:T(128)S(1)} %dynamic-slice_bitcast_fusion.s, bf16[512,512]{1,0:T(8,128)(2,1)S(1)} %shard_map.38.own_a, bf16[512,512]{1,0:T(8,128)(2,1)S(1)} %collective-permute-done.4.other_a, bf16[512,512]{1,0:T(8,128)(2,1)S(1)} %shard_map.40.own_b, ...), custom_call_target="tpu_custom_call" | custom-call | flops 1073741824 | bytes 4194304 | tf_op jit(solution)/shard_map/pallas_call | solution.py:48
  58.0 10.3 %collective-permute-done.13.b = s16[256,2176]{1,0:T(8,128)(2,1)S(1)} collective-permute-done((s16[256,2176]{1,0:T(8,128)(2,1)S(1)}, s16[256,2176]{1,0:T(8,128)(2,1)S(1)}, u32[]{:S(2)}, u32[]{:S(2)}) %collective-permute-start.13) | collective-permute-done | bytes 1114144 | tf_op jit(solution)/shard_map/ppermute | solution.py:243
  68.3 4.3 %collective-permute-done.11.a = s16[256,2176]{1,0:T(8,128)(2,1)S(1)} collective-permute-done((s16[256,2176]{1,0:T(8,128)(2,1)S(1)}, s16[256,2176]{1,0:T(8,128)(2,1)S(1)}, u32[]{:S(2)}, u32[]{:S(2)}) %collective-permute-start.11) | collective-permute-done | bytes 1114144 | tf_op jit(solution)/shard_map/ppermute | solution.py:243
  72.6 1.4 shard_map.48
  74.1 6.8 %collective-permute-start.14 = (s16[64,2176]{1,0:T(8,128)(2,1)S(1)}, s16[64,2176]{1,0:T(8,128)(2,1)S(1)}, u32[]{:S(2)}, u32[]{:S(2)}) collective-permute-start(s16[64,2176]{1,0:T(8,128)(2,1)S(1)} %get-tuple-element.30), channel_id=1, source_target_pairs={{0,16},{1,65},{2,18},{3,67},{4,20},{5,69},{6,22},{7,71},{8,24},{9,... | collective-permute-start | bytes 835592 | tf_op jit(solution)/shard_map/ppermute | solution.py:243
  80.9 3.2 %collective-permute-start.16 = (s16[64,2176]{1,0:T(8,128)(2,1)S(1)}, s16[64,2176]{1,0:T(8,128)(2,1)S(1)}, u32[]{:S(2)}, u32[]{:S(2)}) collective-permute-start(s16[64,2176]{1,0:T(8,128)(2,1)S(1)} %get-tuple-element.32), channel_id=1, source_target_pairs={{0,24},{1,97},{2,26},{3,99},{4,28},{5,101},{6,30},{7,103},{8,0},{9... | collective-permute-start | bytes 835592 | tf_op jit(solution)/shard_map/ppermute | solution.py:243
  84.1 1.3 collective-permute-done.14.a
  85.4 3.2 %collective-permute-done.15.b = s16[64,2176]{1,0:T(8,128)(2,1)S(1)} collective-permute-done((s16[64,2176]{1,0:T(8,128)(2,1)S(1)}, s16[64,2176]{1,0:T(8,128)(2,1)S(1)}, u32[]{:S(2)}, u32[]{:S(2)}) %collective-permute-start.15) | collective-permute-done | bytes 278560 | tf_op jit(solution)/shard_map/ppermute | solution.py:243
  89.0 3.3 %collective-permute-start.19 = (s16[64,2176]{1,0:T(8,128)(2,1)S(1)}, s16[64,2176]{1,0:T(8,128)(2,1)S(1)}, u32[]{:S(2)}, u32[]{:S(2)}) collective-permute-start(s16[64,2176]{1,0:T(8,128)(2,1)S(1)} %shard_map.49.refs_0_), channel_id=1, source_target_pairs={{0,24},{1,97},{2,26},{3,99},{4,28},{5,101},{6,30},{7,103},{8,0},{9... | collective-permute-start | bytes 835592 | tf_op jit(solution)/shard_map/ppermute | solution.py:243
  93.2 7.8 %collective-permute-done.19.refs_3_ = s16[64,2176]{1,0:T(8,128)(2,1)S(1)} collective-permute-done((s16[64,2176]{1,0:T(8,128)(2,1)S(1)}, s16[64,2176]{1,0:T(8,128)(2,1)S(1)}, u32[]{:S(2)}, u32[]{:S(2)}) %collective-permute-start.19) | collective-permute-done | bytes 278560 | tf_op jit(solution)/shard_map/ppermute | solution.py:243
  101.0 2.2 %collective-permute-done.18.refs_2_ = s16[64,2176]{1,0:T(8,128)(2,1)S(1)} collective-permute-done((s16[64,2176]{1,0:T(8,128)(2,1)S(1)}, s16[64,2176]{1,0:T(8,128)(2,1)S(1)}, u32[]{:S(2)}, u32[]{:S(2)}) %collective-permute-start.18) | collective-permute-done | bytes 278560 | tf_op jit(solution)/shard_map/ppermute | solution.py:243
  103.2 2.3 %collective-permute-done.17.refs_1_ = s16[64,2176]{1,0:T(8,128)(2,1)S(1)} collective-permute-done((s16[64,2176]{1,0:T(8,128)(2,1)S(1)}, s16[64,2176]{1,0:T(8,128)(2,1)S(1)}, u32[]{:S(2)}, u32[]{:S(2)}) %collective-permute-start.17) | collective-permute-done | bytes 278560 | tf_op jit(solution)/shard_map/ppermute | solution.py:243
  105.7 2.0 %collective-permute-start.20 = (s16[256,2176]{1,0:T(8,128)(2,1)S(1)}, s16[256,2176]{1,0:T(8,128)(2,1)S(1)}, u32[]{:S(2)}, u32[]{:S(2)}) collective-permute-start(s16[256,2176]{1,0:T(8,128)(2,1)S(1)} %shard_map.50.refs_0_), channel_id=1, source_target_pairs={{0,32},{1,9},{2,34},{3,11},{4,36},{5,13},{6,38},{7,15},{8,40},{9,1... | collective-permute-start | bytes 3342344 | tf_op jit(solution)/shard_map/ppermute | solution.py:243
  107.7 13.5 %collective-permute-done.21.refs_2_ = s16[256,2176]{1,0:T(8,128)(2,1)S(1)} collective-permute-done((s16[256,2176]{1,0:T(8,128)(2,1)S(1)}, s16[256,2176]{1,0:T(8,128)(2,1)S(1)}, u32[]{:S(2)}, u32[]{:S(2)}) %collective-permute-start.21) | collective-permute-done | bytes 1114144 | tf_op jit(solution)/shard_map/ppermute | solution.py:243
  121.2 1.3 collective-permute-start.27
  122.6 0.9 collective-permute-start.26
  123.5 2.5 %shard_map.53 = (f32[128,1024]{1,0:T(8,128)S(1)}, f32[128,1024]{1,0:T(8,128)S(1)}) custom-call(s32[16]{0:T(128)S(1)} %dynamic-slice_bitcast_fusion.s, s16[256,2176]{1,0:T(8,128)(2,1)S(1)} %shard_map.50.refs_0_, s16[256,2176]{1,0:T(8,128)(2,1)S(1)} %collective-permute-done.20.refs_1_, s16[256,2176]{1,0:T(8,128)(2,1)S(1)} %collective-permute-done.21.refs_2_, ...), custom_call_target="tpu_custom_call" | custom-call | flops 1073741824 | bytes 4194304 | tf_op jit(solution)/shard_map/pallas_call | solution.py:48
  126.1 2.5 %shard_map.51 = (f32[128,1024]{1,0:T(8,128)S(1)}, f32[128,1024]{1,0:T(8,128)S(1)}) custom-call(s32[16]{0:T(128)S(1)} %dynamic-slice_bitcast_fusion.s, s16[256,2176]{1,0:T(8,128)(2,1)S(1)} %shard_map.50.refs_0_, s16[256,2176]{1,0:T(8,128)(2,1)S(1)} %collective-permute-done.20.refs_1_, s16[256,2176]{1,0:T(8,128)(2,1)S(1)} %collective-permute-done.21.refs_2_, ...), custom_call_target="tpu_custom_call" | custom-call | flops 1073741824 | bytes 4194304 | tf_op jit(solution)/shard_map/pallas_call | solution.py:48
  129.0 1.8 %collective-permute-done.27.refs_4_ = s16[128,2176]{1,0:T(8,128)(2,1)S(1)} collective-permute-done((s16[128,2176]{1,0:T(8,128)(2,1)S(1)}, s16[128,2176]{1,0:T(8,128)(2,1)S(1)}, u32[]{:S(2)}, u32[]{:S(2)}) %collective-permute-start.27) | collective-permute-done | bytes 557088 | tf_op jit(solution)/shard_map/ppermute | solution.py:243
  130.8 2.5 %collective-permute-done.26.refs_3_ = s16[128,2176]{1,0:T(8,128)(2,1)S(1)} collective-permute-done((s16[128,2176]{1,0:T(8,128)(2,1)S(1)}, s16[128,2176]{1,0:T(8,128)(2,1)S(1)}, u32[]{:S(2)}, u32[]{:S(2)}) %collective-permute-start.26) | collective-permute-done | bytes 557088 | tf_op jit(solution)/shard_map/ppermute | solution.py:243
  133.4 2.7 %shard_map.57 = (f32[128,1024]{1,0:T(8,128)S(1)}, f32[128,1024]{1,0:T(8,128)S(1)}) custom-call(s32[16]{0:T(128)S(1)} %dynamic-slice_bitcast_fusion.s, s16[256,2176]{1,0:T(8,128)(2,1)S(1)} %shard_map.50.refs_0_, s16[256,2176]{1,0:T(8,128)(2,1)S(1)} %collective-permute-done.20.refs_1_, s16[256,2176]{1,0:T(8,128)(2,1)S(1)} %collective-permute-done.21.refs_2_, ...), custom_call_target="tpu_custom_call" | custom-call | flops 1073741824 | bytes 4194304 | tf_op jit(solution)/shard_map/pallas_call | solution.py:48
  136.2 2.5 %shard_map.55 = (f32[128,1024]{1,0:T(8,128)S(1)}, f32[128,1024]{1,0:T(8,128)S(1)}) custom-call(s32[16]{0:T(128)S(1)} %dynamic-slice_bitcast_fusion.s, s16[256,2176]{1,0:T(8,128)(2,1)S(1)} %shard_map.50.refs_0_, s16[256,2176]{1,0:T(8,128)(2,1)S(1)} %collective-permute-done.20.refs_1_, s16[256,2176]{1,0:T(8,128)(2,1)S(1)} %collective-permute-done.21.refs_2_, ...), custom_call_target="tpu_custom_call" | custom-call | flops 1073741824 | bytes 4194304 | tf_op jit(solution)/shard_map/pallas_call | solution.py:48
  139.4 4.5 %collective-permute-start.25 = (s16[128,1152]{1,0:T(8,128)(2,1)S(1)}, s16[128,1152]{1,0:T(8,128)(2,1)S(1)}, u32[]{:S(2)}, u32[]{:S(2)}) collective-permute-start(s16[128,1152]{1,0:T(8,128)(2,1)S(1)} %shard_map.54), channel_id=1, source_target_pairs={{0,2},{1,3},{2,4},{3,5},{4,6},{5,7},{6,0},{7,1},{8,10},{9,11},{10,... | collective-permute-start | bytes 884744 | tf_op jit(solution)/shard_map/ppermute | solution.py:243
  145.0 8.0 %collective-permute-start.31 = (s16[128,1152]{1,0:T(8,128)(2,1)S(1)}, s16[128,1152]{1,0:T(8,128)(2,1)S(1)}, u32[]{:S(2)}, u32[]{:S(2)}) collective-permute-start(s16[128,1152]{1,0:T(8,128)(2,1)S(1)} %shard_map.58), channel_id=1, source_target_pairs={{0,4},{1,5},{2,6},{3,7},{4,0},{5,1},{6,2},{7,3},{8,14},{9,15},{10,... | collective-permute-start | bytes 884744 | tf_op jit(solution)/shard_map/ppermute | solution.py:243
  153.2 4.5 %collective-permute-start.29 = (s16[128,1152]{1,0:T(8,128)(2,1)S(1)}, s16[128,1152]{1,0:T(8,128)(2,1)S(1)}, u32[]{:S(2)}, u32[]{:S(2)}) collective-permute-start(s16[128,1152]{1,0:T(8,128)(2,1)S(1)} %shard_map.56), channel_id=1, source_target_pairs={{0,6},{1,7},{2,0},{3,1},{4,2},{5,3},{6,4},{7,5},{8,12},{9,13},{10,... | collective-permute-start | bytes 884744 | tf_op jit(solution)/shard_map/ppermute | solution.py:243
  157.8 5.7 %collective-permute-done.31.d = s16[128,1152]{1,0:T(8,128)(2,1)S(1)} collective-permute-done((s16[128,1152]{1,0:T(8,128)(2,1)S(1)}, s16[128,1152]{1,0:T(8,128)(2,1)S(1)}, u32[]{:S(2)}, u32[]{:S(2)}) %collective-permute-start.31) | collective-permute-done | bytes 294944 | tf_op jit(solution)/shard_map/ppermute | solution.py:243
  163.5 2.7 %collective-permute-done.29.c = s16[128,1152]{1,0:T(8,128)(2,1)S(1)} collective-permute-done((s16[128,1152]{1,0:T(8,128)(2,1)S(1)}, s16[128,1152]{1,0:T(8,128)(2,1)S(1)}, u32[]{:S(2)}, u32[]{:S(2)}) %collective-permute-start.29) | collective-permute-done | bytes 294944 | tf_op jit(solution)/shard_map/ppermute | solution.py:243
  166.2 1.1 shard_map.59
  (51 shorter events, 8.9 us)
Async XLA Ops:
  3.7 7.8 %copy-start.1 = (bf16[512,512]{1,0:T(8,128)(2,1)S(1)}, bf16[512,512]{1,0:T(8,128)(2,1)}, u32[]{:S(2)}) copy-start(bf16[512,512]{1,0:T(8,128)(2,1)} %get-tuple-element.25.refs_0_) | copy-start | bytes 1572868
  3.7 2.2 %collective-permute-start = (bf16[512,512]{1,0:T(8,128)(2,1)}, bf16[512,512]{1,0:T(8,128)(2,1)S(1)}, u32[]{:S(2)}, u32[]{:S(2)}) collective-permute-start(bf16[512,512]{1,0:T(8,128)(2,1)} %get-tuple-element.24), channel_id=1, source_target_pairs={{0,1},{1,0},{2,3},{3,2},{4,5},{5,4},{6,7},{7,6},{8,9},{9,8},{10,11... | collective-permute-start | bytes 1572872 | tf_op jit(solution)/shard_map/ppermute | solution.py:273
  3.8 7.7 %collective-permute-start.5 = (bf16[512,512]{1,0:T(8,128)(2,1)}, bf16[512,512]{1,0:T(8,128)(2,1)S(1)}, u32[]{:S(2)}, u32[]{:S(2)}) collective-permute-start(bf16[512,512]{1,0:T(8,128)(2,1)} %get-tuple-element.26), channel_id=1, source_target_pairs={{0,1},{1,0},{2,3},{3,2},{4,5},{5,4},{6,7},{7,6},{8,9},{9,8},{10,11... | collective-permute-start | bytes 1572872 | tf_op jit(solution)/shard_map/ppermute | solution.py:273
  5.9 1.0 copy-start.2
  7.6 11.7 %collective-permute-start.1 = (bf16[512,512]{1,0:T(8,128)(2,1)S(1)}, bf16[512,512]{1,0:T(8,128)(2,1)S(1)}, u32[]{:S(2)}, u32[]{:S(2)}) collective-permute-start(bf16[512,512]{1,0:T(8,128)(2,1)S(1)} %shard_map.37.refs_0_), channel_id=1, source_target_pairs={{0,2},{1,7},{8,10},{9,15},{16,18},{17,23},{24,26},{25,31},{32,34},... | collective-permute-start | bytes 1572872 | tf_op jit(solution)/shard_map/ppermute | solution.py:275
  12.2 18.3 %collective-permute-start.6 = (bf16[512,512]{1,0:T(8,128)(2,1)S(1)}, bf16[512,512]{1,0:T(8,128)(2,1)S(1)}, u32[]{:S(2)}, u32[]{:S(2)}) collective-permute-start(bf16[512,512]{1,0:T(8,128)(2,1)S(1)} %shard_map.39.refs_0_), channel_id=1, source_target_pairs={{0,2},{1,7},{8,10},{9,15},{16,18},{17,23},{24,26},{25,31},{32,34},... | collective-permute-start | bytes 1572872 | tf_op jit(solution)/shard_map/ppermute | solution.py:275
  13.5 17.7 %collective-permute-start.2 = (bf16[512,512]{1,0:T(8,128)(2,1)S(1)}, bf16[512,512]{1,0:T(8,128)(2,1)S(1)}, u32[]{:S(2)}, u32[]{:S(2)}) collective-permute-start(bf16[512,512]{1,0:T(8,128)(2,1)S(1)} %shard_map.37.refs_0_), channel_id=1, source_target_pairs={{0,6},{1,3},{8,14},{9,11},{16,22},{17,19},{24,30},{25,27},{32,38},... | collective-permute-start | bytes 1572872 | tf_op jit(solution)/shard_map/ppermute | solution.py:276
  19.2 11.9 %collective-permute-start.3 = (bf16[512,512]{1,0:T(8,128)(2,1)S(1)}, bf16[512,512]{1,0:T(8,128)(2,1)S(1)}, u32[]{:S(2)}, u32[]{:S(2)}) collective-permute-start(bf16[512,512]{1,0:T(8,128)(2,1)S(1)} %collective-permute-done.1.refs_1_), channel_id=1, source_target_pairs={{2,4},{7,5},{10,12},{15,13},{18,20},{23,21},{26,28},{31,29},{34,36... | collective-permute-start | bytes 1572872 | tf_op jit(solution)/shard_map/ppermute | solution.py:277
  19.9 16.4 %collective-permute-start.7 = (bf16[512,512]{1,0:T(8,128)(2,1)S(1)}, bf16[512,512]{1,0:T(8,128)(2,1)S(1)}, u32[]{:S(2)}, u32[]{:S(2)}) collective-permute-start(bf16[512,512]{1,0:T(8,128)(2,1)S(1)} %shard_map.39.refs_0_), channel_id=1, source_target_pairs={{0,6},{1,3},{8,14},{9,11},{16,22},{17,19},{24,30},{25,27},{32,38},... | collective-permute-start | bytes 1572872 | tf_op jit(solution)/shard_map/ppermute | solution.py:276
  30.5 5.9 %collective-permute-start.8 = (bf16[512,512]{1,0:T(8,128)(2,1)S(1)}, bf16[512,512]{1,0:T(8,128)(2,1)S(1)}, u32[]{:S(2)}, u32[]{:S(2)}) collective-permute-start(bf16[512,512]{1,0:T(8,128)(2,1)S(1)} %collective-permute-done.6.refs_1_), channel_id=1, source_target_pairs={{2,4},{7,5},{10,12},{15,13},{18,20},{23,21},{26,28},{31,29},{34,36... | collective-permute-start | bytes 1572872 | tf_op jit(solution)/shard_map/ppermute | solution.py:277
  31.2 5.8 %copy-start = (bf16[1024,2048]{1,0:T(8,128)(2,1)S(1)}, bf16[1024,2048]{1,0:T(8,128)(2,1)}, u32[]{:S(2)}) copy-start(bf16[1024,2048]{1,0:T(8,128)(2,1)} %density.1) | copy-start | bytes 12582916
  31.8 5.2 %copy-start.3 = (s32[8,16]{1,0:T(8,128)S(1)}, s32[8,16]{1,0:T(8,128)}, u32[]{:S(2)}) copy-start(s32[8,16]{1,0:T(8,128)} %m.3) | copy-start | bytes 1540
  31.8 7.0 %collective-permute-start.4 = (bf16[512,512]{1,0:T(8,128)(2,1)S(1)}, bf16[512,512]{1,0:T(8,128)(2,1)S(1)}, u32[]{:S(2)}, u32[]{:S(2)}) collective-permute-start(bf16[512,512]{1,0:T(8,128)(2,1)S(1)} %shard_map.38.own_a), channel_id=1, source_target_pairs={{0,1},{1,0},{2,3},{3,2},{4,5},{5,4},{6,7},{7,6},{8,9},{9,8},{10,11... | collective-permute-start | bytes 1572872 | tf_op jit(solution)/shard_map/ppermute | solution.py:255
  36.9 2.0 %collective-permute-start.9 = (bf16[512,512]{1,0:T(8,128)(2,1)S(1)}, bf16[512,512]{1,0:T(8,128)(2,1)S(1)}, u32[]{:S(2)}, u32[]{:S(2)}) collective-permute-start(bf16[512,512]{1,0:T(8,128)(2,1)S(1)} %shard_map.40.own_b), channel_id=1, source_target_pairs={{0,1},{1,0},{2,3},{3,2},{4,5},{5,4},{6,7},{7,6},{8,9},{9,8},{10,11... | collective-permute-start | bytes 1572872 | tf_op jit(solution)/shard_map/ppermute | solution.py:255
  41.1 9.9 %collective-permute-start.12 = (s16[128,2176]{1,0:T(8,128)(2,1)S(1)}, s16[128,2176]{1,0:T(8,128)(2,1)S(1)}, u32[]{:S(2)}, u32[]{:S(2)}) collective-permute-start(s16[128,2176]{1,0:T(8,128)(2,1)S(1)} %get-tuple-element.28), channel_id=1, source_target_pairs={{0,96},{1,25},{2,98},{3,27},{4,100},{5,29},{6,102},{7,31},{8,104},... | collective-permute-start | bytes 1671176 | tf_op jit(solution)/shard_map/ppermute | solution.py:243
  44.0 11.3 %collective-permute-start.10 = (s16[128,2176]{1,0:T(8,128)(2,1)S(1)}, s16[128,2176]{1,0:T(8,128)(2,1)S(1)}, u32[]{:S(2)}, u32[]{:S(2)}) collective-permute-start(s16[128,2176]{1,0:T(8,128)(2,1)S(1)} %get-tuple-element.27), channel_id=1, source_target_pairs={{0,32},{1,9},{2,34},{3,11},{4,36},{5,13},{6,38},{7,15},{8,40},{9,1... | collective-permute-start | bytes 1671176 | tf_op jit(solution)/shard_map/ppermute | solution.py:243
  51.6 16.8 %collective-permute-start.13 = (s16[256,2176]{1,0:T(8,128)(2,1)S(1)}, s16[256,2176]{1,0:T(8,128)(2,1)S(1)}, u32[]{:S(2)}, u32[]{:S(2)}) collective-permute-start(s16[256,2176]{1,0:T(8,128)(2,1)S(1)} %shard_map.47), channel_id=1, source_target_pairs={{0,96},{1,25},{2,98},{3,27},{4,100},{5,29},{6,102},{7,31},{8,104},... | collective-permute-start | bytes 3342344 | tf_op jit(solution)/shard_map/ppermute | solution.py:243
  55.9 16.8 %collective-permute-start.11 = (s16[256,2176]{1,0:T(8,128)(2,1)S(1)}, s16[256,2176]{1,0:T(8,128)(2,1)S(1)}, u32[]{:S(2)}, u32[]{:S(2)}) collective-permute-start(s16[256,2176]{1,0:T(8,128)(2,1)S(1)} %shard_map.45), channel_id=1, source_target_pairs={{0,32},{1,9},{2,34},{3,11},{4,36},{5,13},{6,38},{7,15},{8,40},{9,1... | collective-permute-start | bytes 3342344 | tf_op jit(solution)/shard_map/ppermute | solution.py:243
  74.1 11.3 %collective-permute-start.14 = (s16[64,2176]{1,0:T(8,128)(2,1)S(1)}, s16[64,2176]{1,0:T(8,128)(2,1)S(1)}, u32[]{:S(2)}, u32[]{:S(2)}) collective-permute-start(s16[64,2176]{1,0:T(8,128)(2,1)S(1)} %get-tuple-element.30), channel_id=1, source_target_pairs={{0,16},{1,65},{2,18},{3,67},{4,20},{5,69},{6,22},{7,71},{8,24},{9,... | collective-permute-start | bytes 835592 | tf_op jit(solution)/shard_map/ppermute | solution.py:243
  80.9 7.8 %collective-permute-start.15 = (s16[64,2176]{1,0:T(8,128)(2,1)S(1)}, s16[64,2176]{1,0:T(8,128)(2,1)S(1)}, u32[]{:S(2)}, u32[]{:S(2)}) collective-permute-start(s16[64,2176]{1,0:T(8,128)(2,1)S(1)} %get-tuple-element.31), channel_id=1, source_target_pairs={{0,8},{1,33},{2,10},{3,35},{4,12},{5,37},{6,14},{7,39},{8,16},{9,4... | collective-permute-start | bytes 835592 | tf_op jit(solution)/shard_map/ppermute | solution.py:243
  80.9 7.8 %collective-permute-start.16 = (s16[64,2176]{1,0:T(8,128)(2,1)S(1)}, s16[64,2176]{1,0:T(8,128)(2,1)S(1)}, u32[]{:S(2)}, u32[]{:S(2)}) collective-permute-start(s16[64,2176]{1,0:T(8,128)(2,1)S(1)} %get-tuple-element.32), channel_id=1, source_target_pairs={{0,24},{1,97},{2,26},{3,99},{4,28},{5,101},{6,30},{7,103},{8,0},{9... | collective-permute-start | bytes 835592 | tf_op jit(solution)/shard_map/ppermute | solution.py:243
  89.0 12.0 %collective-permute-start.19 = (s16[64,2176]{1,0:T(8,128)(2,1)S(1)}, s16[64,2176]{1,0:T(8,128)(2,1)S(1)}, u32[]{:S(2)}, u32[]{:S(2)}) collective-permute-start(s16[64,2176]{1,0:T(8,128)(2,1)S(1)} %shard_map.49.refs_0_), channel_id=1, source_target_pairs={{0,24},{1,97},{2,26},{3,99},{4,28},{5,101},{6,30},{7,103},{8,0},{9... | collective-permute-start | bytes 835592 | tf_op jit(solution)/shard_map/ppermute | solution.py:243
  92.3 11.0 %collective-permute-start.18 = (s16[64,2176]{1,0:T(8,128)(2,1)S(1)}, s16[64,2176]{1,0:T(8,128)(2,1)S(1)}, u32[]{:S(2)}, u32[]{:S(2)}) collective-permute-start(s16[64,2176]{1,0:T(8,128)(2,1)S(1)} %shard_map.49.refs_0_), channel_id=1, source_target_pairs={{0,16},{1,65},{2,18},{3,67},{4,20},{5,69},{6,22},{7,71},{8,24},{9,... | collective-permute-start | bytes 835592 | tf_op jit(solution)/shard_map/ppermute | solution.py:243
  92.9 12.6 %collective-permute-start.17 = (s16[64,2176]{1,0:T(8,128)(2,1)S(1)}, s16[64,2176]{1,0:T(8,128)(2,1)S(1)}, u32[]{:S(2)}, u32[]{:S(2)}) collective-permute-start(s16[64,2176]{1,0:T(8,128)(2,1)S(1)} %shard_map.49.refs_0_), channel_id=1, source_target_pairs={{0,8},{1,33},{2,10},{3,35},{4,12},{5,37},{6,14},{7,39},{8,16},{9,4... | collective-permute-start | bytes 835592 | tf_op jit(solution)/shard_map/ppermute | solution.py:243
  105.6 15.6 %collective-permute-start.21 = (s16[256,2176]{1,0:T(8,128)(2,1)S(1)}, s16[256,2176]{1,0:T(8,128)(2,1)S(1)}, u32[]{:S(2)}, u32[]{:S(2)}) collective-permute-start(s16[256,2176]{1,0:T(8,128)(2,1)S(1)} %shard_map.50.refs_0_), channel_id=1, source_target_pairs={{0,96},{1,25},{2,98},{3,27},{4,100},{5,29},{6,102},{7,31},{8,104},... | collective-permute-start | bytes 3342344 | tf_op jit(solution)/shard_map/ppermute | solution.py:243
  105.7 16.8 %collective-permute-start.20 = (s16[256,2176]{1,0:T(8,128)(2,1)S(1)}, s16[256,2176]{1,0:T(8,128)(2,1)S(1)}, u32[]{:S(2)}, u32[]{:S(2)}) collective-permute-start(s16[256,2176]{1,0:T(8,128)(2,1)S(1)} %shard_map.50.refs_0_), channel_id=1, source_target_pairs={{0,32},{1,9},{2,34},{3,11},{4,36},{5,13},{6,38},{7,15},{8,40},{9,1... | collective-permute-start | bytes 3342344 | tf_op jit(solution)/shard_map/ppermute | solution.py:243
  121.2 9.6 %collective-permute-start.27 = (s16[128,2176]{1,0:T(8,128)(2,1)S(1)}, s16[128,2176]{1,0:T(8,128)(2,1)S(1)}, u32[]{:S(2)}, u32[]{:S(2)}) collective-permute-start(s16[128,2176]{1,0:T(8,128)(2,1)S(1)} %slice.9), channel_id=1, source_target_pairs={{0,96},{1,25},{2,98},{3,27},{4,100},{5,29},{6,102},{7,31},{8,104},... | collective-permute-start | bytes 1671176 | tf_op jit(solution)/shard_map/ppermute | solution.py:243
  122.6 10.8 %collective-permute-start.26 = (s16[128,2176]{1,0:T(8,128)(2,1)S(1)}, s16[128,2176]{1,0:T(8,128)(2,1)S(1)}, u32[]{:S(2)}, u32[]{:S(2)}) collective-permute-start(s16[128,2176]{1,0:T(8,128)(2,1)S(1)} %slice.8), channel_id=1, source_target_pairs={{0,32},{1,9},{2,34},{3,11},{4,36},{5,13},{6,38},{7,15},{8,40},{9,1... | collective-permute-start | bytes 1671176 | tf_op jit(solution)/shard_map/ppermute | solution.py:243
  126.0 13.2 %collective-permute-start.24 = (f32[128,1024]{1,0:T(8,128)S(1)}, f32[128,1024]{1,0:T(8,128)S(1)}, u32[]{:S(2)}, u32[]{:S(2)}) collective-permute-start(f32[128,1024]{1,0:T(8,128)S(1)} %get-tuple-element.36), channel_id=1, source_target_pairs={{0,1},{1,0},{2,3},{3,2},{4,5},{5,4},{6,7},{7,6},{8,9},{9,8},{10,11... | collective-permute-start | bytes 1572872 | tf_op jit(solution)/shard_map/ppermute | solution.py:255
  128.6 15.3 %collective-permute-start.22 = (f32[128,1024]{1,0:T(8,128)S(1)}, f32[128,1024]{1,0:T(8,128)S(1)}, u32[]{:S(2)}, u32[]{:S(2)}) collective-permute-start(f32[128,1024]{1,0:T(8,128)S(1)} %get-tuple-element.34), channel_id=1, source_target_pairs={{0,1},{1,0},{2,3},{3,2},{4,5},{5,4},{6,7},{7,6},{8,9},{9,8},{10,11... | collective-permute-start | bytes 1572872 | tf_op jit(solution)/shard_map/ppermute | solution.py:255
  136.1 8.7 %collective-permute-start.30 = (f32[128,1024]{1,0:T(8,128)S(1)}, f32[128,1024]{1,0:T(8,128)S(1)}, u32[]{:S(2)}, u32[]{:S(2)}) collective-permute-start(f32[128,1024]{1,0:T(8,128)S(1)} %get-tuple-element.40), channel_id=1, source_target_pairs={{0,1},{1,0},{2,3},{3,2},{4,5},{5,4},{6,7},{7,6},{8,9},{9,8},{10,11... | collective-permute-start | bytes 1572872 | tf_op jit(solution)/shard_map/ppermute | solution.py:255
  138.8 14.2 %collective-permute-start.28 = (f32[128,1024]{1,0:T(8,128)S(1)}, f32[128,1024]{1,0:T(8,128)S(1)}, u32[]{:S(2)}, u32[]{:S(2)}) collective-permute-start(f32[128,1024]{1,0:T(8,128)S(1)} %get-tuple-element.38), channel_id=1, source_target_pairs={{0,1},{1,0},{2,3},{3,2},{4,5},{5,4},{6,7},{7,6},{8,9},{9,8},{10,11... | collective-permute-start | bytes 1572872 | tf_op jit(solution)/shard_map/ppermute | solution.py:255
  139.4 18.4 %collective-permute-start.25 = (s16[128,1152]{1,0:T(8,128)(2,1)S(1)}, s16[128,1152]{1,0:T(8,128)(2,1)S(1)}, u32[]{:S(2)}, u32[]{:S(2)}) collective-permute-start(s16[128,1152]{1,0:T(8,128)(2,1)S(1)} %shard_map.54), channel_id=1, source_target_pairs={{0,2},{1,3},{2,4},{3,5},{4,6},{5,7},{6,0},{7,1},{8,10},{9,11},{10,... | collective-permute-start | bytes 884744 | tf_op jit(solution)/shard_map/ppermute | solution.py:243
  144.1 13.6 %collective-permute-start.23 = (s16[128,1152]{1,0:T(8,128)(2,1)S(1)}, s16[128,1152]{1,0:T(8,128)(2,1)S(1)}, u32[]{:S(2)}, u32[]{:S(2)}) collective-permute-start(s16[128,1152]{1,0:T(8,128)(2,1)S(1)} %shard_map.52), channel_id=1, source_target_pairs={{0,0},{1,1},{2,2},{3,3},{4,4},{5,5},{6,6},{7,7},{8,8},{9,9},{10,10... | collective-permute-start | bytes 884744 | tf_op jit(solution)/shard_map/ppermute | solution.py:243
  145.0 18.5 %collective-permute-start.31 = (s16[128,1152]{1,0:T(8,128)(2,1)S(1)}, s16[128,1152]{1,0:T(8,128)(2,1)S(1)}, u32[]{:S(2)}, u32[]{:S(2)}) collective-permute-start(s16[128,1152]{1,0:T(8,128)(2,1)S(1)} %shard_map.58), channel_id=1, source_target_pairs={{0,4},{1,5},{2,6},{3,7},{4,0},{5,1},{6,2},{7,3},{8,14},{9,15},{10,... | collective-permute-start | bytes 884744 | tf_op jit(solution)/shard_map/ppermute | solution.py:243
  153.2 12.9 %collective-permute-start.29 = (s16[128,1152]{1,0:T(8,128)(2,1)S(1)}, s16[128,1152]{1,0:T(8,128)(2,1)S(1)}, u32[]{:S(2)}, u32[]{:S(2)}) collective-permute-start(s16[128,1152]{1,0:T(8,128)(2,1)S(1)} %shard_map.56), channel_id=1, source_target_pairs={{0,6},{1,7},{2,0},{3,1},{4,2},{5,3},{6,4},{7,5},{8,12},{9,13},{10,... | collective-permute-start | bytes 884744 | tf_op jit(solution)/shard_map/ppermute | solution.py:243
where the time goes:
time: 170 us; the launch traced here: 167 us
  waiting for transfers between devices  76 us (45%)
  starting transfers between devices  58 us (34%)
  Pallas kernels  31 us (18%)
  local copies, waits for them, and re-layouts  1.83 us (1%)
    ppermute x18, waiting for transfers between devices, send(): return lax.ppermute(v, AXES, [(place(*d), place(*to(*d))) for d in DEVICES])  61 us
    ppermute x18, starting transfers between devices, send(): return lax.ppermute(v, AXES, [(place(*d), place(*to(*d))) for d in DEVICES])  42.9 us
    pallas_call x23, Pallas kernels, call(): pl.pallas_call(kernel, out_shape=out, in_specs=[pl.BlockSpec(memory_space...  27.3 us
    ppermute x2, waiting for transfers between devices, spread_column(): one = lax.ppermute(half, axes, [(0, 2), (1, 7)])  12.8 us
    ppermute x2, starting transfers between devices, spread_column(): one = lax.ppermute(half, axes, [(0, 2), (1, 7)])  5.29 us
    ppermute x6, starting transfers between devices, swap(): return lax.ppermute(v, 'core', [(0, 1), (1, 0)])  4.27 us
    pallas_call x1, Pallas kernels, local(): pl.pallas_call(column_kernel, out_shape=[shape(512, 512, BF16)] * 4, in_s...  3.71 us
    ppermute x2, starting transfers between devices, spread_column(): two = lax.ppermute(half, axes, [(0, 6), (1, 3)])  3.51 us
  transfers between devices with their start and end apart: 32, of which 18 were waited for; matrix products, arithmetic and copies ran while one was open for 0% of the time, Pallas kernels for 13%

commit v1 on v0

--- a/solution.py
+++ b/solution.py
@@ -33,10 +33,11 @@
     row = x * 4 + y
     source = 0 if z == 0 else 1 if z == 1 + 2 * core else 3 if z == 2 else 2
     own_square = int(z * 2 + core == row // 2)
-    return [*quarters, *chosen, second, core, own_square, row % 2, source, 0, 0, 0]
-
-
-QUARTERS, CHOSEN, SECOND, CORE, OWNER, HALF, SOURCE = 0, 4, 8, 9, 10, 11, 12
+    where = [turns(x, y).index(q) for q in range(4)]
+    return [*quarters, *chosen, *where, second, core, own_square, row % 2, source] + [0] * 15
+
+
+QUARTERS, CHOSEN, WHERE, SECOND, CORE, OWNER, HALF, SOURCE = 0, 4, 8, 12, 13, 14, 15, 16
 
 
 def shape(rows, columns, dtype):
@@ -87,16 +88,8 @@
     return jnp.where(m[i, j] != 0, block, jnp.zeros_like(block))
 
 
-def column_kernel(m, hbm, *refs):
-    *outs, density, sem = refs
-    copies = []
-    for i in range(4):
-        rows = slice(i * 256, (i + 1) * 256)
-        copies.append(pltpu.make_async_copy(hbm.at[rows, :SLAB], density.at[rows], sem.at[i]))
-        copies[i].start()
+def column_kernel(m, density, *outs):
     for i in range(8):
-        if i % 2 == 0:
-            copies[i // 2].wait()
         rows = slice(i % 4 * BLOCK, (i % 4 + 1) * BLOCK)
         for j in range(8):
             out = outs[i // 4 + j // 4 * 2]
@@ -173,21 +166,20 @@
         out[i * PIECE : (i + 1) * PIECE] = part[...]
 
 
-def second_kernel(i, s, *refs):
+def second_kernel(turn, s, *refs):
     *quarters, masked, mine, theirs, left, triple = refs
     own, back, ahead, *far = quarters
-    d = s[CHOSEN + i]
     starts = []
     for j in range(4):
         sub = (s[SECOND] + 4 - j) % 4
-        starts.append(((sub // 2) ^ s[CORE]) * 128 + (sub % 2) * 64)
-
-    def unpack(refs):
+        starts.append(((sub // 2) ^ s[CORE]) * 256 + (sub % 2) * 64)
+
+    def unpack(i, refs):
         for j, start in enumerate(starts):
             size = refs[0].shape[0]
             ref, first = refs[j * PIECE // size], j * PIECE % size
             v = take(ref, slice(first, first + PIECE))
-            rows = pl.ds(pl.multiple_of(start, 64), PIECE)
+            rows = pl.ds(pl.multiple_of(start + i * 128, 64), PIECE)
             left[rows, :] = v.astype(BF16)
             for half in range(2):
 
@@ -195,9 +187,11 @@
                 def _(v=v, rows=rows, half=half):
                     triple[rows, :] = 3.0 * v[:, half * SLAB : (half + 1) * SLAB]
 
-    for shift, refs in ((0, [own]), (1, [back]), (3, [ahead]), (2, far)):
-        if refs:
-            pl.when(d == shift)(functools.partial(unpack, refs))
+    for i in range(2):
+        for shift, refs in ((0, [own]), (1, [back]), (3, [ahead]), (2, far)):
+            if refs:
+                pl.when(s[CHOSEN + turn + i] == shift)(functools.partial(unpack, i, refs))
+
     for n in range(4):
         columns = slice(n * 256, (n + 1) * 256)
         t = -2.0 * lax.dot_general(
@@ -206,33 +200,43 @@
             (((1,), (1,)), ((), ())),
             preferred_element_type=F32,
         )
-        mine[:, columns] = t[:128]
-        theirs[:, columns] = t[128:]
+        mine[:, columns] = t[:256]
+        theirs[:, columns] = t[256:]
 
     @pl.when(s[OWNER] == 1)
     def _():
-        mine[...] += triple[:128]
-        theirs[...] += triple[128:]
-
-
-def second_product(i, s, quarters, masked):
+        mine[...] += triple[:256]
+        theirs[...] += triple[256:]
+
+
+def second_product(turn, s, quarters, masked):
     return call(
-        functools.partial(second_kernel, i),
-        [shape(128, SLAB, F32)] * 2,
+        functools.partial(second_kernel, turn),
+        [shape(256, SLAB, F32)] * 2,
         [s],
         *quarters,
         masked,
-        flops=2 * QUARTER * SLAB * WIDE,
-        scratch=[pltpu.VMEM((QUARTER, WIDE), BF16), pltpu.VMEM((QUARTER, SLAB), F32)],
+        flops=4 * QUARTER * SLAB * WIDE,
+        scratch=[pltpu.VMEM((512, WIDE), BF16), pltpu.VMEM((512, SLAB), F32)],
     )
 
 
-def pair_kernel(mine, came, out):
-    put(out, mine[...] + came[...])
-
-
-def finish_kernel(a, b, c, d, out):
-    out[...] = take(a) + take(b) + take(c) + take(d)
+def deal_kernel(s, mine_a, came_a, mine_b, came_b, *outs):
+    for q, out in enumerate(outs):
+        for i, (mine, came) in enumerate(((mine_a, came_a), (mine_b, came_b))):
+
+            @pl.when(s[WHERE + q] // 2 == i)
+            def _(q=q, out=out, mine=mine, came=came):
+                rows = at(s[WHERE + q] % 2, 128)
+                v = mine[rows, :] + came[rows, :]
+                if q == 0:
+                    out[...] = v
+                else:
+                    put(out, v)
+
+
+def finish_kernel(own, a, b, c, out):
+    out[...] = own[...] + take(a) + take(b) + take(c)
 
 
 def place(x, y, z, core):
@@ -282,15 +286,8 @@
 def local(density, block_mask):
     table = jnp.asarray([facts(*d) for d in DEVICES], I32)
     s = lax.dynamic_index_in_dim(table, lax.axis_index(AXES), 0, False)
-    top_a, low_a, top_b, low_b = pl.pallas_call(
-        column_kernel,
-        out_shape=[shape(512, 512, BF16)] * 4,
-        in_specs=[pl.BlockSpec(memory_space=pltpu.SMEM), pl.BlockSpec(memory_space=pltpu.HBM)],
-        out_specs=[pl.BlockSpec(memory_space=pltpu.VMEM)] * 4,
-        scratch_shapes=[pltpu.VMEM((SLAB, SLAB), BF16), pltpu.SemaphoreType.DMA((4,))],
-        compiler_params=pltpu.CompilerParams(vmem_limit_bytes=60 << 20),
-        name="column",
-    )(block_mask, density)
+    outs = [shape(512, 512, BF16)] * 4
+    top_a, low_a, top_b, low_b = call(column_kernel, outs, [block_mask], density[:, :SLAB])
     masked = call(mask_kernel, shape(SLAB, WIDE, BF16), [block_mask], density)
     parts = spread_column(s, top_a, low_a)
     parts += spread_column(s, top_b, low_b)
@@ -315,14 +312,15 @@
     back, ahead = along(own, 1), along(own, -1)
     top = along(back[:128], 1)
     low = along(ahead[128:], -1)
-    came = []
-    for i in range(4):
-        quarters = [own, back, ahead] + [top, low] * (i >= 2)
+    sums = []
+    for i in (0, 2):
+        quarters = [own, back, ahead] + [top, low] * (i == 2)
         mine, theirs = second_product(i, s, quarters, masked)
-        theirs = swap(theirs)
-        v = call(pair_kernel, shape(128, SLAB + LANES, I16), [], mine, theirs)
-        came.append(send(v, lambda x, y, z, core: (x, y, z + turns(x, y)[i], core)))
-    return call(finish_kernel, shape(128, SLAB, F32), [], *came)
+        sums += [mine, swap(theirs)]
+    coded = shape(128, SLAB + LANES, I16)
+    own, *parts = call(deal_kernel, [shape(128, SLAB, F32)] + [coded] * 3, [s], *sums)
+    came = [send(parts[d - 1], lambda x, y, z, core: (x, y, z + d, core)) for d in (2, 1, 3)]
+    return call(finish_kernel, shape(128, SLAB, F32), [], own, *came)
 
 
 def solution(mesh):

time: 170 us -> 167 us (0.982); the launches traced: 167 us -> 166 us
  waiting for transfers between devices: 76 us -> 80 us
  Pallas kernels: 31 us -> 27.4 us
  starting transfers between devices: 58 us -> 55.8 us
    pallas_call x1 -> x0, Pallas kernels: 3.71 us -> none  [local(): pl.pallas_call(column_kernel, out_shape=[shape(512, 512, BF16)] * 4, in_s...]
    ppermute x6 -> x4, waiting for transfers between devices: 0.07 us -> 2.71 us  [swap(): return lax.ppermute(v, 'core', [(0, 1), (1, 0)])]
    slice x0 -> x1, local copies, waits for them, and re-layouts: none -> 1.77 us  [local(): density[:, :SLAB]]
    ppermute x18 -> x17, waiting for transfers between devices: 61 us -> 62.5 us  [send(): return lax.ppermute(v, AXES, [(place(*d), place(*to(*d))) for d in DEVICES])]
    ppermute x18 -> x17, starting transfers between devices: 42.9 us -> 41.7 us  [send(): return lax.ppermute(v, AXES, [(place(*d), place(*to(*d))) for d in DEVICES])]
    ppermute x6 -> x4, starting transfers between devices: 4.27 us -> 3.44 us  [swap(): return lax.ppermute(v, 'core', [(0, 1), (1, 0)])]
    pallas_call x23 -> x19, Pallas kernels: 27.3 us -> 27.4 us  [call(): pl.pallas_call(kernel, out_shape=out, in_specs=[pl.BlockSpec(memory_space...]
  transfers between devices with their start and end apart: 32 -> 29, of which waited for: 18 -> 17; matrix products, arithmetic and copies ran while one was open for 0% -> 0% of each run, Pallas kernels for 13% -> 12%
where the time goes in v1:
time: 167 us; the launch traced here: 166 us
  waiting for transfers between devices  80 us (48%)
  starting transfers between devices  55.8 us (33%)
  Pallas kernels  27.4 us (16%)
  local copies, waits for them, and re-layouts  2.56 us (2%)
    ppermute x17, waiting for transfers between devices, send(): return lax.ppermute(v, AXES, [(place(*d), place(*to(*d))) for d in DEVICES])  62.5 us
    ppermute x17, starting transfers between devices, send(): return lax.ppermute(v, AXES, [(place(*d), place(*to(*d))) for d in DEVICES])  41.7 us
    pallas_call x19, Pallas kernels, call(): pl.pallas_call(kernel, out_shape=out, in_specs=[pl.BlockSpec(memory_space...  27.4 us
    ppermute x2, waiting for transfers between devices, spread_column(): one = lax.ppermute(half, axes, [(0, 2), (1, 7)])  12.8 us
    ppermute x2, starting transfers between devices, spread_column(): one = lax.ppermute(half, axes, [(0, 2), (1, 7)])  5.29 us
    ppermute x2, starting transfers between devices, spread_column(): two = lax.ppermute(half, axes, [(0, 6), (1, 3)])  3.51 us
    ppermute x4, starting transfers between devices, swap(): return lax.ppermute(v, 'core', [(0, 1), (1, 0)])  3.44 us
  transfers between devices with their start and end apart: 29, of which 17 were waited for; matrix products, arithmetic and copies ran while one was open for 0% of the time, Pallas kernels for 12%

profile of v1, /device:TPU:0, one launch (start us, length us, event | category | flops | bytes accessed | tf_op | source)
XLA Modules:
  0.0 166.1 jit_solution(242550476145274718)
XLA Ops:
  0.0 1.8 %slice.9.density = bf16[1024,1024]{1,0:T(8,128)(2,1)S(1)} slice(bf16[1024,2048]{1,0:T(8,128)(2,1)} %density.1), slice={[0:1024], [0:1024]} | slice | bytes 4194304 | tf_op jit(solution)/shard_map/slice | solution.py:290
  1.8 1.1 shard_map.37
  3.5 0.7 dynamic-slice_bitcast_fusion.s
  4.2 0.7 collective-permute-done.5.refs_1_
  5.5 4.0 %collective-permute-start.6 = (bf16[512,512]{1,0:T(8,128)(2,1)S(1)}, bf16[512,512]{1,0:T(8,128)(2,1)S(1)}, u32[]{:S(2)}, u32[]{:S(2)}) collective-permute-start(bf16[512,512]{1,0:T(8,128)(2,1)S(1)} %shard_map.40.refs_0_), channel_id=1, source_target_pairs={{0,2},{1,7},{8,10},{9,15},{16,18},{17,23},{24,26},{25,31},{32,34},... | collective-permute-start | bytes 1572872 | tf_op jit(solution)/shard_map/ppermute | solution.py:279
  10.1 1.3 collective-permute-start.1
  11.4 2.2 %collective-permute-start.7 = (bf16[512,512]{1,0:T(8,128)(2,1)S(1)}, bf16[512,512]{1,0:T(8,128)(2,1)S(1)}, u32[]{:S(2)}, u32[]{:S(2)}) collective-permute-start(bf16[512,512]{1,0:T(8,128)(2,1)S(1)} %shard_map.40.refs_0_), channel_id=1, source_target_pairs={{0,6},{1,3},{8,14},{9,11},{16,22},{17,19},{24,30},{25,27},{32,38},... | collective-permute-start | bytes 1572872 | tf_op jit(solution)/shard_map/ppermute | solution.py:280
  13.6 3.6 %collective-permute-done.6.refs_1_ = bf16[512,512]{1,0:T(8,128)(2,1)S(1)} collective-permute-done((bf16[512,512]{1,0:T(8,128)(2,1)S(1)}, bf16[512,512]{1,0:T(8,128)(2,1)S(1)}, u32[]{:S(2)}, u32[]{:S(2)}) %collective-permute-start.6) | collective-permute-done | bytes 524320 | tf_op jit(solution)/shard_map/ppermute | solution.py:279
  17.2 0.7 collective-permute-start.8
  17.8 1.3 collective-permute-start.2
  19.2 9.2 %collective-permute-done.1.refs_1_ = bf16[512,512]{1,0:T(8,128)(2,1)S(1)} collective-permute-done((bf16[512,512]{1,0:T(8,128)(2,1)S(1)}, bf16[512,512]{1,0:T(8,128)(2,1)S(1)}, u32[]{:S(2)}, u32[]{:S(2)}) %collective-permute-start.1) | collective-permute-done | bytes 524320 | tf_op jit(solution)/shard_map/ppermute | solution.py:279
  28.4 0.7 collective-permute-start.3
  29.1 0.6 shard_map.41.own_b
  29.7 3.2 %collective-permute-start.9 = (bf16[512,512]{1,0:T(8,128)(2,1)S(1)}, bf16[512,512]{1,0:T(8,128)(2,1)S(1)}, u32[]{:S(2)}, u32[]{:S(2)}) collective-permute-start(bf16[512,512]{1,0:T(8,128)(2,1)S(1)} %shard_map.41.own_b), channel_id=1, source_target_pairs={{0,1},{1,0},{2,3},{3,2},{4,5},{5,4},{6,7},{7,6},{8,9},{9,8},{10,11... | collective-permute-start | bytes 1572872 | tf_op jit(solution)/shard_map/ppermute | solution.py:259
  32.9 1.3 collective-permute-done.2.refs_2_
  34.2 0.6 shard_map.39.own_a
  34.9 1.8 %shard_map.42.masked.refs_3_.refs_5_ = bf16[1024,2048]{1,0:T(8,128)(2,1)S(1)} custom-call(s32[8,16]{1,0:T(8,128)S(1)} %copy-done.1, bf16[1024,2048]{1,0:T(8,128)(2,1)S(1)} %copy-done), custom_call_target="tpu_custom_call" | custom-call | flops 4194304 | bytes 4194304 | tf_op jit(solution)/shard_map/pallas_call | solution.py:49
  36.8 2.2 %shard_map.45 = (s16[128,2176]{1,0:T(8,128)(2,1)S(1)}, s16[128,2176]{1,0:T(8,128)(2,1)S(1)}) custom-call(s32[32]{0:T(128)S(1)} %dynamic-slice_bitcast_fusion.s, bf16[512,512]{1,0:T(8,128)(2,1)S(1)} %shard_map.39.own_a, bf16[512,512]{1,0:T(8,128)(2,1)S(1)} %collective-permute-done.4.other_a, bf16[512,512]{1,0:T(8,128)(2,1)S(1)} %shard_map.41.own_b, ...), custom_call_target="tpu_custom_call" | custom-call | flops 1073741824 | bytes 4194304 | tf_op jit(solution)/shard_map/pallas_call | solution.py:49
  39.0 2.8 %collective-permute-start.12 = (s16[128,2176]{1,0:T(8,128)(2,1)S(1)}, s16[128,2176]{1,0:T(8,128)(2,1)S(1)}, u32[]{:S(2)}, u32[]{:S(2)}) collective-permute-start(s16[128,2176]{1,0:T(8,128)(2,1)S(1)} %get-tuple-element.28), channel_id=1, source_target_pairs={{0,96},{1,25},{2,98},{3,27},{4,100},{5,29},{6,102},{7,31},{8,104},... | collective-permute-start | bytes 1671176 | tf_op jit(solution)/shard_map/ppermute | solution.py:247
  41.9 1.9 %shard_map.47.mine = f32[256,2048]{1,0:T(8,128)S(1)} custom-call(s32[32]{0:T(128)S(1)} %dynamic-slice_bitcast_fusion.s, bf16[512,512]{1,0:T(8,128)(2,1)S(1)} %shard_map.39.own_a, bf16[512,512]{1,0:T(8,128)(2,1)S(1)} %collective-permute-done.4.other_a, bf16[512,512]{1,0:T(8,128)(2,1)S(1)} %shard_map.41.own_b, ...), custom_call_target="tpu_custom_call" | custom-call | flops 1073741824 | bytes 4194304 | tf_op jit(solution)/shard_map/pallas_call | solution.py:49
  43.8 1.9 %shard_map.44.mine = f32[256,2048]{1,0:T(8,128)S(1)} custom-call(s32[32]{0:T(128)S(1)} %dynamic-slice_bitcast_fusion.s, bf16[512,512]{1,0:T(8,128)(2,1)S(1)} %shard_map.39.own_a, bf16[512,512]{1,0:T(8,128)(2,1)S(1)} %collective-permute-done.4.other_a, bf16[512,512]{1,0:T(8,128)(2,1)S(1)} %shard_map.41.own_b, ...), custom_call_target="tpu_custom_call" | custom-call | flops 1073741824 | bytes 4194304 | tf_op jit(solution)/shard_map/pallas_call | solution.py:49
  45.7 3.3 %collective-permute-done.12.came = s16[128,2176]{1,0:T(8,128)(2,1)S(1)} collective-permute-done((s16[128,2176]{1,0:T(8,128)(2,1)S(1)}, s16[128,2176]{1,0:T(8,128)(2,1)S(1)}, u32[]{:S(2)}, u32[]{:S(2)}) %collective-permute-start.12) | collective-permute-done | bytes 557088 | tf_op jit(solution)/shard_map/ppermute | solution.py:247
  49.5 3.8 %collective-permute-start.13 = (s16[256,2176]{1,0:T(8,128)(2,1)S(1)}, s16[256,2176]{1,0:T(8,128)(2,1)S(1)}, u32[]{:S(2)}, u32[]{:S(2)}) collective-permute-start(s16[256,2176]{1,0:T(8,128)(2,1)S(1)} %shard_map.48), channel_id=1, source_target_pairs={{0,96},{1,25},{2,98},{3,27},{4,100},{5,29},{6,102},{7,31},{8,104},... | collective-permute-start | bytes 3342344 | tf_op jit(solution)/shard_map/ppermute | solution.py:247
  53.9 2.1 %shard_map.43.own = f32[256,2048]{1,0:T(8,128)S(1)} custom-call(s32[32]{0:T(128)S(1)} %dynamic-slice_bitcast_fusion.s, bf16[512,512]{1,0:T(8,128)(2,1)S(1)} %shard_map.39.own_a, bf16[512,512]{1,0:T(8,128)(2,1)S(1)} %collective-permute-done.4.other_a, bf16[512,512]{1,0:T(8,128)(2,1)S(1)} %shard_map.41.own_b, ...), custom_call_target="tpu_custom_call" | custom-call | flops 1073741824 | bytes 4194304 | tf_op jit(solution)/shard_map/pallas_call | solution.py:49
  55.9 10.3 %collective-permute-done.13.b = s16[256,2176]{1,0:T(8,128)(2,1)S(1)} collective-permute-done((s16[256,2176]{1,0:T(8,128)(2,1)S(1)}, s16[256,2176]{1,0:T(8,128)(2,1)S(1)}, u32[]{:S(2)}, u32[]{:S(2)}) %collective-permute-start.13) | collective-permute-done | bytes 1114144 | tf_op jit(solution)/shard_map/ppermute | solution.py:247
  66.2 4.3 %collective-permute-done.11.a = s16[256,2176]{1,0:T(8,128)(2,1)S(1)} collective-permute-done((s16[256,2176]{1,0:T(8,128)(2,1)S(1)}, s16[256,2176]{1,0:T(8,128)(2,1)S(1)}, u32[]{:S(2)}, u32[]{:S(2)}) %collective-permute-start.11) | collective-permute-done | bytes 1114144 | tf_op jit(solution)/shard_map/ppermute | solution.py:247
  70.6 1.4 shard_map.49
  72.0 6.9 %collective-permute-start.14 = (s16[64,2176]{1,0:T(8,128)(2,1)S(1)}, s16[64,2176]{1,0:T(8,128)(2,1)S(1)}, u32[]{:S(2)}, u32[]{:S(2)}) collective-permute-start(s16[64,2176]{1,0:T(8,128)(2,1)S(1)} %get-tuple-element.30), channel_id=1, source_target_pairs={{0,16},{1,65},{2,18},{3,67},{4,20},{5,69},{6,22},{7,71},{8,24},{9,... | collective-permute-start | bytes 835592 | tf_op jit(solution)/shard_map/ppermute | solution.py:247
  78.8 3.2 %collective-permute-start.16 = (s16[64,2176]{1,0:T(8,128)(2,1)S(1)}, s16[64,2176]{1,0:T(8,128)(2,1)S(1)}, u32[]{:S(2)}, u32[]{:S(2)}) collective-permute-start(s16[64,2176]{1,0:T(8,128)(2,1)S(1)} %get-tuple-element.32), channel_id=1, source_target_pairs={{0,24},{1,97},{2,26},{3,99},{4,28},{5,101},{6,30},{7,103},{8,0},{9... | collective-permute-start | bytes 835592 | tf_op jit(solution)/shard_map/ppermute | solution.py:247
  82.1 1.3 collective-permute-done.14.a
  83.4 3.2 %collective-permute-done.15.b = s16[64,2176]{1,0:T(8,128)(2,1)S(1)} collective-permute-done((s16[64,2176]{1,0:T(8,128)(2,1)S(1)}, s16[64,2176]{1,0:T(8,128)(2,1)S(1)}, u32[]{:S(2)}, u32[]{:S(2)}) %collective-permute-start.15) | collective-permute-done | bytes 278560 | tf_op jit(solution)/shard_map/ppermute | solution.py:247
  87.0 1.9 %collective-permute-start.17 = (s16[64,2176]{1,0:T(8,128)(2,1)S(1)}, s16[64,2176]{1,0:T(8,128)(2,1)S(1)}, u32[]{:S(2)}, u32[]{:S(2)}) collective-permute-start(s16[64,2176]{1,0:T(8,128)(2,1)S(1)} %shard_map.50.refs_0_), channel_id=1, source_target_pairs={{0,8},{1,33},{2,10},{3,35},{4,12},{5,37},{6,14},{7,39},{8,16},{9,4... | collective-permute-start | bytes 835592 | tf_op jit(solution)/shard_map/ppermute | solution.py:247
  88.9 2.9 %collective-permute-start.18 = (s16[64,2176]{1,0:T(8,128)(2,1)S(1)}, s16[64,2176]{1,0:T(8,128)(2,1)S(1)}, u32[]{:S(2)}, u32[]{:S(2)}) collective-permute-start(s16[64,2176]{1,0:T(8,128)(2,1)S(1)} %shard_map.50.refs_0_), channel_id=1, source_target_pairs={{0,16},{1,65},{2,18},{3,67},{4,20},{5,69},{6,22},{7,71},{8,24},{9,... | collective-permute-start | bytes 835592 | tf_op jit(solution)/shard_map/ppermute | solution.py:247
  91.7 3.1 %collective-permute-done.17.refs_1_ = s16[64,2176]{1,0:T(8,128)(2,1)S(1)} collective-permute-done((s16[64,2176]{1,0:T(8,128)(2,1)S(1)}, s16[64,2176]{1,0:T(8,128)(2,1)S(1)}, u32[]{:S(2)}, u32[]{:S(2)}) %collective-permute-start.17) | collective-permute-done | bytes 278560 | tf_op jit(solution)/shard_map/ppermute | solution.py:247
  94.8 10.2 %collective-permute-done.18.refs_2_ = s16[64,2176]{1,0:T(8,128)(2,1)S(1)} collective-permute-done((s16[64,2176]{1,0:T(8,128)(2,1)S(1)}, s16[64,2176]{1,0:T(8,128)(2,1)S(1)}, u32[]{:S(2)}, u32[]{:S(2)}) %collective-permute-start.18) | collective-permute-done | bytes 278560 | tf_op jit(solution)/shard_map/ppermute | solution.py:247
  105.1 3.2 %collective-permute-start.21 = (s16[256,2176]{1,0:T(8,128)(2,1)S(1)}, s16[256,2176]{1,0:T(8,128)(2,1)S(1)}, u32[]{:S(2)}, u32[]{:S(2)}) collective-permute-start(s16[256,2176]{1,0:T(8,128)(2,1)S(1)} %shard_map.51.refs_0_), channel_id=1, source_target_pairs={{0,96},{1,25},{2,98},{3,27},{4,100},{5,29},{6,102},{7,31},{8,104},... | collective-permute-start | bytes 3342344 | tf_op jit(solution)/shard_map/ppermute | solution.py:247
  108.3 13.5 %collective-permute-done.20.refs_1_ = s16[256,2176]{1,0:T(8,128)(2,1)S(1)} collective-permute-done((s16[256,2176]{1,0:T(8,128)(2,1)S(1)}, s16[256,2176]{1,0:T(8,128)(2,1)S(1)}, u32[]{:S(2)}, u32[]{:S(2)}) %collective-permute-start.20) | collective-permute-done | bytes 1114144 | tf_op jit(solution)/shard_map/ppermute | solution.py:247
  122.0 3.3 %collective-permute-start.24 = (s16[128,2176]{1,0:T(8,128)(2,1)S(1)}, s16[128,2176]{1,0:T(8,128)(2,1)S(1)}, u32[]{:S(2)}, u32[]{:S(2)}) collective-permute-start(s16[128,2176]{1,0:T(8,128)(2,1)S(1)} %slice.13), channel_id=1, source_target_pairs={{0,96},{1,25},{2,98},{3,27},{4,100},{5,29},{6,102},{7,31},{8,104},... | collective-permute-start | bytes 1671176 | tf_op jit(solution)/shard_map/ppermute | solution.py:247
  125.3 4.3 %shard_map.52 = (f32[256,1024]{1,0:T(8,128)S(1)}, f32[256,1024]{1,0:T(8,128)S(1)}) custom-call(s32[32]{0:T(128)S(1)} %dynamic-slice_bitcast_fusion.s, s16[256,2176]{1,0:T(8,128)(2,1)S(1)} %shard_map.51.refs_0_, s16[256,2176]{1,0:T(8,128)(2,1)S(1)} %collective-permute-done.20.refs_1_, s16[256,2176]{1,0:T(8,128)(2,1)S(1)} %collective-permute-done.21.refs_2_, ...), custom_call_target="tpu_custom_call" | custom-call | flops 2147483648 | bytes 4194304 | tf_op jit(solution)/shard_map/pallas_call | solution.py:49
  129.7 3.0 %collective-permute-done.23.refs_3_ = s16[128,2176]{1,0:T(8,128)(2,1)S(1)} collective-permute-done((s16[128,2176]{1,0:T(8,128)(2,1)S(1)}, s16[128,2176]{1,0:T(8,128)(2,1)S(1)}, u32[]{:S(2)}, u32[]{:S(2)}) %collective-permute-start.23) | collective-permute-done | bytes 557088 | tf_op jit(solution)/shard_map/ppermute | solution.py:247
  132.7 4.5 %shard_map.53 = (f32[256,1024]{1,0:T(8,128)S(1)}, f32[256,1024]{1,0:T(8,128)S(1)}) custom-call(s32[32]{0:T(128)S(1)} %dynamic-slice_bitcast_fusion.s, s16[256,2176]{1,0:T(8,128)(2,1)S(1)} %shard_map.51.refs_0_, s16[256,2176]{1,0:T(8,128)(2,1)S(1)} %collective-permute-done.20.refs_1_, s16[256,2176]{1,0:T(8,128)(2,1)S(1)} %collective-permute-done.21.refs_2_, ...), custom_call_target="tpu_custom_call" | custom-call | flops 2147483648 | bytes 4194304 | tf_op jit(solution)/shard_map/pallas_call | solution.py:49
  137.3 2.6 %collective-permute-done.25.came_b = f32[256,1024]{1,0:T(8,128)S(1)} collective-permute-done((f32[256,1024]{1,0:T(8,128)S(1)}, f32[256,1024]{1,0:T(8,128)S(1)}, u32[]{:S(2)}, u32[]{:S(2)}) %collective-permute-start.25) | collective-permute-done | bytes 1048608 | tf_op jit(solution)/shard_map/ppermute | solution.py:259
  139.9 1.3 shard_map.54
  141.2 10.2 %collective-permute-start.26 = (s16[128,1152]{1,0:T(8,128)(2,1)S(1)}, s16[128,1152]{1,0:T(8,128)(2,1)S(1)}, u32[]{:S(2)}, u32[]{:S(2)}) collective-permute-start(s16[128,1152]{1,0:T(8,128)(2,1)S(1)} %get-tuple-element.38), channel_id=1, source_target_pairs={{0,4},{1,5},{2,6},{3,7},{4,0},{5,1},{6,2},{7,3},{8,12},{9,13},{10,... | collective-permute-start | bytes 884744 | tf_op jit(solution)/shard_map/ppermute | solution.py:247
  151.5 3.2 %collective-permute-start.28 = (s16[128,1152]{1,0:T(8,128)(2,1)S(1)}, s16[128,1152]{1,0:T(8,128)(2,1)S(1)}, u32[]{:S(2)}, u32[]{:S(2)}) collective-permute-start(s16[128,1152]{1,0:T(8,128)(2,1)S(1)} %get-tuple-element.40), channel_id=1, source_target_pairs={{0,6},{1,7},{2,0},{3,1},{4,2},{5,3},{6,4},{7,5},{8,14},{9,15},{10,... | collective-permute-start | bytes 884744 | tf_op jit(solution)/shard_map/ppermute | solution.py:247
  154.7 4.7 %collective-permute-done.26.a = s16[128,1152]{1,0:T(8,128)(2,1)S(1)} collective-permute-done((s16[128,1152]{1,0:T(8,128)(2,1)S(1)}, s16[128,1152]{1,0:T(8,128)(2,1)S(1)}, u32[]{:S(2)}, u32[]{:S(2)}) %collective-permute-start.26) | collective-permute-done | bytes 294944 | tf_op jit(solution)/shard_map/ppermute | solution.py:247
  159.4 5.7 %collective-permute-done.27.b = s16[128,1152]{1,0:T(8,128)(2,1)S(1)} collective-permute-done((s16[128,1152]{1,0:T(8,128)(2,1)S(1)}, s16[128,1152]{1,0:T(8,128)(2,1)S(1)}, u32[]{:S(2)}, u32[]{:S(2)}) %collective-permute-start.27) | collective-permute-done | bytes 294944 | tf_op jit(solution)/shard_map/ppermute | solution.py:247
  165.1 1.0 shard_map.55
  (37 shorter events, 4.0 us)
Async XLA Ops:
  0.0 1.8 %copy-start.1 = (s32[8,16]{1,0:T(8,128)S(1)}, s32[8,16]{1,0:T(8,128)}, u32[]{:S(2)}) copy-start(s32[8,16]{1,0:T(8,128)} %m.3) | copy-start | bytes 1540
  2.9 2.0 %collective-permute-start.5 = (bf16[512,512]{1,0:T(8,128)(2,1)S(1)}, bf16[512,512]{1,0:T(8,128)(2,1)S(1)}, u32[]{:S(2)}, u32[]{:S(2)}) collective-permute-start(bf16[512,512]{1,0:T(8,128)(2,1)S(1)} %get-tuple-element.26), channel_id=1, source_target_pairs={{0,1},{1,0},{2,3},{3,2},{4,5},{5,4},{6,7},{7,6},{8,9},{9,8},{10,11... | collective-permute-start | bytes 1572872 | tf_op jit(solution)/shard_map/ppermute | solution.py:277
  3.0 6.5 %collective-permute-start = (bf16[512,512]{1,0:T(8,128)(2,1)S(1)}, bf16[512,512]{1,0:T(8,128)(2,1)S(1)}, u32[]{:S(2)}, u32[]{:S(2)}) collective-permute-start(bf16[512,512]{1,0:T(8,128)(2,1)S(1)} %get-tuple-element.24), channel_id=1, source_target_pairs={{0,1},{1,0},{2,3},{3,2},{4,5},{5,4},{6,7},{7,6},{8,9},{9,8},{10,11... | collective-permute-start | bytes 1572872 | tf_op jit(solution)/shard_map/ppermute | solution.py:277
  5.5 11.7 %collective-permute-start.6 = (bf16[512,512]{1,0:T(8,128)(2,1)S(1)}, bf16[512,512]{1,0:T(8,128)(2,1)S(1)}, u32[]{:S(2)}, u32[]{:S(2)}) collective-permute-start(bf16[512,512]{1,0:T(8,128)(2,1)S(1)} %shard_map.40.refs_0_), channel_id=1, source_target_pairs={{0,2},{1,7},{8,10},{9,15},{16,18},{17,23},{24,26},{25,31},{32,34},... | collective-permute-start | bytes 1572872 | tf_op jit(solution)/shard_map/ppermute | solution.py:279
  10.1 18.3 %collective-permute-start.1 = (bf16[512,512]{1,0:T(8,128)(2,1)S(1)}, bf16[512,512]{1,0:T(8,128)(2,1)S(1)}, u32[]{:S(2)}, u32[]{:S(2)}) collective-permute-start(bf16[512,512]{1,0:T(8,128)(2,1)S(1)} %shard_map.38.refs_0_), channel_id=1, source_target_pairs={{0,2},{1,7},{8,10},{9,15},{16,18},{17,23},{24,26},{25,31},{32,34},... | collective-permute-start | bytes 1572872 | tf_op jit(solution)/shard_map/ppermute | solution.py:279
  11.4 17.7 %collective-permute-start.7 = (bf16[512,512]{1,0:T(8,128)(2,1)S(1)}, bf16[512,512]{1,0:T(8,128)(2,1)S(1)}, u32[]{:S(2)}, u32[]{:S(2)}) collective-permute-start(bf16[512,512]{1,0:T(8,128)(2,1)S(1)} %shard_map.40.refs_0_), channel_id=1, source_target_pairs={{0,6},{1,3},{8,14},{9,11},{16,22},{17,19},{24,30},{25,27},{32,38},... | collective-permute-start | bytes 1572872 | tf_op jit(solution)/shard_map/ppermute | solution.py:280
  17.2 11.9 %collective-permute-start.8 = (bf16[512,512]{1,0:T(8,128)(2,1)S(1)}, bf16[512,512]{1,0:T(8,128)(2,1)S(1)}, u32[]{:S(2)}, u32[]{:S(2)}) collective-permute-start(bf16[512,512]{1,0:T(8,128)(2,1)S(1)} %collective-permute-done.6.refs_1_), channel_id=1, source_target_pairs={{2,4},{7,5},{10,12},{15,13},{18,20},{23,21},{26,28},{31,29},{34,36... | collective-permute-start | bytes 1572872 | tf_op jit(solution)/shard_map/ppermute | solution.py:281
  17.8 16.4 %collective-permute-start.2 = (bf16[512,512]{1,0:T(8,128)(2,1)S(1)}, bf16[512,512]{1,0:T(8,128)(2,1)S(1)}, u32[]{:S(2)}, u32[]{:S(2)}) collective-permute-start(bf16[512,512]{1,0:T(8,128)(2,1)S(1)} %shard_map.38.refs_0_), channel_id=1, source_target_pairs={{0,6},{1,3},{8,14},{9,11},{16,22},{17,19},{24,30},{25,27},{32,38},... | collective-permute-start | bytes 1572872 | tf_op jit(solution)/shard_map/ppermute | solution.py:280
  28.4 5.8 %collective-permute-start.3 = (bf16[512,512]{1,0:T(8,128)(2,1)S(1)}, bf16[512,512]{1,0:T(8,128)(2,1)S(1)}, u32[]{:S(2)}, u32[]{:S(2)}) collective-permute-start(bf16[512,512]{1,0:T(8,128)(2,1)S(1)} %collective-permute-done.1.refs_1_), channel_id=1, source_target_pairs={{2,4},{7,5},{10,12},{15,13},{18,20},{23,21},{26,28},{31,29},{34,36... | collective-permute-start | bytes 1572872 | tf_op jit(solution)/shard_map/ppermute | solution.py:281
  29.1 5.8 %copy-start = (bf16[1024,2048]{1,0:T(8,128)(2,1)S(1)}, bf16[1024,2048]{1,0:T(8,128)(2,1)}, u32[]{:S(2)}) copy-start(bf16[1024,2048]{1,0:T(8,128)(2,1)} %density.1) | copy-start | bytes 12582916
  29.7 7.0 %collective-permute-start.9 = (bf16[512,512]{1,0:T(8,128)(2,1)S(1)}, bf16[512,512]{1,0:T(8,128)(2,1)S(1)}, u32[]{:S(2)}, u32[]{:S(2)}) collective-permute-start(bf16[512,512]{1,0:T(8,128)(2,1)S(1)} %shard_map.41.own_b), channel_id=1, source_target_pairs={{0,1},{1,0},{2,3},{3,2},{4,5},{5,4},{6,7},{7,6},{8,9},{9,8},{10,11... | collective-permute-start | bytes 1572872 | tf_op jit(solution)/shard_map/ppermute | solution.py:259
  34.8 2.0 %collective-permute-start.4 = (bf16[512,512]{1,0:T(8,128)(2,1)S(1)}, bf16[512,512]{1,0:T(8,128)(2,1)S(1)}, u32[]{:S(2)}, u32[]{:S(2)}) collective-permute-start(bf16[512,512]{1,0:T(8,128)(2,1)S(1)} %shard_map.39.own_a), channel_id=1, source_target_pairs={{0,1},{1,0},{2,3},{3,2},{4,5},{5,4},{6,7},{7,6},{8,9},{9,8},{10,11... | collective-permute-start | bytes 1572872 | tf_op jit(solution)/shard_map/ppermute | solution.py:259
  39.0 9.9 %collective-permute-start.12 = (s16[128,2176]{1,0:T(8,128)(2,1)S(1)}, s16[128,2176]{1,0:T(8,128)(2,1)S(1)}, u32[]{:S(2)}, u32[]{:S(2)}) collective-permute-start(s16[128,2176]{1,0:T(8,128)(2,1)S(1)} %get-tuple-element.28), channel_id=1, source_target_pairs={{0,96},{1,25},{2,98},{3,27},{4,100},{5,29},{6,102},{7,31},{8,104},... | collective-permute-start | bytes 1671176 | tf_op jit(solution)/shard_map/ppermute | solution.py:247
  41.9 11.4 %collective-permute-start.10 = (s16[128,2176]{1,0:T(8,128)(2,1)S(1)}, s16[128,2176]{1,0:T(8,128)(2,1)S(1)}, u32[]{:S(2)}, u32[]{:S(2)}) collective-permute-start(s16[128,2176]{1,0:T(8,128)(2,1)S(1)} %get-tuple-element.27), channel_id=1, source_target_pairs={{0,32},{1,9},{2,34},{3,11},{4,36},{5,13},{6,38},{7,15},{8,40},{9,1... | collective-permute-start | bytes 1671176 | tf_op jit(solution)/shard_map/ppermute | solution.py:247
  49.5 16.8 %collective-permute-start.13 = (s16[256,2176]{1,0:T(8,128)(2,1)S(1)}, s16[256,2176]{1,0:T(8,128)(2,1)S(1)}, u32[]{:S(2)}, u32[]{:S(2)}) collective-permute-start(s16[256,2176]{1,0:T(8,128)(2,1)S(1)} %shard_map.48), channel_id=1, source_target_pairs={{0,96},{1,25},{2,98},{3,27},{4,100},{5,29},{6,102},{7,31},{8,104},... | collective-permute-start | bytes 3342344 | tf_op jit(solution)/shard_map/ppermute | solution.py:247
  53.8 16.8 %collective-permute-start.11 = (s16[256,2176]{1,0:T(8,128)(2,1)S(1)}, s16[256,2176]{1,0:T(8,128)(2,1)S(1)}, u32[]{:S(2)}, u32[]{:S(2)}) collective-permute-start(s16[256,2176]{1,0:T(8,128)(2,1)S(1)} %shard_map.46), channel_id=1, source_target_pairs={{0,32},{1,9},{2,34},{3,11},{4,36},{5,13},{6,38},{7,15},{8,40},{9,1... | collective-permute-start | bytes 3342344 | tf_op jit(solution)/shard_map/ppermute | solution.py:247
  72.0 11.4 %collective-permute-start.14 = (s16[64,2176]{1,0:T(8,128)(2,1)S(1)}, s16[64,2176]{1,0:T(8,128)(2,1)S(1)}, u32[]{:S(2)}, u32[]{:S(2)}) collective-permute-start(s16[64,2176]{1,0:T(8,128)(2,1)S(1)} %get-tuple-element.30), channel_id=1, source_target_pairs={{0,16},{1,65},{2,18},{3,67},{4,20},{5,69},{6,22},{7,71},{8,24},{9,... | collective-permute-start | bytes 835592 | tf_op jit(solution)/shard_map/ppermute | solution.py:247
  78.8 7.8 %collective-permute-start.15 = (s16[64,2176]{1,0:T(8,128)(2,1)S(1)}, s16[64,2176]{1,0:T(8,128)(2,1)S(1)}, u32[]{:S(2)}, u32[]{:S(2)}) collective-permute-start(s16[64,2176]{1,0:T(8,128)(2,1)S(1)} %get-tuple-element.31), channel_id=1, source_target_pairs={{0,8},{1,33},{2,10},{3,35},{4,12},{5,37},{6,14},{7,39},{8,16},{9,4... | collective-permute-start | bytes 835592 | tf_op jit(solution)/shard_map/ppermute | solution.py:247
  78.8 7.8 %collective-permute-start.16 = (s16[64,2176]{1,0:T(8,128)(2,1)S(1)}, s16[64,2176]{1,0:T(8,128)(2,1)S(1)}, u32[]{:S(2)}, u32[]{:S(2)}) collective-permute-start(s16[64,2176]{1,0:T(8,128)(2,1)S(1)} %get-tuple-element.32), channel_id=1, source_target_pairs={{0,24},{1,97},{2,26},{3,99},{4,28},{5,101},{6,30},{7,103},{8,0},{9... | collective-permute-start | bytes 835592 | tf_op jit(solution)/shard_map/ppermute | solution.py:247
  87.0 7.8 %collective-permute-start.17 = (s16[64,2176]{1,0:T(8,128)(2,1)S(1)}, s16[64,2176]{1,0:T(8,128)(2,1)S(1)}, u32[]{:S(2)}, u32[]{:S(2)}) collective-permute-start(s16[64,2176]{1,0:T(8,128)(2,1)S(1)} %shard_map.50.refs_0_), channel_id=1, source_target_pairs={{0,8},{1,33},{2,10},{3,35},{4,12},{5,37},{6,14},{7,39},{8,16},{9,4... | collective-permute-start | bytes 835592 | tf_op jit(solution)/shard_map/ppermute | solution.py:247
  88.9 16.1 %collective-permute-start.18 = (s16[64,2176]{1,0:T(8,128)(2,1)S(1)}, s16[64,2176]{1,0:T(8,128)(2,1)S(1)}, u32[]{:S(2)}, u32[]{:S(2)}) collective-permute-start(s16[64,2176]{1,0:T(8,128)(2,1)S(1)} %shard_map.50.refs_0_), channel_id=1, source_target_pairs={{0,16},{1,65},{2,18},{3,67},{4,20},{5,69},{6,22},{7,71},{8,24},{9,... | collective-permute-start | bytes 835592 | tf_op jit(solution)/shard_map/ppermute | solution.py:247
  91.7 13.2 %collective-permute-start.19 = (s16[64,2176]{1,0:T(8,128)(2,1)S(1)}, s16[64,2176]{1,0:T(8,128)(2,1)S(1)}, u32[]{:S(2)}, u32[]{:S(2)}) collective-permute-start(s16[64,2176]{1,0:T(8,128)(2,1)S(1)} %shard_map.50.refs_0_), channel_id=1, source_target_pairs={{0,24},{1,97},{2,26},{3,99},{4,28},{5,101},{6,30},{7,103},{8,0},{9... | collective-permute-start | bytes 835592 | tf_op jit(solution)/shard_map/ppermute | solution.py:247
  105.0 16.8 %collective-permute-start.20 = (s16[256,2176]{1,0:T(8,128)(2,1)S(1)}, s16[256,2176]{1,0:T(8,128)(2,1)S(1)}, u32[]{:S(2)}, u32[]{:S(2)}) collective-permute-start(s16[256,2176]{1,0:T(8,128)(2,1)S(1)} %shard_map.51.refs_0_), channel_id=1, source_target_pairs={{0,32},{1,9},{2,34},{3,11},{4,36},{5,13},{6,38},{7,15},{8,40},{9,1... | collective-permute-start | bytes 3342344 | tf_op jit(solution)/shard_map/ppermute | solution.py:247
  105.1 16.8 %collective-permute-start.21 = (s16[256,2176]{1,0:T(8,128)(2,1)S(1)}, s16[256,2176]{1,0:T(8,128)(2,1)S(1)}, u32[]{:S(2)}, u32[]{:S(2)}) collective-permute-start(s16[256,2176]{1,0:T(8,128)(2,1)S(1)} %shard_map.51.refs_0_), channel_id=1, source_target_pairs={{0,96},{1,25},{2,98},{3,27},{4,100},{5,29},{6,102},{7,31},{8,104},... | collective-permute-start | bytes 3342344 | tf_op jit(solution)/shard_map/ppermute | solution.py:247
  121.9 10.8 %collective-permute-start.23 = (s16[128,2176]{1,0:T(8,128)(2,1)S(1)}, s16[128,2176]{1,0:T(8,128)(2,1)S(1)}, u32[]{:S(2)}, u32[]{:S(2)}) collective-permute-start(s16[128,2176]{1,0:T(8,128)(2,1)S(1)} %slice.12), channel_id=1, source_target_pairs={{0,32},{1,9},{2,34},{3,11},{4,36},{5,13},{6,38},{7,15},{8,40},{9,1... | collective-permute-start | bytes 1671176 | tf_op jit(solution)/shard_map/ppermute | solution.py:247
  122.0 10.7 %collective-permute-start.24 = (s16[128,2176]{1,0:T(8,128)(2,1)S(1)}, s16[128,2176]{1,0:T(8,128)(2,1)S(1)}, u32[]{:S(2)}, u32[]{:S(2)}) collective-permute-start(s16[128,2176]{1,0:T(8,128)(2,1)S(1)} %slice.13), channel_id=1, source_target_pairs={{0,96},{1,25},{2,98},{3,27},{4,100},{5,29},{6,102},{7,31},{8,104},... | collective-permute-start | bytes 1671176 | tf_op jit(solution)/shard_map/ppermute | solution.py:247
  129.6 7.7 %collective-permute-start.22 = (f32[256,1024]{1,0:T(8,128)S(1)}, f32[256,1024]{1,0:T(8,128)S(1)}, u32[]{:S(2)}, u32[]{:S(2)}) collective-permute-start(f32[256,1024]{1,0:T(8,128)S(1)} %get-tuple-element.34), channel_id=1, source_target_pairs={{0,1},{1,0},{2,3},{3,2},{4,5},{5,4},{6,7},{7,6},{8,9},{9,8},{10,11... | collective-permute-start | bytes 3145736 | tf_op jit(solution)/shard_map/ppermute | solution.py:259
  137.2 2.7 %collective-permute-start.25 = (f32[256,1024]{1,0:T(8,128)S(1)}, f32[256,1024]{1,0:T(8,128)S(1)}, u32[]{:S(2)}, u32[]{:S(2)}) collective-permute-start(f32[256,1024]{1,0:T(8,128)S(1)} %get-tuple-element.36), channel_id=1, source_target_pairs={{0,1},{1,0},{2,3},{3,2},{4,5},{5,4},{6,7},{7,6},{8,9},{9,8},{10,11... | collective-permute-start | bytes 3145736 | tf_op jit(solution)/shard_map/ppermute | solution.py:259
  141.2 18.1 %collective-permute-start.26 = (s16[128,1152]{1,0:T(8,128)(2,1)S(1)}, s16[128,1152]{1,0:T(8,128)(2,1)S(1)}, u32[]{:S(2)}, u32[]{:S(2)}) collective-permute-start(s16[128,1152]{1,0:T(8,128)(2,1)S(1)} %get-tuple-element.38), channel_id=1, source_target_pairs={{0,4},{1,5},{2,6},{3,7},{4,0},{5,1},{6,2},{7,3},{8,12},{9,13},{10,... | collective-permute-start | bytes 884744 | tf_op jit(solution)/shard_map/ppermute | solution.py:247
  151.5 13.6 %collective-permute-start.27 = (s16[128,1152]{1,0:T(8,128)(2,1)S(1)}, s16[128,1152]{1,0:T(8,128)(2,1)S(1)}, u32[]{:S(2)}, u32[]{:S(2)}) collective-permute-start(s16[128,1152]{1,0:T(8,128)(2,1)S(1)} %get-tuple-element.39), channel_id=1, source_target_pairs={{0,2},{1,3},{2,4},{3,5},{4,6},{5,7},{6,0},{7,1},{8,10},{9,11},{10,... | collective-permute-start | bytes 884744 | tf_op jit(solution)/shard_map/ppermute | solution.py:247
  151.5 13.6 %collective-permute-start.28 = (s16[128,1152]{1,0:T(8,128)(2,1)S(1)}, s16[128,1152]{1,0:T(8,128)(2,1)S(1)}, u32[]{:S(2)}, u32[]{:S(2)}) collective-permute-start(s16[128,1152]{1,0:T(8,128)(2,1)S(1)} %get-tuple-element.40), channel_id=1, source_target_pairs={{0,6},{1,7},{2,0},{3,1},{4,2},{5,3},{6,4},{7,5},{8,14},{9,15},{10,... | collective-permute-start | bytes 884744 | tf_op jit(solution)/shard_map/ppermute | solution.py:247

commit v2 on v1

--- a/solution.py
+++ b/solution.py
@@ -33,11 +33,10 @@
     row = x * 4 + y
     source = 0 if z == 0 else 1 if z == 1 + 2 * core else 3 if z == 2 else 2
     own_square = int(z * 2 + core == row // 2)
-    where = [turns(x, y).index(q) for q in range(4)]
-    return [*quarters, *chosen, *where, second, core, own_square, row % 2, source] + [0] * 15
-
-
-QUARTERS, CHOSEN, WHERE, SECOND, CORE, OWNER, HALF, SOURCE = 0, 4, 8, 12, 13, 14, 15, 16
+    return [*quarters, *chosen, second, core, own_square, row % 2, source, 0, 0, 0]
+
+
+QUARTERS, CHOSEN, SECOND, CORE, OWNER, HALF, SOURCE = 0, 4, 8, 9, 10, 11, 12
 
 
 def shape(rows, columns, dtype):
@@ -221,22 +220,14 @@
     )
 
 
-def deal_kernel(s, mine_a, came_a, mine_b, came_b, *outs):
-    for q, out in enumerate(outs):
-        for i, (mine, came) in enumerate(((mine_a, came_a), (mine_b, came_b))):
-
-            @pl.when(s[WHERE + q] // 2 == i)
-            def _(q=q, out=out, mine=mine, came=came):
-                rows = at(s[WHERE + q] % 2, 128)
-                v = mine[rows, :] + came[rows, :]
-                if q == 0:
-                    out[...] = v
-                else:
-                    put(out, v)
-
-
-def finish_kernel(own, a, b, c, out):
-    out[...] = own[...] + take(a) + take(b) + take(c)
+def deal_kernel(mine, came, *outs):
+    for i, out in enumerate(outs):
+        rows = slice(i * 128, (i + 1) * 128)
+        put(out, mine[rows, :] + came[rows, :])
+
+
+def finish_kernel(a, b, c, d, out):
+    out[...] = take(a) + take(b) + take(c) + take(d)
 
 
 def place(x, y, z, core):
@@ -312,15 +303,16 @@
     back, ahead = along(own, 1), along(own, -1)
     top = along(back[:128], 1)
     low = along(ahead[128:], -1)
-    sums = []
+    came = []
     for i in (0, 2):
         quarters = [own, back, ahead] + [top, low] * (i == 2)
         mine, theirs = second_product(i, s, quarters, masked)
-        sums += [mine, swap(theirs)]
-    coded = shape(128, SLAB + LANES, I16)
-    own, *parts = call(deal_kernel, [shape(128, SLAB, F32)] + [coded] * 3, [s], *sums)
-    came = [send(parts[d - 1], lambda x, y, z, core: (x, y, z + d, core)) for d in (2, 1, 3)]
-    return call(finish_kernel, shape(128, SLAB, F32), [], own, *came)
+        theirs = swap(theirs)
+        outs = [shape(128, SLAB + LANES, I16)] * 2
+        parts = call(deal_kernel, outs, [], mine, theirs)
+        for j, v in enumerate(parts):
+            came.append(send(v, lambda x, y, z, core: (x, y, z + turns(x, y)[i + j], core)))
+    return call(finish_kernel, shape(128, SLAB, F32), [], *came)
 
 
 def solution(mesh):

time: 167 us -> 168 us (level)
  the two profiles are of different devices: /device:TPU:0 before, /device:TPU:6 now
where the time goes in v2:
time: 168 us
  waiting for transfers between devices  75.2 us (45%)
  starting transfers between devices  63.5 us (38%)
  Pallas kernels  26.1 us (16%)
  local copies, waits for them, and re-layouts  2.56 us (2%)
    ppermute x18, waiting for transfers between devices, send(): return lax.ppermute(v, AXES, [(place(*d), place(*to(*d))) for d in DEVICES])  60.3 us
    ppermute x18, starting transfers between devices, send(): return lax.ppermute(v, AXES, [(place(*d), place(*to(*d))) for d in DEVICES])  49.4 us
    pallas_call x20, Pallas kernels, call(): pl.pallas_call(kernel, out_shape=out, in_specs=[pl.BlockSpec(memory_space...  26.1 us
    ppermute x2, waiting for transfers between devices, spread_column(): one = lax.ppermute(half, axes, [(0, 2), (1, 7)])  12.8 us
    ppermute x2, starting transfers between devices, spread_column(): one = lax.ppermute(half, axes, [(0, 2), (1, 7)])  5.18 us
    ppermute x2, starting transfers between devices, spread_column(): two = lax.ppermute(half, axes, [(0, 6), (1, 3)])  3.51 us
    ppermute x4, starting transfers between devices, swap(): return lax.ppermute(v, 'core', [(0, 1), (1, 0)])  3.44 us
  transfers between devices with their start and end apart: 30, of which 17 were waited for; matrix products, arithmetic and copies ran while one was open for 0% of the time, Pallas kernels for 12%

profile of v2, /device:TPU:6, one launch (start us, length us, event | category | flops | bytes accessed | tf_op | source)
XLA Modules:
  0.0 167.8 jit_solution(5633226488370440957)
XLA Ops:
  0.0 1.8 %slice.9.density = bf16[1024,1024]{1,0:T(8,128)(2,1)S(1)} slice(bf16[1024,2048]{1,0:T(8,128)(2,1)} %density.1), slice={[0:1024], [0:1024]} | slice | bytes 4194304 | tf_op jit(solution)/shard_map/slice | solution.py:281
  1.8 1.1 shard_map.37
  3.5 0.7 dynamic-slice_bitcast_fusion.s
  4.2 0.7 collective-permute-done.5.refs_1_
  5.5 3.9 %collective-permute-start.6 = (bf16[512,512]{1,0:T(8,128)(2,1)S(1)}, bf16[512,512]{1,0:T(8,128)(2,1)S(1)}, u32[]{:S(2)}, u32[]{:S(2)}) collective-permute-start(bf16[512,512]{1,0:T(8,128)(2,1)S(1)} %shard_map.40.refs_0_), channel_id=1, source_target_pairs={{0,2},{1,7},{8,10},{9,15},{16,18},{17,23},{24,26},{25,31},{32,34},... | collective-permute-start | bytes 1572872 | tf_op jit(solution)/shard_map/ppermute | solution.py:270
  9.9 1.3 collective-permute-start.1
  11.3 2.2 %collective-permute-start.7 = (bf16[512,512]{1,0:T(8,128)(2,1)S(1)}, bf16[512,512]{1,0:T(8,128)(2,1)S(1)}, u32[]{:S(2)}, u32[]{:S(2)}) collective-permute-start(bf16[512,512]{1,0:T(8,128)(2,1)S(1)} %shard_map.40.refs_0_), channel_id=1, source_target_pairs={{0,6},{1,3},{8,14},{9,11},{16,22},{17,19},{24,30},{25,27},{32,38},... | collective-permute-start | bytes 1572872 | tf_op jit(solution)/shard_map/ppermute | solution.py:271
  13.5 3.6 %collective-permute-done.6.refs_1_ = bf16[512,512]{1,0:T(8,128)(2,1)S(1)} collective-permute-done((bf16[512,512]{1,0:T(8,128)(2,1)S(1)}, bf16[512,512]{1,0:T(8,128)(2,1)S(1)}, u32[]{:S(2)}, u32[]{:S(2)}) %collective-permute-start.6) | collective-permute-done | bytes 524320 | tf_op jit(solution)/shard_map/ppermute | solution.py:270
  17.0 0.7 collective-permute-start.8
  17.7 1.3 collective-permute-start.2
  19.1 9.2 %collective-permute-done.1.refs_1_ = bf16[512,512]{1,0:T(8,128)(2,1)S(1)} collective-permute-done((bf16[512,512]{1,0:T(8,128)(2,1)S(1)}, bf16[512,512]{1,0:T(8,128)(2,1)S(1)}, u32[]{:S(2)}, u32[]{:S(2)}) %collective-permute-start.1) | collective-permute-done | bytes 524320 | tf_op jit(solution)/shard_map/ppermute | solution.py:270
  28.3 0.7 collective-permute-start.3
  29.0 0.6 shard_map.41.own_b
  29.6 3.2 %collective-permute-start.9 = (bf16[512,512]{1,0:T(8,128)(2,1)S(1)}, bf16[512,512]{1,0:T(8,128)(2,1)S(1)}, u32[]{:S(2)}, u32[]{:S(2)}) collective-permute-start(bf16[512,512]{1,0:T(8,128)(2,1)S(1)} %shard_map.41.own_b), channel_id=1, source_target_pairs={{0,1},{1,0},{2,3},{3,2},{4,5},{5,4},{6,7},{7,6},{8,9},{9,8},{10,11... | collective-permute-start | bytes 1572872 | tf_op jit(solution)/shard_map/ppermute | solution.py:250
  32.8 1.3 collective-permute-done.2.refs_2_
  34.8 1.8 %shard_map.42.masked.refs_3_.refs_5_ = bf16[1024,2048]{1,0:T(8,128)(2,1)S(1)} custom-call(s32[8,16]{1,0:T(8,128)S(1)} %copy-done.1, bf16[1024,2048]{1,0:T(8,128)(2,1)S(1)} %copy-done), custom_call_target="tpu_custom_call" | custom-call | flops 4194304 | bytes 4194304 | tf_op jit(solution)/shard_map/pallas_call | solution.py:48
  36.7 2.2 %shard_map.45 = (s16[128,2176]{1,0:T(8,128)(2,1)S(1)}, s16[128,2176]{1,0:T(8,128)(2,1)S(1)}) custom-call(s32[16]{0:T(128)S(1)} %dynamic-slice_bitcast_fusion.s, bf16[512,512]{1,0:T(8,128)(2,1)S(1)} %shard_map.39.own_a, bf16[512,512]{1,0:T(8,128)(2,1)S(1)} %collective-permute-done.4.other_a, bf16[512,512]{1,0:T(8,128)(2,1)S(1)} %shard_map.41.own_b, ...), custom_call_target="tpu_custom_call" | custom-call | flops 1073741824 | bytes 4194304 | tf_op jit(solution)/shard_map/pallas_call | solution.py:48
  38.9 0.9 collective-permute-start.12
  39.8 2.4 %collective-permute-start.10 = (s16[128,2176]{1,0:T(8,128)(2,1)S(1)}, s16[128,2176]{1,0:T(8,128)(2,1)S(1)}, u32[]{:S(2)}, u32[]{:S(2)}) collective-permute-start(s16[128,2176]{1,0:T(8,128)(2,1)S(1)} %get-tuple-element.27), channel_id=1, source_target_pairs={{0,32},{1,9},{2,34},{3,11},{4,36},{5,13},{6,38},{7,15},{8,40},{9,1... | collective-permute-start | bytes 1671176 | tf_op jit(solution)/shard_map/ppermute | solution.py:238
  42.2 1.9 %shard_map.47.mine = f32[256,2048]{1,0:T(8,128)S(1)} custom-call(s32[16]{0:T(128)S(1)} %dynamic-slice_bitcast_fusion.s, bf16[512,512]{1,0:T(8,128)(2,1)S(1)} %shard_map.39.own_a, bf16[512,512]{1,0:T(8,128)(2,1)S(1)} %collective-permute-done.4.other_a, bf16[512,512]{1,0:T(8,128)(2,1)S(1)} %shard_map.41.own_b, ...), custom_call_target="tpu_custom_call" | custom-call | flops 1073741824 | bytes 4194304 | tf_op jit(solution)/shard_map/pallas_call | solution.py:48
  44.1 1.9 %shard_map.44.mine = f32[256,2048]{1,0:T(8,128)S(1)} custom-call(s32[16]{0:T(128)S(1)} %dynamic-slice_bitcast_fusion.s, bf16[512,512]{1,0:T(8,128)(2,1)S(1)} %shard_map.39.own_a, bf16[512,512]{1,0:T(8,128)(2,1)S(1)} %collective-permute-done.4.other_a, bf16[512,512]{1,0:T(8,128)(2,1)S(1)} %shard_map.41.own_b, ...), custom_call_target="tpu_custom_call" | custom-call | flops 1073741824 | bytes 4194304 | tf_op jit(solution)/shard_map/pallas_call | solution.py:48
  46.0 3.7 %collective-permute-done.12.came = s16[128,2176]{1,0:T(8,128)(2,1)S(1)} collective-permute-done((s16[128,2176]{1,0:T(8,128)(2,1)S(1)}, s16[128,2176]{1,0:T(8,128)(2,1)S(1)}, u32[]{:S(2)}, u32[]{:S(2)}) %collective-permute-start.12) | collective-permute-done | bytes 557088 | tf_op jit(solution)/shard_map/ppermute | solution.py:238
  50.9 3.3 %collective-permute-start.11 = (s16[256,2176]{1,0:T(8,128)(2,1)S(1)}, s16[256,2176]{1,0:T(8,128)(2,1)S(1)}, u32[]{:S(2)}, u32[]{:S(2)}) collective-permute-start(s16[256,2176]{1,0:T(8,128)(2,1)S(1)} %shard_map.46), channel_id=1, source_target_pairs={{0,32},{1,9},{2,34},{3,11},{4,36},{5,13},{6,38},{7,15},{8,40},{9,1... | collective-permute-start | bytes 3342344 | tf_op jit(solution)/shard_map/ppermute | solution.py:238
  54.2 2.1 %shard_map.43.own = f32[256,2048]{1,0:T(8,128)S(1)} custom-call(s32[16]{0:T(128)S(1)} %dynamic-slice_bitcast_fusion.s, bf16[512,512]{1,0:T(8,128)(2,1)S(1)} %shard_map.39.own_a, bf16[512,512]{1,0:T(8,128)(2,1)S(1)} %collective-permute-done.4.other_a, bf16[512,512]{1,0:T(8,128)(2,1)S(1)} %shard_map.41.own_b, ...), custom_call_target="tpu_custom_call" | custom-call | flops 1073741824 | bytes 4194304 | tf_op jit(solution)/shard_map/pallas_call | solution.py:48
  56.3 10.8 %collective-permute-done.13.b = s16[256,2176]{1,0:T(8,128)(2,1)S(1)} collective-permute-done((s16[256,2176]{1,0:T(8,128)(2,1)S(1)}, s16[256,2176]{1,0:T(8,128)(2,1)S(1)}, u32[]{:S(2)}, u32[]{:S(2)}) %collective-permute-start.13) | collective-permute-done | bytes 1114144 | tf_op jit(solution)/shard_map/ppermute | solution.py:238
  67.2 1.4 shard_map.49
  68.6 6.7 %collective-permute-start.14 = (s16[64,2176]{1,0:T(8,128)(2,1)S(1)}, s16[64,2176]{1,0:T(8,128)(2,1)S(1)}, u32[]{:S(2)}, u32[]{:S(2)}) collective-permute-start(s16[64,2176]{1,0:T(8,128)(2,1)S(1)} %get-tuple-element.30), channel_id=1, source_target_pairs={{0,16},{1,65},{2,18},{3,67},{4,20},{5,69},{6,22},{7,71},{8,24},{9,... | collective-permute-start | bytes 835592 | tf_op jit(solution)/shard_map/ppermute | solution.py:238
  75.4 3.2 %collective-permute-start.16 = (s16[64,2176]{1,0:T(8,128)(2,1)S(1)}, s16[64,2176]{1,0:T(8,128)(2,1)S(1)}, u32[]{:S(2)}, u32[]{:S(2)}) collective-permute-start(s16[64,2176]{1,0:T(8,128)(2,1)S(1)} %get-tuple-element.32), channel_id=1, source_target_pairs={{0,24},{1,97},{2,26},{3,99},{4,28},{5,101},{6,30},{7,103},{8,0},{9... | collective-permute-start | bytes 835592 | tf_op jit(solution)/shard_map/ppermute | solution.py:238
  78.6 1.3 collective-permute-done.14.a
  79.9 3.2 %collective-permute-done.15.b = s16[64,2176]{1,0:T(8,128)(2,1)S(1)} collective-permute-done((s16[64,2176]{1,0:T(8,128)(2,1)S(1)}, s16[64,2176]{1,0:T(8,128)(2,1)S(1)}, u32[]{:S(2)}, u32[]{:S(2)}) %collective-permute-start.15) | collective-permute-done | bytes 278560 | tf_op jit(solution)/shard_map/ppermute | solution.py:238
  83.5 1.9 %collective-permute-start.17 = (s16[64,2176]{1,0:T(8,128)(2,1)S(1)}, s16[64,2176]{1,0:T(8,128)(2,1)S(1)}, u32[]{:S(2)}, u32[]{:S(2)}) collective-permute-start(s16[64,2176]{1,0:T(8,128)(2,1)S(1)} %shard_map.50.refs_0_), channel_id=1, source_target_pairs={{0,8},{1,33},{2,10},{3,35},{4,12},{5,37},{6,14},{7,39},{8,16},{9,4... | collective-permute-start | bytes 835592 | tf_op jit(solution)/shard_map/ppermute | solution.py:238
  85.4 2.9 %collective-permute-start.18 = (s16[64,2176]{1,0:T(8,128)(2,1)S(1)}, s16[64,2176]{1,0:T(8,128)(2,1)S(1)}, u32[]{:S(2)}, u32[]{:S(2)}) collective-permute-start(s16[64,2176]{1,0:T(8,128)(2,1)S(1)} %shard_map.50.refs_0_), channel_id=1, source_target_pairs={{0,16},{1,65},{2,18},{3,67},{4,20},{5,69},{6,22},{7,71},{8,24},{9,... | collective-permute-start | bytes 835592 | tf_op jit(solution)/shard_map/ppermute | solution.py:238
  88.3 3.1 %collective-permute-done.17.refs_1_ = s16[64,2176]{1,0:T(8,128)(2,1)S(1)} collective-permute-done((s16[64,2176]{1,0:T(8,128)(2,1)S(1)}, s16[64,2176]{1,0:T(8,128)(2,1)S(1)}, u32[]{:S(2)}, u32[]{:S(2)}) %collective-permute-start.17) | collective-permute-done | bytes 278560 | tf_op jit(solution)/shard_map/ppermute | solution.py:238
  91.3 6.9 %collective-permute-done.18.refs_2_ = s16[64,2176]{1,0:T(8,128)(2,1)S(1)} collective-permute-done((s16[64,2176]{1,0:T(8,128)(2,1)S(1)}, s16[64,2176]{1,0:T(8,128)(2,1)S(1)}, u32[]{:S(2)}, u32[]{:S(2)}) %collective-permute-start.18) | collective-permute-done | bytes 278560 | tf_op jit(solution)/shard_map/ppermute | solution.py:238
  98.3 7.1 %collective-permute-start.20 = (s16[256,2176]{1,0:T(8,128)(2,1)S(1)}, s16[256,2176]{1,0:T(8,128)(2,1)S(1)}, u32[]{:S(2)}, u32[]{:S(2)}) collective-permute-start(s16[256,2176]{1,0:T(8,128)(2,1)S(1)} %shard_map.51.refs_0_), channel_id=1, source_target_pairs={{0,32},{1,9},{2,34},{3,11},{4,36},{5,13},{6,38},{7,15},{8,40},{9,1... | collective-permute-start | bytes 3342344 | tf_op jit(solution)/shard_map/ppermute | solution.py:238
  105.5 13.0 %collective-permute-done.20.refs_1_ = s16[256,2176]{1,0:T(8,128)(2,1)S(1)} collective-permute-done((s16[256,2176]{1,0:T(8,128)(2,1)S(1)}, s16[256,2176]{1,0:T(8,128)(2,1)S(1)}, u32[]{:S(2)}, u32[]{:S(2)}) %collective-permute-start.20) | collective-permute-done | bytes 1114144 | tf_op jit(solution)/shard_map/ppermute | solution.py:238
  118.5 3.8 %collective-permute-start.25 = (s16[128,2176]{1,0:T(8,128)(2,1)S(1)}, s16[128,2176]{1,0:T(8,128)(2,1)S(1)}, u32[]{:S(2)}, u32[]{:S(2)}) collective-permute-start(s16[128,2176]{1,0:T(8,128)(2,1)S(1)} %slice.12), channel_id=1, source_target_pairs={{0,32},{1,9},{2,34},{3,11},{4,36},{5,13},{6,38},{7,15},{8,40},{9,1... | collective-permute-start | bytes 1671176 | tf_op jit(solution)/shard_map/ppermute | solution.py:238
  122.4 4.0 %shard_map.52 = (f32[256,1024]{1,0:T(8,128)S(1)}, f32[256,1024]{1,0:T(8,128)S(1)}) custom-call(s32[16]{0:T(128)S(1)} %dynamic-slice_bitcast_fusion.s, s16[256,2176]{1,0:T(8,128)(2,1)S(1)} %shard_map.51.refs_0_, s16[256,2176]{1,0:T(8,128)(2,1)S(1)} %collective-permute-done.20.refs_1_, s16[256,2176]{1,0:T(8,128)(2,1)S(1)} %collective-permute-done.21.refs_2_, ...), custom_call_target="tpu_custom_call" | custom-call | flops 2147483648 | bytes 4194304 | tf_op jit(solution)/shard_map/pallas_call | solution.py:48
  126.5 2.9 %collective-permute-done.25.refs_3_ = s16[128,2176]{1,0:T(8,128)(2,1)S(1)} collective-permute-done((s16[128,2176]{1,0:T(8,128)(2,1)S(1)}, s16[128,2176]{1,0:T(8,128)(2,1)S(1)}, u32[]{:S(2)}, u32[]{:S(2)}) %collective-permute-start.25) | collective-permute-done | bytes 557088 | tf_op jit(solution)/shard_map/ppermute | solution.py:238
  129.3 3.8 %collective-permute-done.26.refs_4_ = s16[128,2176]{1,0:T(8,128)(2,1)S(1)} collective-permute-done((s16[128,2176]{1,0:T(8,128)(2,1)S(1)}, s16[128,2176]{1,0:T(8,128)(2,1)S(1)}, u32[]{:S(2)}, u32[]{:S(2)}) %collective-permute-start.26) | collective-permute-done | bytes 557088 | tf_op jit(solution)/shard_map/ppermute | solution.py:238
  133.2 4.2 %shard_map.54 = (f32[256,1024]{1,0:T(8,128)S(1)}, f32[256,1024]{1,0:T(8,128)S(1)}) custom-call(s32[16]{0:T(128)S(1)} %dynamic-slice_bitcast_fusion.s, s16[256,2176]{1,0:T(8,128)(2,1)S(1)} %shard_map.51.refs_0_, s16[256,2176]{1,0:T(8,128)(2,1)S(1)} %collective-permute-done.20.refs_1_, s16[256,2176]{1,0:T(8,128)(2,1)S(1)} %collective-permute-done.21.refs_2_, ...), custom_call_target="tpu_custom_call" | custom-call | flops 2147483648 | bytes 4194304 | tf_op jit(solution)/shard_map/pallas_call | solution.py:48
  137.8 0.7 collective-permute-start.23
  138.5 9.3 %collective-permute-start.24 = (s16[128,1152]{1,0:T(8,128)(2,1)S(1)}, s16[128,1152]{1,0:T(8,128)(2,1)S(1)}, u32[]{:S(2)}, u32[]{:S(2)}) collective-permute-start(s16[128,1152]{1,0:T(8,128)(2,1)S(1)} %get-tuple-element.36), channel_id=1, source_target_pairs={{0,2},{1,3},{2,4},{3,5},{4,6},{5,7},{6,0},{7,1},{8,10},{9,11},{10,... | collective-permute-start | bytes 884744 | tf_op jit(solution)/shard_map/ppermute | solution.py:238
  148.0 1.9 %collective-permute-start.28 = (s16[128,1152]{1,0:T(8,128)(2,1)S(1)}, s16[128,1152]{1,0:T(8,128)(2,1)S(1)}, u32[]{:S(2)}, u32[]{:S(2)}) collective-permute-start(s16[128,1152]{1,0:T(8,128)(2,1)S(1)} %get-tuple-element.39), channel_id=1, source_target_pairs={{0,6},{1,7},{2,0},{3,1},{4,2},{5,3},{6,4},{7,5},{8,12},{9,13},{10,... | collective-permute-start | bytes 884744 | tf_op jit(solution)/shard_map/ppermute | solution.py:238
  150.0 5.2 %collective-permute-start.29 = (s16[128,1152]{1,0:T(8,128)(2,1)S(1)}, s16[128,1152]{1,0:T(8,128)(2,1)S(1)}, u32[]{:S(2)}, u32[]{:S(2)}) collective-permute-start(s16[128,1152]{1,0:T(8,128)(2,1)S(1)} %get-tuple-element.40), channel_id=1, source_target_pairs={{0,4},{1,5},{2,6},{3,7},{4,0},{5,1},{6,2},{7,3},{8,14},{9,15},{10,... | collective-permute-start | bytes 884744 | tf_op jit(solution)/shard_map/ppermute | solution.py:238
  155.2 5.7 %collective-permute-done.28.c = s16[128,1152]{1,0:T(8,128)(2,1)S(1)} collective-permute-done((s16[128,1152]{1,0:T(8,128)(2,1)S(1)}, s16[128,1152]{1,0:T(8,128)(2,1)S(1)}, u32[]{:S(2)}, u32[]{:S(2)}) %collective-permute-start.28) | collective-permute-done | bytes 294944 | tf_op jit(solution)/shard_map/ppermute | solution.py:238
  160.9 5.7 %collective-permute-done.29.d = s16[128,1152]{1,0:T(8,128)(2,1)S(1)} collective-permute-done((s16[128,1152]{1,0:T(8,128)(2,1)S(1)}, s16[128,1152]{1,0:T(8,128)(2,1)S(1)}, u32[]{:S(2)}, u32[]{:S(2)}) %collective-permute-start.29) | collective-permute-done | bytes 294944 | tf_op jit(solution)/shard_map/ppermute | solution.py:238
  166.7 1.1 shard_map.56
  (40 shorter events, 5.3 us)
Async XLA Ops:
  0.0 1.8 %copy-start.1 = (s32[8,16]{1,0:T(8,128)S(1)}, s32[8,16]{1,0:T(8,128)}, u32[]{:S(2)}) copy-start(s32[8,16]{1,0:T(8,128)} %m.3) | copy-start | bytes 1540
  2.9 2.0 %collective-permute-start.5 = (bf16[512,512]{1,0:T(8,128)(2,1)S(1)}, bf16[512,512]{1,0:T(8,128)(2,1)S(1)}, u32[]{:S(2)}, u32[]{:S(2)}) collective-permute-start(bf16[512,512]{1,0:T(8,128)(2,1)S(1)} %get-tuple-element.26), channel_id=1, source_target_pairs={{0,1},{1,0},{2,3},{3,2},{4,5},{5,4},{6,7},{7,6},{8,9},{9,8},{10,11... | collective-permute-start | bytes 1572872 | tf_op jit(solution)/shard_map/ppermute | solution.py:268
  3.0 6.4 %collective-permute-start = (bf16[512,512]{1,0:T(8,128)(2,1)S(1)}, bf16[512,512]{1,0:T(8,128)(2,1)S(1)}, u32[]{:S(2)}, u32[]{:S(2)}) collective-permute-start(bf16[512,512]{1,0:T(8,128)(2,1)S(1)} %get-tuple-element.24), channel_id=1, source_target_pairs={{0,1},{1,0},{2,3},{3,2},{4,5},{5,4},{6,7},{7,6},{8,9},{9,8},{10,11... | collective-permute-start | bytes 1572872 | tf_op jit(solution)/shard_map/ppermute | solution.py:268
  5.5 11.6 %collective-permute-start.6 = (bf16[512,512]{1,0:T(8,128)(2,1)S(1)}, bf16[512,512]{1,0:T(8,128)(2,1)S(1)}, u32[]{:S(2)}, u32[]{:S(2)}) collective-permute-start(bf16[512,512]{1,0:T(8,128)(2,1)S(1)} %shard_map.40.refs_0_), channel_id=1, source_target_pairs={{0,2},{1,7},{8,10},{9,15},{16,18},{17,23},{24,26},{25,31},{32,34},... | collective-permute-start | bytes 1572872 | tf_op jit(solution)/shard_map/ppermute | solution.py:270
  9.9 18.3 %collective-permute-start.1 = (bf16[512,512]{1,0:T(8,128)(2,1)S(1)}, bf16[512,512]{1,0:T(8,128)(2,1)S(1)}, u32[]{:S(2)}, u32[]{:S(2)}) collective-permute-start(bf16[512,512]{1,0:T(8,128)(2,1)S(1)} %shard_map.38.refs_0_), channel_id=1, source_target_pairs={{0,2},{1,7},{8,10},{9,15},{16,18},{17,23},{24,26},{25,31},{32,34},... | collective-permute-start | bytes 1572872 | tf_op jit(solution)/shard_map/ppermute | solution.py:270
  11.3 17.7 %collective-permute-start.7 = (bf16[512,512]{1,0:T(8,128)(2,1)S(1)}, bf16[512,512]{1,0:T(8,128)(2,1)S(1)}, u32[]{:S(2)}, u32[]{:S(2)}) collective-permute-start(bf16[512,512]{1,0:T(8,128)(2,1)S(1)} %shard_map.40.refs_0_), channel_id=1, source_target_pairs={{0,6},{1,3},{8,14},{9,11},{16,22},{17,19},{24,30},{25,27},{32,38},... | collective-permute-start | bytes 1572872 | tf_op jit(solution)/shard_map/ppermute | solution.py:271
  17.0 11.9 %collective-permute-start.8 = (bf16[512,512]{1,0:T(8,128)(2,1)S(1)}, bf16[512,512]{1,0:T(8,128)(2,1)S(1)}, u32[]{:S(2)}, u32[]{:S(2)}) collective-permute-start(bf16[512,512]{1,0:T(8,128)(2,1)S(1)} %collective-permute-done.6.refs_1_), channel_id=1, source_target_pairs={{2,4},{7,5},{10,12},{15,13},{18,20},{23,21},{26,28},{31,29},{34,36... | collective-permute-start | bytes 1572872 | tf_op jit(solution)/shard_map/ppermute | solution.py:272
  17.7 16.4 %collective-permute-start.2 = (bf16[512,512]{1,0:T(8,128)(2,1)S(1)}, bf16[512,512]{1,0:T(8,128)(2,1)S(1)}, u32[]{:S(2)}, u32[]{:S(2)}) collective-permute-start(bf16[512,512]{1,0:T(8,128)(2,1)S(1)} %shard_map.38.refs_0_), channel_id=1, source_target_pairs={{0,6},{1,3},{8,14},{9,11},{16,22},{17,19},{24,30},{25,27},{32,38},... | collective-permute-start | bytes 1572872 | tf_op jit(solution)/shard_map/ppermute | solution.py:271
  28.3 5.8 %collective-permute-start.3 = (bf16[512,512]{1,0:T(8,128)(2,1)S(1)}, bf16[512,512]{1,0:T(8,128)(2,1)S(1)}, u32[]{:S(2)}, u32[]{:S(2)}) collective-permute-start(bf16[512,512]{1,0:T(8,128)(2,1)S(1)} %collective-permute-done.1.refs_1_), channel_id=1, source_target_pairs={{2,4},{7,5},{10,12},{15,13},{18,20},{23,21},{26,28},{31,29},{34,36... | collective-permute-start | bytes 1572872 | tf_op jit(solution)/shard_map/ppermute | solution.py:272
  29.0 5.8 %copy-start = (bf16[1024,2048]{1,0:T(8,128)(2,1)S(1)}, bf16[1024,2048]{1,0:T(8,128)(2,1)}, u32[]{:S(2)}) copy-start(bf16[1024,2048]{1,0:T(8,128)(2,1)} %density.1) | copy-start | bytes 12582916
  29.6 7.0 %collective-permute-start.9 = (bf16[512,512]{1,0:T(8,128)(2,1)S(1)}, bf16[512,512]{1,0:T(8,128)(2,1)S(1)}, u32[]{:S(2)}, u32[]{:S(2)}) collective-permute-start(bf16[512,512]{1,0:T(8,128)(2,1)S(1)} %shard_map.41.own_b), channel_id=1, source_target_pairs={{0,1},{1,0},{2,3},{3,2},{4,5},{5,4},{6,7},{7,6},{8,9},{9,8},{10,11... | collective-permute-start | bytes 1572872 | tf_op jit(solution)/shard_map/ppermute | solution.py:250
  34.7 2.0 %collective-permute-start.4 = (bf16[512,512]{1,0:T(8,128)(2,1)S(1)}, bf16[512,512]{1,0:T(8,128)(2,1)S(1)}, u32[]{:S(2)}, u32[]{:S(2)}) collective-permute-start(bf16[512,512]{1,0:T(8,128)(2,1)S(1)} %shard_map.39.own_a), channel_id=1, source_target_pairs={{0,1},{1,0},{2,3},{3,2},{4,5},{5,4},{6,7},{7,6},{8,9},{9,8},{10,11... | collective-permute-start | bytes 1572872 | tf_op jit(solution)/shard_map/ppermute | solution.py:250
  38.9 10.8 %collective-permute-start.12 = (s16[128,2176]{1,0:T(8,128)(2,1)S(1)}, s16[128,2176]{1,0:T(8,128)(2,1)S(1)}, u32[]{:S(2)}, u32[]{:S(2)}) collective-permute-start(s16[128,2176]{1,0:T(8,128)(2,1)S(1)} %get-tuple-element.28), channel_id=1, source_target_pairs={{0,96},{1,25},{2,98},{3,27},{4,100},{5,29},{6,102},{7,31},{8,104},... | collective-permute-start | bytes 1671176 | tf_op jit(solution)/shard_map/ppermute | solution.py:238
  39.8 10.5 %collective-permute-start.10 = (s16[128,2176]{1,0:T(8,128)(2,1)S(1)}, s16[128,2176]{1,0:T(8,128)(2,1)S(1)}, u32[]{:S(2)}, u32[]{:S(2)}) collective-permute-start(s16[128,2176]{1,0:T(8,128)(2,1)S(1)} %get-tuple-element.27), channel_id=1, source_target_pairs={{0,32},{1,9},{2,34},{3,11},{4,36},{5,13},{6,38},{7,15},{8,40},{9,1... | collective-permute-start | bytes 1671176 | tf_op jit(solution)/shard_map/ppermute | solution.py:238
  50.3 16.8 %collective-permute-start.13 = (s16[256,2176]{1,0:T(8,128)(2,1)S(1)}, s16[256,2176]{1,0:T(8,128)(2,1)S(1)}, u32[]{:S(2)}, u32[]{:S(2)}) collective-permute-start(s16[256,2176]{1,0:T(8,128)(2,1)S(1)} %shard_map.48), channel_id=1, source_target_pairs={{0,96},{1,25},{2,98},{3,27},{4,100},{5,29},{6,102},{7,31},{8,104},... | collective-permute-start | bytes 3342344 | tf_op jit(solution)/shard_map/ppermute | solution.py:238
  50.9 16.3 %collective-permute-start.11 = (s16[256,2176]{1,0:T(8,128)(2,1)S(1)}, s16[256,2176]{1,0:T(8,128)(2,1)S(1)}, u32[]{:S(2)}, u32[]{:S(2)}) collective-permute-start(s16[256,2176]{1,0:T(8,128)(2,1)S(1)} %shard_map.46), channel_id=1, source_target_pairs={{0,32},{1,9},{2,34},{3,11},{4,36},{5,13},{6,38},{7,15},{8,40},{9,1... | collective-permute-start | bytes 3342344 | tf_op jit(solution)/shard_map/ppermute | solution.py:238
  68.6 11.3 %collective-permute-start.14 = (s16[64,2176]{1,0:T(8,128)(2,1)S(1)}, s16[64,2176]{1,0:T(8,128)(2,1)S(1)}, u32[]{:S(2)}, u32[]{:S(2)}) collective-permute-start(s16[64,2176]{1,0:T(8,128)(2,1)S(1)} %get-tuple-element.30), channel_id=1, source_target_pairs={{0,16},{1,65},{2,18},{3,67},{4,20},{5,69},{6,22},{7,71},{8,24},{9,... | collective-permute-start | bytes 835592 | tf_op jit(solution)/shard_map/ppermute | solution.py:238
  75.4 7.8 %collective-permute-start.15 = (s16[64,2176]{1,0:T(8,128)(2,1)S(1)}, s16[64,2176]{1,0:T(8,128)(2,1)S(1)}, u32[]{:S(2)}, u32[]{:S(2)}) collective-permute-start(s16[64,2176]{1,0:T(8,128)(2,1)S(1)} %get-tuple-element.31), channel_id=1, source_target_pairs={{0,8},{1,33},{2,10},{3,35},{4,12},{5,37},{6,14},{7,39},{8,16},{9,4... | collective-permute-start | bytes 835592 | tf_op jit(solution)/shard_map/ppermute | solution.py:238
  75.4 7.8 %collective-permute-start.16 = (s16[64,2176]{1,0:T(8,128)(2,1)S(1)}, s16[64,2176]{1,0:T(8,128)(2,1)S(1)}, u32[]{:S(2)}, u32[]{:S(2)}) collective-permute-start(s16[64,2176]{1,0:T(8,128)(2,1)S(1)} %get-tuple-element.32), channel_id=1, source_target_pairs={{0,24},{1,97},{2,26},{3,99},{4,28},{5,101},{6,30},{7,103},{8,0},{9... | collective-permute-start | bytes 835592 | tf_op jit(solution)/shard_map/ppermute | solution.py:238
  83.5 7.8 %collective-permute-start.17 = (s16[64,2176]{1,0:T(8,128)(2,1)S(1)}, s16[64,2176]{1,0:T(8,128)(2,1)S(1)}, u32[]{:S(2)}, u32[]{:S(2)}) collective-permute-start(s16[64,2176]{1,0:T(8,128)(2,1)S(1)} %shard_map.50.refs_0_), channel_id=1, source_target_pairs={{0,8},{1,33},{2,10},{3,35},{4,12},{5,37},{6,14},{7,39},{8,16},{9,4... | collective-permute-start | bytes 835592 | tf_op jit(solution)/shard_map/ppermute | solution.py:238
  85.4 12.9 %collective-permute-start.18 = (s16[64,2176]{1,0:T(8,128)(2,1)S(1)}, s16[64,2176]{1,0:T(8,128)(2,1)S(1)}, u32[]{:S(2)}, u32[]{:S(2)}) collective-permute-start(s16[64,2176]{1,0:T(8,128)(2,1)S(1)} %shard_map.50.refs_0_), channel_id=1, source_target_pairs={{0,16},{1,65},{2,18},{3,67},{4,20},{5,69},{6,22},{7,71},{8,24},{9,... | collective-permute-start | bytes 835592 | tf_op jit(solution)/shard_map/ppermute | solution.py:238
  88.3 10.0 %collective-permute-start.19 = (s16[64,2176]{1,0:T(8,128)(2,1)S(1)}, s16[64,2176]{1,0:T(8,128)(2,1)S(1)}, u32[]{:S(2)}, u32[]{:S(2)}) collective-permute-start(s16[64,2176]{1,0:T(8,128)(2,1)S(1)} %shard_map.50.refs_0_), channel_id=1, source_target_pairs={{0,24},{1,97},{2,26},{3,99},{4,28},{5,101},{6,30},{7,103},{8,0},{9... | collective-permute-start | bytes 835592 | tf_op jit(solution)/shard_map/ppermute | solution.py:238
  98.3 20.2 %collective-permute-start.20 = (s16[256,2176]{1,0:T(8,128)(2,1)S(1)}, s16[256,2176]{1,0:T(8,128)(2,1)S(1)}, u32[]{:S(2)}, u32[]{:S(2)}) collective-permute-start(s16[256,2176]{1,0:T(8,128)(2,1)S(1)} %shard_map.51.refs_0_), channel_id=1, source_target_pairs={{0,32},{1,9},{2,34},{3,11},{4,36},{5,13},{6,38},{7,15},{8,40},{9,1... | collective-permute-start | bytes 3342344 | tf_op jit(solution)/shard_map/ppermute | solution.py:238
  105.5 16.8 %collective-permute-start.21 = (s16[256,2176]{1,0:T(8,128)(2,1)S(1)}, s16[256,2176]{1,0:T(8,128)(2,1)S(1)}, u32[]{:S(2)}, u32[]{:S(2)}) collective-permute-start(s16[256,2176]{1,0:T(8,128)(2,1)S(1)} %shard_map.51.refs_0_), channel_id=1, source_target_pairs={{0,96},{1,25},{2,98},{3,27},{4,100},{5,29},{6,102},{7,31},{8,104},... | collective-permute-start | bytes 3342344 | tf_op jit(solution)/shard_map/ppermute | solution.py:238
  118.5 10.8 %collective-permute-start.25 = (s16[128,2176]{1,0:T(8,128)(2,1)S(1)}, s16[128,2176]{1,0:T(8,128)(2,1)S(1)}, u32[]{:S(2)}, u32[]{:S(2)}) collective-permute-start(s16[128,2176]{1,0:T(8,128)(2,1)S(1)} %slice.12), channel_id=1, source_target_pairs={{0,32},{1,9},{2,34},{3,11},{4,36},{5,13},{6,38},{7,15},{8,40},{9,1... | collective-permute-start | bytes 1671176 | tf_op jit(solution)/shard_map/ppermute | solution.py:238
  122.3 10.8 %collective-permute-start.26 = (s16[128,2176]{1,0:T(8,128)(2,1)S(1)}, s16[128,2176]{1,0:T(8,128)(2,1)S(1)}, u32[]{:S(2)}, u32[]{:S(2)}) collective-permute-start(s16[128,2176]{1,0:T(8,128)(2,1)S(1)} %slice.13), channel_id=1, source_target_pairs={{0,96},{1,25},{2,98},{3,27},{4,100},{5,29},{6,102},{7,31},{8,104},... | collective-permute-start | bytes 1671176 | tf_op jit(solution)/shard_map/ppermute | solution.py:238
  126.4 11.1 %collective-permute-start.22 = (f32[256,1024]{1,0:T(8,128)S(1)}, f32[256,1024]{1,0:T(8,128)S(1)}, u32[]{:S(2)}, u32[]{:S(2)}) collective-permute-start(f32[256,1024]{1,0:T(8,128)S(1)} %get-tuple-element.34), channel_id=1, source_target_pairs={{0,1},{1,0},{2,3},{3,2},{4,5},{5,4},{6,7},{7,6},{8,9},{9,8},{10,11... | collective-permute-start | bytes 3145736 | tf_op jit(solution)/shard_map/ppermute | solution.py:250
  137.4 10.4 %collective-permute-start.27 = (f32[256,1024]{1,0:T(8,128)S(1)}, f32[256,1024]{1,0:T(8,128)S(1)}, u32[]{:S(2)}, u32[]{:S(2)}) collective-permute-start(f32[256,1024]{1,0:T(8,128)S(1)} %get-tuple-element.38), channel_id=1, source_target_pairs={{0,1},{1,0},{2,3},{3,2},{4,5},{5,4},{6,7},{7,6},{8,9},{9,8},{10,11... | collective-permute-start | bytes 3145736 | tf_op jit(solution)/shard_map/ppermute | solution.py:250
  137.8 17.4 %collective-permute-start.23 = (s16[128,1152]{1,0:T(8,128)(2,1)S(1)}, s16[128,1152]{1,0:T(8,128)(2,1)S(1)}, u32[]{:S(2)}, u32[]{:S(2)}) collective-permute-start(s16[128,1152]{1,0:T(8,128)(2,1)S(1)} %get-tuple-element.35), channel_id=1, source_target_pairs={{0,0},{1,1},{2,2},{3,3},{4,4},{5,5},{6,6},{7,7},{8,8},{9,9},{10,10... | collective-permute-start | bytes 884744 | tf_op jit(solution)/shard_map/ppermute | solution.py:238
  138.5 16.7 %collective-permute-start.24 = (s16[128,1152]{1,0:T(8,128)(2,1)S(1)}, s16[128,1152]{1,0:T(8,128)(2,1)S(1)}, u32[]{:S(2)}, u32[]{:S(2)}) collective-permute-start(s16[128,1152]{1,0:T(8,128)(2,1)S(1)} %get-tuple-element.36), channel_id=1, source_target_pairs={{0,2},{1,3},{2,4},{3,5},{4,6},{5,7},{6,0},{7,1},{8,10},{9,11},{10,... | collective-permute-start | bytes 884744 | tf_op jit(solution)/shard_map/ppermute | solution.py:238
  148.0 12.9 %collective-permute-start.28 = (s16[128,1152]{1,0:T(8,128)(2,1)S(1)}, s16[128,1152]{1,0:T(8,128)(2,1)S(1)}, u32[]{:S(2)}, u32[]{:S(2)}) collective-permute-start(s16[128,1152]{1,0:T(8,128)(2,1)S(1)} %get-tuple-element.39), channel_id=1, source_target_pairs={{0,6},{1,7},{2,0},{3,1},{4,2},{5,3},{6,4},{7,5},{8,12},{9,13},{10,... | collective-permute-start | bytes 884744 | tf_op jit(solution)/shard_map/ppermute | solution.py:238
  150.0 16.7 %collective-permute-start.29 = (s16[128,1152]{1,0:T(8,128)(2,1)S(1)}, s16[128,1152]{1,0:T(8,128)(2,1)S(1)}, u32[]{:S(2)}, u32[]{:S(2)}) collective-permute-start(s16[128,1152]{1,0:T(8,128)(2,1)S(1)} %get-tuple-element.40), channel_id=1, source_target_pairs={{0,4},{1,5},{2,6},{3,7},{4,0},{5,1},{6,2},{7,3},{8,14},{9,15},{10,... | collective-permute-start | bytes 884744 | tf_op jit(solution)/shard_map/ppermute | solution.py:238

commit v3 on v2

--- a/solution.py
+++ b/solution.py
@@ -27,16 +27,18 @@
 
 def facts(x, y, z, core):
     first, second = (y, x) if core else (x, y)
-    own = first + z
-    quarters = [(own + d) % 4 for d in range(4)]
-    chosen = [(first - q) % 4 for q in turns(x, y)]
-    row = x * 4 + y
+    own, odd = first + z, first % 2
+    step = -1 if odd else 1
+    quarters = [(own + d) % 4 for d in (0, step, 2, -step)]
+    codes = {0: 0, -step % 4: 1, step % 4: 2, 2: 4 if odd else 3}
+    chosen = [codes[(first - q) % 4] for q in turns(x, y)]
+    subs = [second, second ^ 1, second ^ 2, second ^ 3]
     source = 0 if z == 0 else 1 if z == 1 + 2 * core else 3 if z == 2 else 2
-    own_square = int(z * 2 + core == row // 2)
-    return [*quarters, *chosen, second, core, own_square, row % 2, source, 0, 0, 0]
-
-
-QUARTERS, CHOSEN, SECOND, CORE, OWNER, HALF, SOURCE = 0, 4, 8, 9, 10, 11, 12
+    own_square = int(z * 2 + core == (x * 4 + y) // 2)
+    return [*quarters, *chosen, *subs, core, own_square, y % 2, source, odd] + [0] * 15
+
+
+QUARTERS, CHOSEN, SUBS, CORE, OWNER, HALF, SOURCE, ODD = 0, 4, 8, 12, 13, 14, 15, 16
 
 
 def shape(rows, columns, dtype):
@@ -121,8 +123,8 @@
             left[512:], masked[at(1 - s[CORE], 512), columns], dims, preferred_element_type=F32
         )
     if d == 2:
-        put(outs[0], acc[:128])
-        put(outs[1], acc[128:])
+        for i, out in enumerate(outs):
+            put(out, acc[at(s[ODD] ^ i, 128), :])
 
 
 def first_product(d, s, parts, masked):
@@ -138,16 +140,19 @@
     )
 
 
-def push_kernel(start, mine, came, out):
-    add = slice(start, start + 128)
-    rest = slice(128 - start, 256 - start)
+def push_kernel(i, s, mine, came, out):
+    add, rest = at(s[ODD] ^ i, 128), at(s[ODD] ^ i ^ 1, 128)
     put(out.at[add], mine[add, :] + take(came))
     put(out.at[rest], mine[rest, :])
 
 
+def cut_kernel(i, s, v, out):
+    out[...] = v[at(s[ODD] ^ i, 128), :]
+
+
 def spread_kernel(s, own, a, b, *outs):
     for d, out in enumerate(outs):
-        rows = at((s[SECOND] + d) % 4, PIECE)
+        rows = at(s[SUBS + d], PIECE)
         v = own[rows, :] + take(a, rows) + take(b, rows)
         if d == 0:
             out[...] = v
@@ -167,10 +172,10 @@
 
 def second_kernel(turn, s, *refs):
     *quarters, masked, mine, theirs, left, triple = refs
-    own, back, ahead, *far = quarters
+    own, near, next_, *far = quarters
     starts = []
     for j in range(4):
-        sub = (s[SECOND] + 4 - j) % 4
+        sub = s[SUBS + j]
         starts.append(((sub // 2) ^ s[CORE]) * 256 + (sub % 2) * 64)
 
     def unpack(i, refs):
@@ -187,9 +192,9 @@
                     triple[rows, :] = 3.0 * v[:, half * SLAB : (half + 1) * SLAB]
 
     for i in range(2):
-        for shift, refs in ((0, [own]), (1, [back]), (3, [ahead]), (2, far)):
+        for code, refs in enumerate(([own], [near], [next_], far[::-1], far)):
             if refs:
-                pl.when(s[CHOSEN + turn + i] == shift)(functools.partial(unpack, i, refs))
+                pl.when(s[CHOSEN + turn + i] == code)(functools.partial(unpack, i, refs))
 
     for n in range(4):
         columns = slice(n * 256, (n + 1) * 256)
@@ -238,12 +243,12 @@
     return lax.ppermute(v, AXES, [(place(*d), place(*to(*d))) for d in DEVICES])
 
 
-def along(v, d):
-    return send(v, lambda x, y, z, core: (x, y + d, z, core) if core else (x + d, y, z, core))
-
-
-def across(v, d):
-    return send(v, lambda x, y, z, core: (x + d, y, z, core) if core else (x, y + d, z, core))
+def along(v, flip):
+    return send(v, lambda x, y, z, core: (x, y ^ flip, z, core) if core else (x ^ flip, y, z, core))
+
+
+def across(v, flip):
+    return send(v, lambda x, y, z, core: (x ^ flip, y, z, core) if core else (x, y ^ flip, z, core))
 
 
 def swap(v):
@@ -284,28 +289,35 @@
     parts += spread_column(s, top_b, low_b)
 
     wide = shape(QUARTER, WIDE + LANES, I16)
-    top, low = first_product(2, s, parts, masked)
-    top = along(top, 1)
-    low = along(low, -1)
-    ahead, back, mine = (first_product(d, s, parts, masked) for d in (1, 3, 0))
-    ahead = call(functools.partial(push_kernel, 0), wide, [], ahead, top)
-    ahead = along(ahead, 1)
-    back = call(functools.partial(push_kernel, 128), wide, [], back, low)
-    back = along(back, -1)
+    halves = first_product(2, s, parts, masked)
+    far = along(halves[1], 3)
+    near = along(halves[0], 1)
+    first, last, mine = (first_product(d, s, parts, masked) for d in (1, 3, 0))
+    first = call(functools.partial(push_kernel, 0), wide, [s], first, far)
+    first = along(first, 1)
+    last = call(functools.partial(push_kernel, 1), wide, [s], last, near)
+    last = along(last, 3)
     coded = shape(PIECE, WIDE + LANES, I16)
     outs = [shape(PIECE, WIDE, F32), coded, coded, coded]
-    mine, *pieces = call(spread_kernel, outs, [s], mine, ahead, back)
-    came = [across(pieces[d - 1], d) for d in (2, 1, 3)]
+    mine, *pieces = call(spread_kernel, outs, [s], mine, first, last)
+    came = []
+    for flip in (1, 2, 3):
+        came.append(across(pieces[flip - 1], flip))
     v = call(gather_kernel, coded, [], mine, *came)
 
-    pieces = [across(v, d) for d in (1, 2, 3)]
+    pieces = []
+    for flip in (1, 2, 3):
+        pieces.append(across(v, flip))
     own = call(join_kernel, wide, [], v, *pieces)
-    back, ahead = along(own, 1), along(own, -1)
-    top = along(back[:128], 1)
-    low = along(ahead[128:], -1)
+    near = along(own, 1)
+    next_ = along(own, 3)
+    half = shape(128, WIDE + LANES, I16)
+    cut = [call(functools.partial(cut_kernel, i), half, [s], v) for i, v in enumerate((next_, near))]
+    far = [along(cut[0], 1)]
+    far += [along(cut[1], 3)]
     came = []
     for i in (0, 2):
-        quarters = [own, back, ahead] + [top, low] * (i == 2)
+        quarters = [own, near, next_] + far * (i == 2)
         mine, theirs = second_product(i, s, quarters, masked)
         theirs = swap(theirs)
         outs = [shape(128, SLAB + LANES, I16)] * 2

time: 168 us -> 164 us (0.976)
  the two profiles are of different devices: /device:TPU:6 before, /device:TPU:24 now
where the time goes in v3:
time: 164 us
  waiting for transfers between devices  82.8 us (50%)
  starting transfers between devices  49.8 us (30%)
  Pallas kernels  28.4 us (17%)
  local copies, waits for them, and re-layouts  2.48 us (2%)
    ppermute x18, waiting for transfers between devices, send(): return lax.ppermute(v, AXES, [(place(*d), place(*to(*d))) for d in DEVICES])  67.9 us
    ppermute x18, starting transfers between devices, send(): return lax.ppermute(v, AXES, [(place(*d), place(*to(*d))) for d in DEVICES])  35.7 us
    pallas_call x22, Pallas kernels, call(): pl.pallas_call(kernel, out_shape=out, in_specs=[pl.BlockSpec(memory_space...  28.4 us
    ppermute x2, waiting for transfers between devices, spread_column(): one = lax.ppermute(half, axes, [(0, 2), (1, 7)])  12.8 us
    ppermute x2, starting transfers between devices, spread_column(): one = lax.ppermute(half, axes, [(0, 2), (1, 7)])  5.18 us
    ppermute x2, starting transfers between devices, spread_column(): two = lax.ppermute(half, axes, [(0, 6), (1, 3)])  3.51 us
    ppermute x4, starting transfers between devices, swap(): return lax.ppermute(v, 'core', [(0, 1), (1, 0)])  3.44 us
  transfers between devices with their start and end apart: 30, of which 19 were waited for; matrix products, arithmetic and copies ran while one was open for 0% of the time, Pallas kernels for 14%

profile of v3, /device:TPU:24, one launch (start us, length us, event | category | flops | bytes accessed | tf_op | source)
XLA Modules:
  0.0 163.8 jit_solution(3765686622593834926)
XLA Ops:
  0.0 1.8 %slice.3.density = bf16[1024,1024]{1,0:T(8,128)(2,1)S(1)} slice(bf16[1024,2048]{1,0:T(8,128)(2,1)} %density.1), slice={[0:1024], [0:1024]} | slice | bytes 4194304 | tf_op jit(solution)/shard_map/slice | solution.py:286
  1.8 1.1 shard_map.37
  4.2 0.7 collective-permute-done.5.refs_1_
  5.5 3.9 %collective-permute-start.6 = (bf16[512,512]{1,0:T(8,128)(2,1)S(1)}, bf16[512,512]{1,0:T(8,128)(2,1)S(1)}, u32[]{:S(2)}, u32[]{:S(2)}) collective-permute-start(bf16[512,512]{1,0:T(8,128)(2,1)S(1)} %shard_map.40.refs_0_), channel_id=1, source_target_pairs={{0,2},{1,7},{8,10},{9,15},{16,18},{17,23},{24,26},{25,31},{32,34},... | collective-permute-start | bytes 1572872 | tf_op jit(solution)/shard_map/ppermute | solution.py:275
  9.9 1.3 collective-permute-start.1
  11.3 2.2 %collective-permute-start.7 = (bf16[512,512]{1,0:T(8,128)(2,1)S(1)}, bf16[512,512]{1,0:T(8,128)(2,1)S(1)}, u32[]{:S(2)}, u32[]{:S(2)}) collective-permute-start(bf16[512,512]{1,0:T(8,128)(2,1)S(1)} %shard_map.40.refs_0_), channel_id=1, source_target_pairs={{0,6},{1,3},{8,14},{9,11},{16,22},{17,19},{24,30},{25,27},{32,38},... | collective-permute-start | bytes 1572872 | tf_op jit(solution)/shard_map/ppermute | solution.py:276
  13.5 3.6 %collective-permute-done.6.refs_1_ = bf16[512,512]{1,0:T(8,128)(2,1)S(1)} collective-permute-done((bf16[512,512]{1,0:T(8,128)(2,1)S(1)}, bf16[512,512]{1,0:T(8,128)(2,1)S(1)}, u32[]{:S(2)}, u32[]{:S(2)}) %collective-permute-start.6) | collective-permute-done | bytes 524320 | tf_op jit(solution)/shard_map/ppermute | solution.py:275
  17.7 1.3 collective-permute-start.2
  19.1 9.2 %collective-permute-done.1.refs_1_ = bf16[512,512]{1,0:T(8,128)(2,1)S(1)} collective-permute-done((bf16[512,512]{1,0:T(8,128)(2,1)S(1)}, bf16[512,512]{1,0:T(8,128)(2,1)S(1)}, u32[]{:S(2)}, u32[]{:S(2)}) %collective-permute-start.1) | collective-permute-done | bytes 524320 | tf_op jit(solution)/shard_map/ppermute | solution.py:275
  29.6 3.2 %collective-permute-start.9 = (bf16[512,512]{1,0:T(8,128)(2,1)S(1)}, bf16[512,512]{1,0:T(8,128)(2,1)S(1)}, u32[]{:S(2)}, u32[]{:S(2)}) collective-permute-start(bf16[512,512]{1,0:T(8,128)(2,1)S(1)} %shard_map.41.own_b), channel_id=1, source_target_pairs={{0,1},{1,0},{2,3},{3,2},{4,5},{5,4},{6,7},{7,6},{8,9},{9,8},{10,11... | collective-permute-start | bytes 1572872 | tf_op jit(solution)/shard_map/ppermute | solution.py:255
  32.8 1.3 collective-permute-done.2.refs_2_
  34.8 1.8 %shard_map.42.masked.refs_3_.refs_5_ = bf16[1024,2048]{1,0:T(8,128)(2,1)S(1)} custom-call(s32[8,16]{1,0:T(8,128)S(1)} %copy-done.1, bf16[1024,2048]{1,0:T(8,128)(2,1)S(1)} %copy-done), custom_call_target="tpu_custom_call" | custom-call | flops 4194304 | bytes 4194304 | tf_op jit(solution)/shard_map/pallas_call | solution.py:50
  36.7 2.3 %shard_map.45 = (s16[128,2176]{1,0:T(8,128)(2,1)S(1)}, s16[128,2176]{1,0:T(8,128)(2,1)S(1)}) custom-call(s32[32]{0:T(128)S(1)} %dynamic-slice_bitcast_fusion.s, bf16[512,512]{1,0:T(8,128)(2,1)S(1)} %shard_map.39.own_a, bf16[512,512]{1,0:T(8,128)(2,1)S(1)} %collective-permute-done.4.other_a, bf16[512,512]{1,0:T(8,128)(2,1)S(1)} %shard_map.41.own_b, ...), custom_call_target="tpu_custom_call" | custom-call | flops 1073741824 | bytes 4194304 | tf_op jit(solution)/shard_map/pallas_call | solution.py:50
  39.0 1.6 collective-permute-start.12
  40.6 2.1 %collective-permute-start.10 = (s16[128,2176]{1,0:T(8,128)(2,1)S(1)}, s16[128,2176]{1,0:T(8,128)(2,1)S(1)}, u32[]{:S(2)}, u32[]{:S(2)}) collective-permute-start(s16[128,2176]{1,0:T(8,128)(2,1)S(1)} %get-tuple-element.27), channel_id=1, source_target_pairs={{0,96},{1,25},{2,98},{3,27},{4,100},{5,29},{6,102},{7,31},{8,104},... | collective-permute-start | bytes 1671176 | tf_op jit(solution)/shard_map/ppermute | solution.py:243
  42.7 1.9 %shard_map.47.mine = f32[256,2048]{1,0:T(8,128)S(1)} custom-call(s32[32]{0:T(128)S(1)} %dynamic-slice_bitcast_fusion.s, bf16[512,512]{1,0:T(8,128)(2,1)S(1)} %shard_map.39.own_a, bf16[512,512]{1,0:T(8,128)(2,1)S(1)} %collective-permute-done.4.other_a, bf16[512,512]{1,0:T(8,128)(2,1)S(1)} %shard_map.41.own_b, ...), custom_call_target="tpu_custom_call" | custom-call | flops 1073741824 | bytes 4194304 | tf_op jit(solution)/shard_map/pallas_call | solution.py:50
  44.6 1.9 %shard_map.44.mine = f32[256,2048]{1,0:T(8,128)S(1)} custom-call(s32[32]{0:T(128)S(1)} %dynamic-slice_bitcast_fusion.s, bf16[512,512]{1,0:T(8,128)(2,1)S(1)} %shard_map.39.own_a, bf16[512,512]{1,0:T(8,128)(2,1)S(1)} %collective-permute-done.4.other_a, bf16[512,512]{1,0:T(8,128)(2,1)S(1)} %shard_map.41.own_b, ...), custom_call_target="tpu_custom_call" | custom-call | flops 1073741824 | bytes 4194304 | tf_op jit(solution)/shard_map/pallas_call | solution.py:50
  46.5 2.2 %collective-permute-done.12.came = s16[128,2176]{1,0:T(8,128)(2,1)S(1)} collective-permute-done((s16[128,2176]{1,0:T(8,128)(2,1)S(1)}, s16[128,2176]{1,0:T(8,128)(2,1)S(1)}, u32[]{:S(2)}, u32[]{:S(2)}) %collective-permute-start.12) | collective-permute-done | bytes 557088 | tf_op jit(solution)/shard_map/ppermute | solution.py:243
  48.6 1.1 shard_map.48
  49.7 2.8 %collective-permute-start.13 = (s16[256,2176]{1,0:T(8,128)(2,1)S(1)}, s16[256,2176]{1,0:T(8,128)(2,1)S(1)}, u32[]{:S(2)}, u32[]{:S(2)}) collective-permute-start(s16[256,2176]{1,0:T(8,128)(2,1)S(1)} %shard_map.48), channel_id=1, source_target_pairs={{0,96},{1,25},{2,98},{3,27},{4,100},{5,29},{6,102},{7,31},{8,104},... | collective-permute-start | bytes 3342344 | tf_op jit(solution)/shard_map/ppermute | solution.py:243
  52.6 1.1 shard_map.46
  54.0 2.1 %shard_map.43.own = f32[256,2048]{1,0:T(8,128)S(1)} custom-call(s32[32]{0:T(128)S(1)} %dynamic-slice_bitcast_fusion.s, bf16[512,512]{1,0:T(8,128)(2,1)S(1)} %shard_map.39.own_a, bf16[512,512]{1,0:T(8,128)(2,1)S(1)} %collective-permute-done.4.other_a, bf16[512,512]{1,0:T(8,128)(2,1)S(1)} %shard_map.41.own_b, ...), custom_call_target="tpu_custom_call" | custom-call | flops 1073741824 | bytes 4194304 | tf_op jit(solution)/shard_map/pallas_call | solution.py:50
  56.0 10.5 %collective-permute-done.13.b = s16[256,2176]{1,0:T(8,128)(2,1)S(1)} collective-permute-done((s16[256,2176]{1,0:T(8,128)(2,1)S(1)}, s16[256,2176]{1,0:T(8,128)(2,1)S(1)}, u32[]{:S(2)}, u32[]{:S(2)}) %collective-permute-start.13) | collective-permute-done | bytes 1114144 | tf_op jit(solution)/shard_map/ppermute | solution.py:243
  66.5 2.7 %collective-permute-done.11.a = s16[256,2176]{1,0:T(8,128)(2,1)S(1)} collective-permute-done((s16[256,2176]{1,0:T(8,128)(2,1)S(1)}, s16[256,2176]{1,0:T(8,128)(2,1)S(1)}, u32[]{:S(2)}, u32[]{:S(2)}) %collective-permute-start.11) | collective-permute-done | bytes 1114144 | tf_op jit(solution)/shard_map/ppermute | solution.py:243
  69.2 1.4 shard_map.49
  70.6 0.8 collective-permute-start.14
  71.5 0.9 collective-permute-start.15
  72.4 3.0 %collective-permute-start.16 = (s16[64,2176]{1,0:T(8,128)(2,1)S(1)}, s16[64,2176]{1,0:T(8,128)(2,1)S(1)}, u32[]{:S(2)}, u32[]{:S(2)}) collective-permute-start(s16[64,2176]{1,0:T(8,128)(2,1)S(1)} %get-tuple-element.32), channel_id=1, source_target_pairs={{0,24},{1,97},{2,26},{3,99},{4,28},{5,101},{6,30},{7,103},{8,16},{... | collective-permute-start | bytes 835592 | tf_op jit(solution)/shard_map/ppermute | solution.py:243
  75.4 1.8 %collective-permute-done.14.a = s16[64,2176]{1,0:T(8,128)(2,1)S(1)} collective-permute-done((s16[64,2176]{1,0:T(8,128)(2,1)S(1)}, s16[64,2176]{1,0:T(8,128)(2,1)S(1)}, u32[]{:S(2)}, u32[]{:S(2)}) %collective-permute-start.14) | collective-permute-done | bytes 278560 | tf_op jit(solution)/shard_map/ppermute | solution.py:243
  77.3 2.7 %collective-permute-done.15.b = s16[64,2176]{1,0:T(8,128)(2,1)S(1)} collective-permute-done((s16[64,2176]{1,0:T(8,128)(2,1)S(1)}, s16[64,2176]{1,0:T(8,128)(2,1)S(1)}, u32[]{:S(2)}, u32[]{:S(2)}) %collective-permute-start.15) | collective-permute-done | bytes 278560 | tf_op jit(solution)/shard_map/ppermute | solution.py:243
  80.0 2.9 %collective-permute-done.16.c = s16[64,2176]{1,0:T(8,128)(2,1)S(1)} collective-permute-done((s16[64,2176]{1,0:T(8,128)(2,1)S(1)}, s16[64,2176]{1,0:T(8,128)(2,1)S(1)}, u32[]{:S(2)}, u32[]{:S(2)}) %collective-permute-start.16) | collective-permute-done | bytes 278560 | tf_op jit(solution)/shard_map/ppermute | solution.py:243
  83.4 4.5 %collective-permute-start.18 = (s16[64,2176]{1,0:T(8,128)(2,1)S(1)}, s16[64,2176]{1,0:T(8,128)(2,1)S(1)}, u32[]{:S(2)}, u32[]{:S(2)}) collective-permute-start(s16[64,2176]{1,0:T(8,128)(2,1)S(1)} %shard_map.50.refs_0_), channel_id=1, source_target_pairs={{0,16},{1,65},{2,18},{3,67},{4,20},{5,69},{6,22},{7,71},{8,24},{9,... | collective-permute-start | bytes 835592 | tf_op jit(solution)/shard_map/ppermute | solution.py:243
  88.0 1.8 %collective-permute-done.17.refs_1_ = s16[64,2176]{1,0:T(8,128)(2,1)S(1)} collective-permute-done((s16[64,2176]{1,0:T(8,128)(2,1)S(1)}, s16[64,2176]{1,0:T(8,128)(2,1)S(1)}, u32[]{:S(2)}, u32[]{:S(2)}) %collective-permute-start.17) | collective-permute-done | bytes 278560 | tf_op jit(solution)/shard_map/ppermute | solution.py:243
  89.9 5.5 %collective-permute-done.18.refs_2_ = s16[64,2176]{1,0:T(8,128)(2,1)S(1)} collective-permute-done((s16[64,2176]{1,0:T(8,128)(2,1)S(1)}, s16[64,2176]{1,0:T(8,128)(2,1)S(1)}, u32[]{:S(2)}, u32[]{:S(2)}) %collective-permute-start.18) | collective-permute-done | bytes 278560 | tf_op jit(solution)/shard_map/ppermute | solution.py:243
  95.4 5.1 %collective-permute-done.19.refs_3_ = s16[64,2176]{1,0:T(8,128)(2,1)S(1)} collective-permute-done((s16[64,2176]{1,0:T(8,128)(2,1)S(1)}, s16[64,2176]{1,0:T(8,128)(2,1)S(1)}, u32[]{:S(2)}, u32[]{:S(2)}) %collective-permute-start.19) | collective-permute-done | bytes 278560 | tf_op jit(solution)/shard_map/ppermute | solution.py:243
  100.7 1.0 collective-permute-start.20
  101.7 15.7 %collective-permute-done.21.refs_2_.v = s16[256,2176]{1,0:T(8,128)(2,1)S(1)} collective-permute-done((s16[256,2176]{1,0:T(8,128)(2,1)S(1)}, s16[256,2176]{1,0:T(8,128)(2,1)S(1)}, u32[]{:S(2)}, u32[]{:S(2)}) %collective-permute-start.21) | collective-permute-done | bytes 1114144 | tf_op jit(solution)/shard_map/ppermute | solution.py:243
  118.7 1.4 collective-permute-start.26
  120.1 3.9 %shard_map.52 = (f32[256,1024]{1,0:T(8,128)S(1)}, f32[256,1024]{1,0:T(8,128)S(1)}) custom-call(s32[32]{0:T(128)S(1)} %dynamic-slice_bitcast_fusion.s, s16[256,2176]{1,0:T(8,128)(2,1)S(1)} %shard_map.51.refs_0_, s16[256,2176]{1,0:T(8,128)(2,1)S(1)} %collective-permute-done.20.refs_1_.v, s16[256,2176]{1,0:T(8,128)(2,1)S(1)} %collective-permute-done.21.refs_2_.v, ...), custom_call_target="tpu_custom_call" | custom-call | flops 2147483648 | bytes 4194304 | tf_op jit(solution)/shard_map/pallas_call | solution.py:50
  124.1 3.5 %collective-permute-done.25.refs_3_ = s16[128,2176]{1,0:T(8,128)(2,1)S(1)} collective-permute-done((s16[128,2176]{1,0:T(8,128)(2,1)S(1)}, s16[128,2176]{1,0:T(8,128)(2,1)S(1)}, u32[]{:S(2)}, u32[]{:S(2)}) %collective-permute-start.25) | collective-permute-done | bytes 557088 | tf_op jit(solution)/shard_map/ppermute | solution.py:243
  127.6 1.9 %collective-permute-done.26.refs_4_ = s16[128,2176]{1,0:T(8,128)(2,1)S(1)} collective-permute-done((s16[128,2176]{1,0:T(8,128)(2,1)S(1)}, s16[128,2176]{1,0:T(8,128)(2,1)S(1)}, u32[]{:S(2)}, u32[]{:S(2)}) %collective-permute-start.26) | collective-permute-done | bytes 557088 | tf_op jit(solution)/shard_map/ppermute | solution.py:243
  129.5 4.2 %shard_map.56 = (f32[256,1024]{1,0:T(8,128)S(1)}, f32[256,1024]{1,0:T(8,128)S(1)}) custom-call(s32[32]{0:T(128)S(1)} %dynamic-slice_bitcast_fusion.s, s16[256,2176]{1,0:T(8,128)(2,1)S(1)} %shard_map.51.refs_0_, s16[256,2176]{1,0:T(8,128)(2,1)S(1)} %collective-permute-done.20.refs_1_.v, s16[256,2176]{1,0:T(8,128)(2,1)S(1)} %collective-permute-done.21.refs_2_.v, ...), custom_call_target="tpu_custom_call" | custom-call | flops 2147483648 | bytes 4194304 | tf_op jit(solution)/shard_map/pallas_call | solution.py:50
  134.8 8.7 %collective-permute-start.24 = (s16[128,1152]{1,0:T(8,128)(2,1)S(1)}, s16[128,1152]{1,0:T(8,128)(2,1)S(1)}, u32[]{:S(2)}, u32[]{:S(2)}) collective-permute-start(s16[128,1152]{1,0:T(8,128)(2,1)S(1)} %get-tuple-element.36), channel_id=1, source_target_pairs={{0,2},{1,3},{2,4},{3,5},{4,6},{5,7},{6,0},{7,1},{8,10},{9,11},{10,... | collective-permute-start | bytes 884744 | tf_op jit(solution)/shard_map/ppermute | solution.py:243
  143.8 1.9 %collective-permute-start.28 = (s16[128,1152]{1,0:T(8,128)(2,1)S(1)}, s16[128,1152]{1,0:T(8,128)(2,1)S(1)}, u32[]{:S(2)}, u32[]{:S(2)}) collective-permute-start(s16[128,1152]{1,0:T(8,128)(2,1)S(1)} %get-tuple-element.39), channel_id=1, source_target_pairs={{0,6},{1,7},{2,0},{3,1},{4,2},{5,3},{6,4},{7,5},{8,12},{9,13},{10,... | collective-permute-start | bytes 884744 | tf_op jit(solution)/shard_map/ppermute | solution.py:243
  145.7 5.5 %collective-permute-start.29 = (s16[128,1152]{1,0:T(8,128)(2,1)S(1)}, s16[128,1152]{1,0:T(8,128)(2,1)S(1)}, u32[]{:S(2)}, u32[]{:S(2)}) collective-permute-start(s16[128,1152]{1,0:T(8,128)(2,1)S(1)} %get-tuple-element.40), channel_id=1, source_target_pairs={{0,4},{1,5},{2,6},{3,7},{4,0},{5,1},{6,2},{7,3},{8,14},{9,15},{10,... | collective-permute-start | bytes 884744 | tf_op jit(solution)/shard_map/ppermute | solution.py:243
  151.3 5.1 %collective-permute-done.28.c = s16[128,1152]{1,0:T(8,128)(2,1)S(1)} collective-permute-done((s16[128,1152]{1,0:T(8,128)(2,1)S(1)}, s16[128,1152]{1,0:T(8,128)(2,1)S(1)}, u32[]{:S(2)}, u32[]{:S(2)}) %collective-permute-start.28) | collective-permute-done | bytes 294944 | tf_op jit(solution)/shard_map/ppermute | solution.py:243
  156.4 6.4 %collective-permute-done.29.d = s16[128,1152]{1,0:T(8,128)(2,1)S(1)} collective-permute-done((s16[128,1152]{1,0:T(8,128)(2,1)S(1)}, s16[128,1152]{1,0:T(8,128)(2,1)S(1)}, u32[]{:S(2)}, u32[]{:S(2)}) %collective-permute-start.29) | collective-permute-done | bytes 294944 | tf_op jit(solution)/shard_map/ppermute | solution.py:243
  162.7 1.1 shard_map.58
  (40 shorter events, 9.0 us)
Async XLA Ops:
  0.0 1.8 %copy-start.1 = (s32[8,16]{1,0:T(8,128)S(1)}, s32[8,16]{1,0:T(8,128)}, u32[]{:S(2)}) copy-start(s32[8,16]{1,0:T(8,128)} %m.3) | copy-start | bytes 1540
  2.9 2.0 %collective-permute-start.5 = (bf16[512,512]{1,0:T(8,128)(2,1)S(1)}, bf16[512,512]{1,0:T(8,128)(2,1)S(1)}, u32[]{:S(2)}, u32[]{:S(2)}) collective-permute-start(bf16[512,512]{1,0:T(8,128)(2,1)S(1)} %get-tuple-element.26), channel_id=1, source_target_pairs={{0,1},{1,0},{2,3},{3,2},{4,5},{5,4},{6,7},{7,6},{8,9},{9,8},{10,11... | collective-permute-start | bytes 1572872 | tf_op jit(solution)/shard_map/ppermute | solution.py:273
  3.0 6.4 %collective-permute-start = (bf16[512,512]{1,0:T(8,128)(2,1)S(1)}, bf16[512,512]{1,0:T(8,128)(2,1)S(1)}, u32[]{:S(2)}, u32[]{:S(2)}) collective-permute-start(bf16[512,512]{1,0:T(8,128)(2,1)S(1)} %get-tuple-element.24), channel_id=1, source_target_pairs={{0,1},{1,0},{2,3},{3,2},{4,5},{5,4},{6,7},{7,6},{8,9},{9,8},{10,11... | collective-permute-start | bytes 1572872 | tf_op jit(solution)/shard_map/ppermute | solution.py:273
  5.5 11.6 %collective-permute-start.6 = (bf16[512,512]{1,0:T(8,128)(2,1)S(1)}, bf16[512,512]{1,0:T(8,128)(2,1)S(1)}, u32[]{:S(2)}, u32[]{:S(2)}) collective-permute-start(bf16[512,512]{1,0:T(8,128)(2,1)S(1)} %shard_map.40.refs_0_), channel_id=1, source_target_pairs={{0,2},{1,7},{8,10},{9,15},{16,18},{17,23},{24,26},{25,31},{32,34},... | collective-permute-start | bytes 1572872 | tf_op jit(solution)/shard_map/ppermute | solution.py:275
  9.9 18.3 %collective-permute-start.1 = (bf16[512,512]{1,0:T(8,128)(2,1)S(1)}, bf16[512,512]{1,0:T(8,128)(2,1)S(1)}, u32[]{:S(2)}, u32[]{:S(2)}) collective-permute-start(bf16[512,512]{1,0:T(8,128)(2,1)S(1)} %shard_map.38.refs_0_), channel_id=1, source_target_pairs={{0,2},{1,7},{8,10},{9,15},{16,18},{17,23},{24,26},{25,31},{32,34},... | collective-permute-start | bytes 1572872 | tf_op jit(solution)/shard_map/ppermute | solution.py:275
  11.3 17.7 %collective-permute-start.7 = (bf16[512,512]{1,0:T(8,128)(2,1)S(1)}, bf16[512,512]{1,0:T(8,128)(2,1)S(1)}, u32[]{:S(2)}, u32[]{:S(2)}) collective-permute-start(bf16[512,512]{1,0:T(8,128)(2,1)S(1)} %shard_map.40.refs_0_), channel_id=1, source_target_pairs={{0,6},{1,3},{8,14},{9,11},{16,22},{17,19},{24,30},{25,27},{32,38},... | collective-permute-start | bytes 1572872 | tf_op jit(solution)/shard_map/ppermute | solution.py:276
  17.0 11.9 %collective-permute-start.8 = (bf16[512,512]{1,0:T(8,128)(2,1)S(1)}, bf16[512,512]{1,0:T(8,128)(2,1)S(1)}, u32[]{:S(2)}, u32[]{:S(2)}) collective-permute-start(bf16[512,512]{1,0:T(8,128)(2,1)S(1)} %collective-permute-done.6.refs_1_), channel_id=1, source_target_pairs={{2,4},{7,5},{10,12},{15,13},{18,20},{23,21},{26,28},{31,29},{34,36... | collective-permute-start | bytes 1572872 | tf_op jit(solution)/shard_map/ppermute | solution.py:277
  17.7 16.4 %collective-permute-start.2 = (bf16[512,512]{1,0:T(8,128)(2,1)S(1)}, bf16[512,512]{1,0:T(8,128)(2,1)S(1)}, u32[]{:S(2)}, u32[]{:S(2)}) collective-permute-start(bf16[512,512]{1,0:T(8,128)(2,1)S(1)} %shard_map.38.refs_0_), channel_id=1, source_target_pairs={{0,6},{1,3},{8,14},{9,11},{16,22},{17,19},{24,30},{25,27},{32,38},... | collective-permute-start | bytes 1572872 | tf_op jit(solution)/shard_map/ppermute | solution.py:276
  28.3 5.8 %collective-permute-start.3 = (bf16[512,512]{1,0:T(8,128)(2,1)S(1)}, bf16[512,512]{1,0:T(8,128)(2,1)S(1)}, u32[]{:S(2)}, u32[]{:S(2)}) collective-permute-start(bf16[512,512]{1,0:T(8,128)(2,1)S(1)} %collective-permute-done.1.refs_1_), channel_id=1, source_target_pairs={{2,4},{7,5},{10,12},{15,13},{18,20},{23,21},{26,28},{31,29},{34,36... | collective-permute-start | bytes 1572872 | tf_op jit(solution)/shard_map/ppermute | solution.py:277
  29.0 5.8 %copy-start = (bf16[1024,2048]{1,0:T(8,128)(2,1)S(1)}, bf16[1024,2048]{1,0:T(8,128)(2,1)}, u32[]{:S(2)}) copy-start(bf16[1024,2048]{1,0:T(8,128)(2,1)} %density.1) | copy-start | bytes 12582916
  29.6 7.0 %collective-permute-start.9 = (bf16[512,512]{1,0:T(8,128)(2,1)S(1)}, bf16[512,512]{1,0:T(8,128)(2,1)S(1)}, u32[]{:S(2)}, u32[]{:S(2)}) collective-permute-start(bf16[512,512]{1,0:T(8,128)(2,1)S(1)} %shard_map.41.own_b), channel_id=1, source_target_pairs={{0,1},{1,0},{2,3},{3,2},{4,5},{5,4},{6,7},{7,6},{8,9},{9,8},{10,11... | collective-permute-start | bytes 1572872 | tf_op jit(solution)/shard_map/ppermute | solution.py:255
  34.7 2.0 %collective-permute-start.4 = (bf16[512,512]{1,0:T(8,128)(2,1)S(1)}, bf16[512,512]{1,0:T(8,128)(2,1)S(1)}, u32[]{:S(2)}, u32[]{:S(2)}) collective-permute-start(bf16[512,512]{1,0:T(8,128)(2,1)S(1)} %shard_map.39.own_a), channel_id=1, source_target_pairs={{0,1},{1,0},{2,3},{3,2},{4,5},{5,4},{6,7},{7,6},{8,9},{9,8},{10,11... | collective-permute-start | bytes 1572872 | tf_op jit(solution)/shard_map/ppermute | solution.py:255
  39.0 9.6 %collective-permute-start.12 = (s16[128,2176]{1,0:T(8,128)(2,1)S(1)}, s16[128,2176]{1,0:T(8,128)(2,1)S(1)}, u32[]{:S(2)}, u32[]{:S(2)}) collective-permute-start(s16[128,2176]{1,0:T(8,128)(2,1)S(1)} %get-tuple-element.28), channel_id=1, source_target_pairs={{0,32},{1,9},{2,34},{3,11},{4,36},{5,13},{6,38},{7,15},{8,40},{9,1... | collective-permute-start | bytes 1671176 | tf_op jit(solution)/shard_map/ppermute | solution.py:243
  40.6 12.0 %collective-permute-start.10 = (s16[128,2176]{1,0:T(8,128)(2,1)S(1)}, s16[128,2176]{1,0:T(8,128)(2,1)S(1)}, u32[]{:S(2)}, u32[]{:S(2)}) collective-permute-start(s16[128,2176]{1,0:T(8,128)(2,1)S(1)} %get-tuple-element.27), channel_id=1, source_target_pairs={{0,96},{1,25},{2,98},{3,27},{4,100},{5,29},{6,102},{7,31},{8,104},... | collective-permute-start | bytes 1671176 | tf_op jit(solution)/shard_map/ppermute | solution.py:243
  49.7 16.8 %collective-permute-start.13 = (s16[256,2176]{1,0:T(8,128)(2,1)S(1)}, s16[256,2176]{1,0:T(8,128)(2,1)S(1)}, u32[]{:S(2)}, u32[]{:S(2)}) collective-permute-start(s16[256,2176]{1,0:T(8,128)(2,1)S(1)} %shard_map.48), channel_id=1, source_target_pairs={{0,96},{1,25},{2,98},{3,27},{4,100},{5,29},{6,102},{7,31},{8,104},... | collective-permute-start | bytes 3342344 | tf_op jit(solution)/shard_map/ppermute | solution.py:243
  53.7 15.6 %collective-permute-start.11 = (s16[256,2176]{1,0:T(8,128)(2,1)S(1)}, s16[256,2176]{1,0:T(8,128)(2,1)S(1)}, u32[]{:S(2)}, u32[]{:S(2)}) collective-permute-start(s16[256,2176]{1,0:T(8,128)(2,1)S(1)} %shard_map.46), channel_id=1, source_target_pairs={{0,32},{1,9},{2,34},{3,11},{4,36},{5,13},{6,38},{7,15},{8,40},{9,1... | collective-permute-start | bytes 3342344 | tf_op jit(solution)/shard_map/ppermute | solution.py:243
  70.6 6.6 %collective-permute-start.14 = (s16[64,2176]{1,0:T(8,128)(2,1)S(1)}, s16[64,2176]{1,0:T(8,128)(2,1)S(1)}, u32[]{:S(2)}, u32[]{:S(2)}) collective-permute-start(s16[64,2176]{1,0:T(8,128)(2,1)S(1)} %get-tuple-element.30), channel_id=1, source_target_pairs={{0,8},{1,33},{2,10},{3,35},{4,12},{5,37},{6,14},{7,39},{8,0},{9,41... | collective-permute-start | bytes 835592 | tf_op jit(solution)/shard_map/ppermute | solution.py:243
  71.5 8.5 %collective-permute-start.15 = (s16[64,2176]{1,0:T(8,128)(2,1)S(1)}, s16[64,2176]{1,0:T(8,128)(2,1)S(1)}, u32[]{:S(2)}, u32[]{:S(2)}) collective-permute-start(s16[64,2176]{1,0:T(8,128)(2,1)S(1)} %get-tuple-element.31), channel_id=1, source_target_pairs={{0,16},{1,65},{2,18},{3,67},{4,20},{5,69},{6,22},{7,71},{8,24},{9,... | collective-permute-start | bytes 835592 | tf_op jit(solution)/shard_map/ppermute | solution.py:243
  72.4 10.5 %collective-permute-start.16 = (s16[64,2176]{1,0:T(8,128)(2,1)S(1)}, s16[64,2176]{1,0:T(8,128)(2,1)S(1)}, u32[]{:S(2)}, u32[]{:S(2)}) collective-permute-start(s16[64,2176]{1,0:T(8,128)(2,1)S(1)} %get-tuple-element.32), channel_id=1, source_target_pairs={{0,24},{1,97},{2,26},{3,99},{4,28},{5,101},{6,30},{7,103},{8,16},{... | collective-permute-start | bytes 835592 | tf_op jit(solution)/shard_map/ppermute | solution.py:243
  83.2 6.6 %collective-permute-start.17 = (s16[64,2176]{1,0:T(8,128)(2,1)S(1)}, s16[64,2176]{1,0:T(8,128)(2,1)S(1)}, u32[]{:S(2)}, u32[]{:S(2)}) collective-permute-start(s16[64,2176]{1,0:T(8,128)(2,1)S(1)} %shard_map.50.refs_0_), channel_id=1, source_target_pairs={{0,8},{1,33},{2,10},{3,35},{4,12},{5,37},{6,14},{7,39},{8,0},{9,41... | collective-permute-start | bytes 835592 | tf_op jit(solution)/shard_map/ppermute | solution.py:243
  83.4 12.1 %collective-permute-start.18 = (s16[64,2176]{1,0:T(8,128)(2,1)S(1)}, s16[64,2176]{1,0:T(8,128)(2,1)S(1)}, u32[]{:S(2)}, u32[]{:S(2)}) collective-permute-start(s16[64,2176]{1,0:T(8,128)(2,1)S(1)} %shard_map.50.refs_0_), channel_id=1, source_target_pairs={{0,16},{1,65},{2,18},{3,67},{4,20},{5,69},{6,22},{7,71},{8,24},{9,... | collective-permute-start | bytes 835592 | tf_op jit(solution)/shard_map/ppermute | solution.py:243
  87.8 12.7 %collective-permute-start.19 = (s16[64,2176]{1,0:T(8,128)(2,1)S(1)}, s16[64,2176]{1,0:T(8,128)(2,1)S(1)}, u32[]{:S(2)}, u32[]{:S(2)}) collective-permute-start(s16[64,2176]{1,0:T(8,128)(2,1)S(1)} %shard_map.50.refs_0_), channel_id=1, source_target_pairs={{0,24},{1,97},{2,26},{3,99},{4,28},{5,101},{6,30},{7,103},{8,16},{... | collective-permute-start | bytes 835592 | tf_op jit(solution)/shard_map/ppermute | solution.py:243
  100.6 16.8 %collective-permute-start.21 = (s16[256,2176]{1,0:T(8,128)(2,1)S(1)}, s16[256,2176]{1,0:T(8,128)(2,1)S(1)}, u32[]{:S(2)}, u32[]{:S(2)}) collective-permute-start(s16[256,2176]{1,0:T(8,128)(2,1)S(1)} %shard_map.51.refs_0_), channel_id=1, source_target_pairs={{0,96},{1,25},{2,98},{3,27},{4,100},{5,29},{6,102},{7,31},{8,104},... | collective-permute-start | bytes 3342344 | tf_op jit(solution)/shard_map/ppermute | solution.py:243
  100.7 17.4 %collective-permute-start.20 = (s16[256,2176]{1,0:T(8,128)(2,1)S(1)}, s16[256,2176]{1,0:T(8,128)(2,1)S(1)}, u32[]{:S(2)}, u32[]{:S(2)}) collective-permute-start(s16[256,2176]{1,0:T(8,128)(2,1)S(1)} %shard_map.51.refs_0_), channel_id=1, source_target_pairs={{0,32},{1,9},{2,34},{3,11},{4,36},{5,13},{6,38},{7,15},{8,40},{9,1... | collective-permute-start | bytes 3342344 | tf_op jit(solution)/shard_map/ppermute | solution.py:243
  118.0 9.6 %collective-permute-start.25 = (s16[128,2176]{1,0:T(8,128)(2,1)S(1)}, s16[128,2176]{1,0:T(8,128)(2,1)S(1)}, u32[]{:S(2)}, u32[]{:S(2)}) collective-permute-start(s16[128,2176]{1,0:T(8,128)(2,1)S(1)} %shard_map.54), channel_id=1, source_target_pairs={{0,32},{1,9},{2,34},{3,11},{4,36},{5,13},{6,38},{7,15},{8,40},{9,1... | collective-permute-start | bytes 1671176 | tf_op jit(solution)/shard_map/ppermute | solution.py:243
  118.7 10.8 %collective-permute-start.26 = (s16[128,2176]{1,0:T(8,128)(2,1)S(1)}, s16[128,2176]{1,0:T(8,128)(2,1)S(1)}, u32[]{:S(2)}, u32[]{:S(2)}) collective-permute-start(s16[128,2176]{1,0:T(8,128)(2,1)S(1)} %shard_map.55), channel_id=1, source_target_pairs={{0,96},{1,25},{2,98},{3,27},{4,100},{5,29},{6,102},{7,31},{8,104},... | collective-permute-start | bytes 1671176 | tf_op jit(solution)/shard_map/ppermute | solution.py:243
  124.0 9.8 %collective-permute-start.22 = (f32[256,1024]{1,0:T(8,128)S(1)}, f32[256,1024]{1,0:T(8,128)S(1)}, u32[]{:S(2)}, u32[]{:S(2)}) collective-permute-start(f32[256,1024]{1,0:T(8,128)S(1)} %get-tuple-element.34), channel_id=1, source_target_pairs={{0,1},{1,0},{2,3},{3,2},{4,5},{5,4},{6,7},{7,6},{8,9},{9,8},{10,11... | collective-permute-start | bytes 3145736 | tf_op jit(solution)/shard_map/ppermute | solution.py:255
  133.7 9.8 %collective-permute-start.27 = (f32[256,1024]{1,0:T(8,128)S(1)}, f32[256,1024]{1,0:T(8,128)S(1)}, u32[]{:S(2)}, u32[]{:S(2)}) collective-permute-start(f32[256,1024]{1,0:T(8,128)S(1)} %get-tuple-element.38), channel_id=1, source_target_pairs={{0,1},{1,0},{2,3},{3,2},{4,5},{5,4},{6,7},{7,6},{8,9},{9,8},{10,11... | collective-permute-start | bytes 3145736 | tf_op jit(solution)/shard_map/ppermute | solution.py:255
  134.1 17.2 %collective-permute-start.23 = (s16[128,1152]{1,0:T(8,128)(2,1)S(1)}, s16[128,1152]{1,0:T(8,128)(2,1)S(1)}, u32[]{:S(2)}, u32[]{:S(2)}) collective-permute-start(s16[128,1152]{1,0:T(8,128)(2,1)S(1)} %get-tuple-element.35), channel_id=1, source_target_pairs={{0,0},{1,1},{2,2},{3,3},{4,4},{5,5},{6,6},{7,7},{8,8},{9,9},{10,10... | collective-permute-start | bytes 884744 | tf_op jit(solution)/shard_map/ppermute | solution.py:243
  134.8 16.5 %collective-permute-start.24 = (s16[128,1152]{1,0:T(8,128)(2,1)S(1)}, s16[128,1152]{1,0:T(8,128)(2,1)S(1)}, u32[]{:S(2)}, u32[]{:S(2)}) collective-permute-start(s16[128,1152]{1,0:T(8,128)(2,1)S(1)} %get-tuple-element.36), channel_id=1, source_target_pairs={{0,2},{1,3},{2,4},{3,5},{4,6},{5,7},{6,0},{7,1},{8,10},{9,11},{10,... | collective-permute-start | bytes 884744 | tf_op jit(solution)/shard_map/ppermute | solution.py:243
  143.8 12.6 %collective-permute-start.28 = (s16[128,1152]{1,0:T(8,128)(2,1)S(1)}, s16[128,1152]{1,0:T(8,128)(2,1)S(1)}, u32[]{:S(2)}, u32[]{:S(2)}) collective-permute-start(s16[128,1152]{1,0:T(8,128)(2,1)S(1)} %get-tuple-element.39), channel_id=1, source_target_pairs={{0,6},{1,7},{2,0},{3,1},{4,2},{5,3},{6,4},{7,5},{8,12},{9,13},{10,... | collective-permute-start | bytes 884744 | tf_op jit(solution)/shard_map/ppermute | solution.py:243
  145.7 17.0 %collective-permute-start.29 = (s16[128,1152]{1,0:T(8,128)(2,1)S(1)}, s16[128,1152]{1,0:T(8,128)(2,1)S(1)}, u32[]{:S(2)}, u32[]{:S(2)}) collective-permute-start(s16[128,1152]{1,0:T(8,128)(2,1)S(1)} %get-tuple-element.40), channel_id=1, source_target_pairs={{0,4},{1,5},{2,6},{3,7},{4,0},{5,1},{6,2},{7,3},{8,14},{9,15},{10,... | collective-permute-start | bytes 884744 | tf_op jit(solution)/shard_map/ppermute | solution.py:243

commit v4 on v3

--- a/solution.py
+++ b/solution.py
@@ -35,10 +35,11 @@
     subs = [second, second ^ 1, second ^ 2, second ^ 3]
     source = 0 if z == 0 else 1 if z == 1 + 2 * core else 3 if z == 2 else 2
     own_square = int(z * 2 + core == (x * 4 + y) // 2)
-    return [*quarters, *chosen, *subs, core, own_square, y % 2, source, odd] + [0] * 15
-
-
-QUARTERS, CHOSEN, SUBS, CORE, OWNER, HALF, SOURCE, ODD = 0, 4, 8, 12, 13, 14, 15, 16
+    where = [turns(x, y).index(((z ^ flip) - z) % 4) for flip in range(4)]
+    return [*quarters, *chosen, *subs, *where, core, own_square, y % 2, source, odd] + [0] * 11
+
+
+QUARTERS, CHOSEN, SUBS, WHERE, CORE, OWNER, HALF, SOURCE, ODD = 0, 4, 8, 12, 16, 17, 18, 19, 20
 
 
 def shape(rows, columns, dtype):
@@ -140,14 +141,26 @@
     )
 
 
+def by_half(i, s, body):
+    for odd in range(2):
+        start = 128 * (odd ^ i)
+        halves = slice(start, start + 128), slice(128 - start, 256 - start)
+        pl.when(s[ODD] == odd)(functools.partial(body, *halves))
+
+
 def push_kernel(i, s, mine, came, out):
-    add, rest = at(s[ODD] ^ i, 128), at(s[ODD] ^ i ^ 1, 128)
-    put(out.at[add], mine[add, :] + take(came))
-    put(out.at[rest], mine[rest, :])
+    def body(add, rest):
+        put(out.at[add], mine[add, :] + take(came))
+        put(out.at[rest], mine[rest, :])
+
+    by_half(i, s, body)
 
 
 def cut_kernel(i, s, v, out):
-    out[...] = v[at(s[ODD] ^ i, 128), :]
+    def body(half, _):
+        out[...] = v[half, :]
+
+    by_half(i, s, body)
 
 
 def spread_kernel(s, own, a, b, *outs):
@@ -225,14 +238,22 @@
     )
 
 
-def deal_kernel(mine, came, *outs):
-    for i, out in enumerate(outs):
-        rows = slice(i * 128, (i + 1) * 128)
-        put(out, mine[rows, :] + came[rows, :])
-
-
-def finish_kernel(a, b, c, d, out):
-    out[...] = take(a) + take(b) + take(c) + take(d)
+def deal_kernel(s, mine_a, came_a, mine_b, came_b, *outs):
+    for q, out in enumerate(outs):
+        for i, (mine, came) in enumerate(((mine_a, came_a), (mine_b, came_b))):
+
+            @pl.when(s[WHERE + q] // 2 == i)
+            def _(q=q, out=out, mine=mine, came=came):
+                rows = at(s[WHERE + q] % 2, 128)
+                v = mine[rows, :] + came[rows, :]
+                if q == 0:
+                    out[...] = v
+                else:
+                    put(out, v)
+
+
+def finish_kernel(own, a, b, c, out):
+    out[...] = own[...] + take(a) + take(b) + take(c)
 
 
 def place(x, y, z, core):
@@ -315,16 +336,17 @@
     cut = [call(functools.partial(cut_kernel, i), half, [s], v) for i, v in enumerate((next_, near))]
     far = [along(cut[0], 1)]
     far += [along(cut[1], 3)]
-    came = []
+    sums = []
     for i in (0, 2):
         quarters = [own, near, next_] + far * (i == 2)
         mine, theirs = second_product(i, s, quarters, masked)
-        theirs = swap(theirs)
-        outs = [shape(128, SLAB + LANES, I16)] * 2
-        parts = call(deal_kernel, outs, [], mine, theirs)
-        for j, v in enumerate(parts):
-            came.append(send(v, lambda x, y, z, core: (x, y, z + turns(x, y)[i + j], core)))
-    return call(finish_kernel, shape(128, SLAB, F32), [], *came)
+        sums += [mine, swap(theirs)]
+    coded = shape(128, SLAB + LANES, I16)
+    own, *parts = call(deal_kernel, [shape(128, SLAB, F32)] + [coded] * 3, [s], *sums)
+    came = []
+    for flip in (1, 2, 3):
+        came.append(send(parts[flip - 1], lambda x, y, z, core: (x, y, z ^ flip, core)))
+    return call(finish_kernel, shape(128, SLAB, F32), [], own, *came)
 
 
 def solution(mesh):

time: 164 us -> 166 us (1.012)
  the two profiles are of different devices: /device:TPU:24 before, /device:TPU:0 now
where the time goes in v4:
time: 166 us; the launch traced here: 165 us
  waiting for transfers between devices  88.7 us (53%)
  starting transfers between devices  43.7 us (26%)
  Pallas kernels  29.7 us (18%)
  local copies, waits for them, and re-layouts  2.48 us (1%)
    ppermute x17, waiting for transfers between devices, send(): return lax.ppermute(v, AXES, [(place(*d), place(*to(*d))) for d in DEVICES])  71.2 us
    pallas_call x21, Pallas kernels, call(): pl.pallas_call(kernel, out_shape=out, in_specs=[pl.BlockSpec(memory_space...  29.7 us
    ppermute x17, starting transfers between devices, send(): return lax.ppermute(v, AXES, [(place(*d), place(*to(*d))) for d in DEVICES])  29.5 us
    ppermute x2, waiting for transfers between devices, spread_column(): one = lax.ppermute(half, axes, [(0, 2), (1, 7)])  12.8 us
    ppermute x2, starting transfers between devices, spread_column(): one = lax.ppermute(half, axes, [(0, 2), (1, 7)])  5.29 us
    ppermute x2, starting transfers between devices, spread_column(): two = lax.ppermute(half, axes, [(0, 6), (1, 3)])  3.51 us
    ppermute x4, starting transfers between devices, swap(): return lax.ppermute(v, 'core', [(0, 1), (1, 0)])  3.44 us
  transfers between devices with their start and end apart: 29, of which 21 were waited for; matrix products, arithmetic and copies ran while one was open for 0% of the time, Pallas kernels for 13%

profile of v4, /device:TPU:0, one launch (start us, length us, event | category | flops | bytes accessed | tf_op | source)
XLA Modules:
  0.0 164.9 jit_solution(2696021295792785220)
XLA Ops:
  0.0 1.8 %slice.3.density = bf16[1024,1024]{1,0:T(8,128)(2,1)S(1)} slice(bf16[1024,2048]{1,0:T(8,128)(2,1)} %density.1), slice={[0:1024], [0:1024]} | slice | bytes 4194304 | tf_op jit(solution)/shard_map/slice | solution.py:307
  1.8 1.1 shard_map.37
  5.5 4.0 %collective-permute-start.6 = (bf16[512,512]{1,0:T(8,128)(2,1)S(1)}, bf16[512,512]{1,0:T(8,128)(2,1)S(1)}, u32[]{:S(2)}, u32[]{:S(2)}) collective-permute-start(bf16[512,512]{1,0:T(8,128)(2,1)S(1)} %shard_map.40.refs_0_), channel_id=1, source_target_pairs={{0,2},{1,7},{8,10},{9,15},{16,18},{17,23},{24,26},{25,31},{32,34},... | collective-permute-start | bytes 1572872 | tf_op jit(solution)/shard_map/ppermute | solution.py:296
  10.1 1.3 collective-permute-start.1
  11.4 2.2 %collective-permute-start.7 = (bf16[512,512]{1,0:T(8,128)(2,1)S(1)}, bf16[512,512]{1,0:T(8,128)(2,1)S(1)}, u32[]{:S(2)}, u32[]{:S(2)}) collective-permute-start(bf16[512,512]{1,0:T(8,128)(2,1)S(1)} %shard_map.40.refs_0_), channel_id=1, source_target_pairs={{0,6},{1,3},{8,14},{9,11},{16,22},{17,19},{24,30},{25,27},{32,38},... | collective-permute-start | bytes 1572872 | tf_op jit(solution)/shard_map/ppermute | solution.py:297
  13.6 3.6 %collective-permute-done.6.refs_1_ = bf16[512,512]{1,0:T(8,128)(2,1)S(1)} collective-permute-done((bf16[512,512]{1,0:T(8,128)(2,1)S(1)}, bf16[512,512]{1,0:T(8,128)(2,1)S(1)}, u32[]{:S(2)}, u32[]{:S(2)}) %collective-permute-start.6) | collective-permute-done | bytes 524320 | tf_op jit(solution)/shard_map/ppermute | solution.py:296
  17.8 1.3 collective-permute-start.2
  19.2 9.2 %collective-permute-done.1.refs_1_ = bf16[512,512]{1,0:T(8,128)(2,1)S(1)} collective-permute-done((bf16[512,512]{1,0:T(8,128)(2,1)S(1)}, bf16[512,512]{1,0:T(8,128)(2,1)S(1)}, u32[]{:S(2)}, u32[]{:S(2)}) %collective-permute-start.1) | collective-permute-done | bytes 524320 | tf_op jit(solution)/shard_map/ppermute | solution.py:296
  29.7 3.2 %collective-permute-start.9 = (bf16[512,512]{1,0:T(8,128)(2,1)S(1)}, bf16[512,512]{1,0:T(8,128)(2,1)S(1)}, u32[]{:S(2)}, u32[]{:S(2)}) collective-permute-start(bf16[512,512]{1,0:T(8,128)(2,1)S(1)} %shard_map.41.own_b), channel_id=1, source_target_pairs={{0,1},{1,0},{2,3},{3,2},{4,5},{5,4},{6,7},{7,6},{8,9},{9,8},{10,11... | collective-permute-start | bytes 1572872 | tf_op jit(solution)/shard_map/ppermute | solution.py:276
  32.9 1.3 collective-permute-done.2.refs_2_
  34.9 1.8 %shard_map.42.masked.refs_3_.refs_5_ = bf16[1024,2048]{1,0:T(8,128)(2,1)S(1)} custom-call(s32[8,16]{1,0:T(8,128)S(1)} %copy-done.1, bf16[1024,2048]{1,0:T(8,128)(2,1)S(1)} %copy-done), custom_call_target="tpu_custom_call" | custom-call | flops 4194304 | bytes 4194304 | tf_op jit(solution)/shard_map/pallas_call | solution.py:51
  36.8 2.3 %shard_map.45 = (s16[128,2176]{1,0:T(8,128)(2,1)S(1)}, s16[128,2176]{1,0:T(8,128)(2,1)S(1)}) custom-call(s32[32]{0:T(128)S(1)} %dynamic-slice_bitcast_fusion.s, bf16[512,512]{1,0:T(8,128)(2,1)S(1)} %shard_map.39.own_a, bf16[512,512]{1,0:T(8,128)(2,1)S(1)} %collective-permute-done.4.other_a, bf16[512,512]{1,0:T(8,128)(2,1)S(1)} %shard_map.41.own_b, ...), custom_call_target="tpu_custom_call" | custom-call | flops 1073741824 | bytes 4194304 | tf_op jit(solution)/shard_map/pallas_call | solution.py:51
  39.1 1.6 collective-permute-start.12
  40.7 2.1 %collective-permute-start.10 = (s16[128,2176]{1,0:T(8,128)(2,1)S(1)}, s16[128,2176]{1,0:T(8,128)(2,1)S(1)}, u32[]{:S(2)}, u32[]{:S(2)}) collective-permute-start(s16[128,2176]{1,0:T(8,128)(2,1)S(1)} %get-tuple-element.27), channel_id=1, source_target_pairs={{0,96},{1,25},{2,98},{3,27},{4,100},{5,29},{6,102},{7,31},{8,104},... | collective-permute-start | bytes 1671176 | tf_op jit(solution)/shard_map/ppermute | solution.py:264
  42.8 1.9 %shard_map.47.mine = f32[256,2048]{1,0:T(8,128)S(1)} custom-call(s32[32]{0:T(128)S(1)} %dynamic-slice_bitcast_fusion.s, bf16[512,512]{1,0:T(8,128)(2,1)S(1)} %shard_map.39.own_a, bf16[512,512]{1,0:T(8,128)(2,1)S(1)} %collective-permute-done.4.other_a, bf16[512,512]{1,0:T(8,128)(2,1)S(1)} %shard_map.41.own_b, ...), custom_call_target="tpu_custom_call" | custom-call | flops 1073741824 | bytes 4194304 | tf_op jit(solution)/shard_map/pallas_call | solution.py:51
  44.7 1.9 %shard_map.44.mine = f32[256,2048]{1,0:T(8,128)S(1)} custom-call(s32[32]{0:T(128)S(1)} %dynamic-slice_bitcast_fusion.s, bf16[512,512]{1,0:T(8,128)(2,1)S(1)} %shard_map.39.own_a, bf16[512,512]{1,0:T(8,128)(2,1)S(1)} %collective-permute-done.4.other_a, bf16[512,512]{1,0:T(8,128)(2,1)S(1)} %shard_map.41.own_b, ...), custom_call_target="tpu_custom_call" | custom-call | flops 1073741824 | bytes 4194304 | tf_op jit(solution)/shard_map/pallas_call | solution.py:51
  46.6 2.1 %collective-permute-done.12.came = s16[128,2176]{1,0:T(8,128)(2,1)S(1)} collective-permute-done((s16[128,2176]{1,0:T(8,128)(2,1)S(1)}, s16[128,2176]{1,0:T(8,128)(2,1)S(1)}, u32[]{:S(2)}, u32[]{:S(2)}) %collective-permute-start.12) | collective-permute-done | bytes 557088 | tf_op jit(solution)/shard_map/ppermute | solution.py:264
  48.7 1.1 shard_map.48
  49.8 2.8 %collective-permute-start.13 = (s16[256,2176]{1,0:T(8,128)(2,1)S(1)}, s16[256,2176]{1,0:T(8,128)(2,1)S(1)}, u32[]{:S(2)}, u32[]{:S(2)}) collective-permute-start(s16[256,2176]{1,0:T(8,128)(2,1)S(1)} %shard_map.48), channel_id=1, source_target_pairs={{0,96},{1,25},{2,98},{3,27},{4,100},{5,29},{6,102},{7,31},{8,104},... | collective-permute-start | bytes 3342344 | tf_op jit(solution)/shard_map/ppermute | solution.py:264
  52.7 1.1 shard_map.46
  54.1 2.1 %shard_map.43.own = f32[256,2048]{1,0:T(8,128)S(1)} custom-call(s32[32]{0:T(128)S(1)} %dynamic-slice_bitcast_fusion.s, bf16[512,512]{1,0:T(8,128)(2,1)S(1)} %shard_map.39.own_a, bf16[512,512]{1,0:T(8,128)(2,1)S(1)} %collective-permute-done.4.other_a, bf16[512,512]{1,0:T(8,128)(2,1)S(1)} %shard_map.41.own_b, ...), custom_call_target="tpu_custom_call" | custom-call | flops 1073741824 | bytes 4194304 | tf_op jit(solution)/shard_map/pallas_call | solution.py:51
  56.2 10.5 %collective-permute-done.13.b = s16[256,2176]{1,0:T(8,128)(2,1)S(1)} collective-permute-done((s16[256,2176]{1,0:T(8,128)(2,1)S(1)}, s16[256,2176]{1,0:T(8,128)(2,1)S(1)}, u32[]{:S(2)}, u32[]{:S(2)}) %collective-permute-start.13) | collective-permute-done | bytes 1114144 | tf_op jit(solution)/shard_map/ppermute | solution.py:264
  66.6 2.7 %collective-permute-done.11.a = s16[256,2176]{1,0:T(8,128)(2,1)S(1)} collective-permute-done((s16[256,2176]{1,0:T(8,128)(2,1)S(1)}, s16[256,2176]{1,0:T(8,128)(2,1)S(1)}, u32[]{:S(2)}, u32[]{:S(2)}) %collective-permute-start.11) | collective-permute-done | bytes 1114144 | tf_op jit(solution)/shard_map/ppermute | solution.py:264
  69.4 1.4 shard_map.49
  70.8 1.7 %collective-permute-start.14 = (s16[64,2176]{1,0:T(8,128)(2,1)S(1)}, s16[64,2176]{1,0:T(8,128)(2,1)S(1)}, u32[]{:S(2)}, u32[]{:S(2)}) collective-permute-start(s16[64,2176]{1,0:T(8,128)(2,1)S(1)} %get-tuple-element.30), channel_id=1, source_target_pairs={{0,8},{1,33},{2,10},{3,35},{4,12},{5,37},{6,14},{7,39},{8,0},{9,41... | collective-permute-start | bytes 835592 | tf_op jit(solution)/shard_map/ppermute | solution.py:264
  72.4 2.9 %collective-permute-start.15 = (s16[64,2176]{1,0:T(8,128)(2,1)S(1)}, s16[64,2176]{1,0:T(8,128)(2,1)S(1)}, u32[]{:S(2)}, u32[]{:S(2)}) collective-permute-start(s16[64,2176]{1,0:T(8,128)(2,1)S(1)} %get-tuple-element.31), channel_id=1, source_target_pairs={{0,16},{1,65},{2,18},{3,67},{4,20},{5,69},{6,22},{7,71},{8,24},{9,... | collective-permute-start | bytes 835592 | tf_op jit(solution)/shard_map/ppermute | solution.py:264
  75.5 1.8 %collective-permute-done.14.a = s16[64,2176]{1,0:T(8,128)(2,1)S(1)} collective-permute-done((s16[64,2176]{1,0:T(8,128)(2,1)S(1)}, s16[64,2176]{1,0:T(8,128)(2,1)S(1)}, u32[]{:S(2)}, u32[]{:S(2)}) %collective-permute-start.14) | collective-permute-done | bytes 278560 | tf_op jit(solution)/shard_map/ppermute | solution.py:264
  77.4 5.5 %collective-permute-done.15.b = s16[64,2176]{1,0:T(8,128)(2,1)S(1)} collective-permute-done((s16[64,2176]{1,0:T(8,128)(2,1)S(1)}, s16[64,2176]{1,0:T(8,128)(2,1)S(1)}, u32[]{:S(2)}, u32[]{:S(2)}) %collective-permute-start.15) | collective-permute-done | bytes 278560 | tf_op jit(solution)/shard_map/ppermute | solution.py:264
  82.9 2.9 %collective-permute-done.16.c = s16[64,2176]{1,0:T(8,128)(2,1)S(1)} collective-permute-done((s16[64,2176]{1,0:T(8,128)(2,1)S(1)}, s16[64,2176]{1,0:T(8,128)(2,1)S(1)}, u32[]{:S(2)}, u32[]{:S(2)}) %collective-permute-start.16) | collective-permute-done | bytes 278560 | tf_op jit(solution)/shard_map/ppermute | solution.py:264
  86.3 1.7 %collective-permute-start.18 = (s16[64,2176]{1,0:T(8,128)(2,1)S(1)}, s16[64,2176]{1,0:T(8,128)(2,1)S(1)}, u32[]{:S(2)}, u32[]{:S(2)}) collective-permute-start(s16[64,2176]{1,0:T(8,128)(2,1)S(1)} %shard_map.50.refs_0_), channel_id=1, source_target_pairs={{0,16},{1,65},{2,18},{3,67},{4,20},{5,69},{6,22},{7,71},{8,24},{9,... | collective-permute-start | bytes 835592 | tf_op jit(solution)/shard_map/ppermute | solution.py:264
  87.9 3.0 %collective-permute-start.19 = (s16[64,2176]{1,0:T(8,128)(2,1)S(1)}, s16[64,2176]{1,0:T(8,128)(2,1)S(1)}, u32[]{:S(2)}, u32[]{:S(2)}) collective-permute-start(s16[64,2176]{1,0:T(8,128)(2,1)S(1)} %shard_map.50.refs_0_), channel_id=1, source_target_pairs={{0,24},{1,97},{2,26},{3,99},{4,28},{5,101},{6,30},{7,103},{8,16},{... | collective-permute-start | bytes 835592 | tf_op jit(solution)/shard_map/ppermute | solution.py:264
  91.0 1.8 %collective-permute-done.17.refs_1_ = s16[64,2176]{1,0:T(8,128)(2,1)S(1)} collective-permute-done((s16[64,2176]{1,0:T(8,128)(2,1)S(1)}, s16[64,2176]{1,0:T(8,128)(2,1)S(1)}, u32[]{:S(2)}, u32[]{:S(2)}) %collective-permute-start.17) | collective-permute-done | bytes 278560 | tf_op jit(solution)/shard_map/ppermute | solution.py:264
  92.8 2.7 %collective-permute-done.18.refs_2_ = s16[64,2176]{1,0:T(8,128)(2,1)S(1)} collective-permute-done((s16[64,2176]{1,0:T(8,128)(2,1)S(1)}, s16[64,2176]{1,0:T(8,128)(2,1)S(1)}, u32[]{:S(2)}, u32[]{:S(2)}) %collective-permute-start.18) | collective-permute-done | bytes 278560 | tf_op jit(solution)/shard_map/ppermute | solution.py:264
  95.5 4.4 %collective-permute-done.19.refs_3_ = s16[64,2176]{1,0:T(8,128)(2,1)S(1)} collective-permute-done((s16[64,2176]{1,0:T(8,128)(2,1)S(1)}, s16[64,2176]{1,0:T(8,128)(2,1)S(1)}, u32[]{:S(2)}, u32[]{:S(2)}) %collective-permute-start.19) | collective-permute-done | bytes 278560 | tf_op jit(solution)/shard_map/ppermute | solution.py:264
  101.1 15.7 %collective-permute-done.21.refs_2_.v = s16[256,2176]{1,0:T(8,128)(2,1)S(1)} collective-permute-done((s16[256,2176]{1,0:T(8,128)(2,1)S(1)}, s16[256,2176]{1,0:T(8,128)(2,1)S(1)}, u32[]{:S(2)}, u32[]{:S(2)}) %collective-permute-start.21) | collective-permute-done | bytes 1114144 | tf_op jit(solution)/shard_map/ppermute | solution.py:264
  118.1 1.4 collective-permute-start.24
  119.5 4.3 %shard_map.52 = (f32[256,1024]{1,0:T(8,128)S(1)}, f32[256,1024]{1,0:T(8,128)S(1)}) custom-call(s32[32]{0:T(128)S(1)} %dynamic-slice_bitcast_fusion.s, s16[256,2176]{1,0:T(8,128)(2,1)S(1)} %shard_map.51.refs_0_, s16[256,2176]{1,0:T(8,128)(2,1)S(1)} %collective-permute-done.20.refs_1_.v, s16[256,2176]{1,0:T(8,128)(2,1)S(1)} %collective-permute-done.21.refs_2_.v, ...), custom_call_target="tpu_custom_call" | custom-call | flops 2147483648 | bytes 4194304 | tf_op jit(solution)/shard_map/pallas_call | solution.py:51
  123.9 3.1 %collective-permute-done.23.refs_3_ = s16[128,2176]{1,0:T(8,128)(2,1)S(1)} collective-permute-done((s16[128,2176]{1,0:T(8,128)(2,1)S(1)}, s16[128,2176]{1,0:T(8,128)(2,1)S(1)}, u32[]{:S(2)}, u32[]{:S(2)}) %collective-permute-start.23) | collective-permute-done | bytes 557088 | tf_op jit(solution)/shard_map/ppermute | solution.py:264
  127.0 1.9 %collective-permute-done.24.refs_4_ = s16[128,2176]{1,0:T(8,128)(2,1)S(1)} collective-permute-done((s16[128,2176]{1,0:T(8,128)(2,1)S(1)}, s16[128,2176]{1,0:T(8,128)(2,1)S(1)}, u32[]{:S(2)}, u32[]{:S(2)}) %collective-permute-start.24) | collective-permute-done | bytes 557088 | tf_op jit(solution)/shard_map/ppermute | solution.py:264
  128.9 4.5 %shard_map.55 = (f32[256,1024]{1,0:T(8,128)S(1)}, f32[256,1024]{1,0:T(8,128)S(1)}) custom-call(s32[32]{0:T(128)S(1)} %dynamic-slice_bitcast_fusion.s, s16[256,2176]{1,0:T(8,128)(2,1)S(1)} %shard_map.51.refs_0_, s16[256,2176]{1,0:T(8,128)(2,1)S(1)} %collective-permute-done.20.refs_1_.v, s16[256,2176]{1,0:T(8,128)(2,1)S(1)} %collective-permute-done.21.refs_2_.v, ...), custom_call_target="tpu_custom_call" | custom-call | flops 2147483648 | bytes 4194304 | tf_op jit(solution)/shard_map/pallas_call | solution.py:51
  133.6 2.6 %collective-permute-done.25.came_b = f32[256,1024]{1,0:T(8,128)S(1)} collective-permute-done((f32[256,1024]{1,0:T(8,128)S(1)}, f32[256,1024]{1,0:T(8,128)S(1)}, u32[]{:S(2)}, u32[]{:S(2)}) %collective-permute-start.25) | collective-permute-done | bytes 1048608 | tf_op jit(solution)/shard_map/ppermute | solution.py:276
  136.2 1.3 shard_map.56
  137.5 4.3 %collective-permute-start.26 = (s16[128,1152]{1,0:T(8,128)(2,1)S(1)}, s16[128,1152]{1,0:T(8,128)(2,1)S(1)}, u32[]{:S(2)}, u32[]{:S(2)}) collective-permute-start(s16[128,1152]{1,0:T(8,128)(2,1)S(1)} %get-tuple-element.38), channel_id=1, source_target_pairs={{0,2},{1,3},{2,0},{3,1},{4,6},{5,7},{6,4},{7,5},{8,10},{9,11},{10,... | collective-permute-start | bytes 884744 | tf_op jit(solution)/shard_map/ppermute | solution.py:264
  141.8 5.7 %collective-permute-start.27 = (s16[128,1152]{1,0:T(8,128)(2,1)S(1)}, s16[128,1152]{1,0:T(8,128)(2,1)S(1)}, u32[]{:S(2)}, u32[]{:S(2)}) collective-permute-start(s16[128,1152]{1,0:T(8,128)(2,1)S(1)} %get-tuple-element.39), channel_id=1, source_target_pairs={{0,4},{1,5},{2,6},{3,7},{4,0},{5,1},{6,2},{7,3},{8,12},{9,13},{10,... | collective-permute-start | bytes 884744 | tf_op jit(solution)/shard_map/ppermute | solution.py:264
  148.1 1.1 collective-permute-done.26.a
  149.2 12.1 %collective-permute-done.27.b = s16[128,1152]{1,0:T(8,128)(2,1)S(1)} collective-permute-done((s16[128,1152]{1,0:T(8,128)(2,1)S(1)}, s16[128,1152]{1,0:T(8,128)(2,1)S(1)}, u32[]{:S(2)}, u32[]{:S(2)}) %collective-permute-start.27) | collective-permute-done | bytes 294944 | tf_op jit(solution)/shard_map/ppermute | solution.py:264
  161.2 2.7 %collective-permute-done.28.c = s16[128,1152]{1,0:T(8,128)(2,1)S(1)} collective-permute-done((s16[128,1152]{1,0:T(8,128)(2,1)S(1)}, s16[128,1152]{1,0:T(8,128)(2,1)S(1)}, u32[]{:S(2)}, u32[]{:S(2)}) %collective-permute-start.28) | collective-permute-done | bytes 294944 | tf_op jit(solution)/shard_map/ppermute | solution.py:264
  163.9 1.0 shard_map.57
  (37 shorter events, 9.9 us)
Async XLA Ops:
  0.0 1.8 %copy-start.1 = (s32[8,16]{1,0:T(8,128)S(1)}, s32[8,16]{1,0:T(8,128)}, u32[]{:S(2)}) copy-start(s32[8,16]{1,0:T(8,128)} %m.3) | copy-start | bytes 1540
  2.9 2.0 %collective-permute-start.5 = (bf16[512,512]{1,0:T(8,128)(2,1)S(1)}, bf16[512,512]{1,0:T(8,128)(2,1)S(1)}, u32[]{:S(2)}, u32[]{:S(2)}) collective-permute-start(bf16[512,512]{1,0:T(8,128)(2,1)S(1)} %get-tuple-element.26), channel_id=1, source_target_pairs={{0,1},{1,0},{2,3},{3,2},{4,5},{5,4},{6,7},{7,6},{8,9},{9,8},{10,11... | collective-permute-start | bytes 1572872 | tf_op jit(solution)/shard_map/ppermute | solution.py:294
  3.0 6.5 %collective-permute-start = (bf16[512,512]{1,0:T(8,128)(2,1)S(1)}, bf16[512,512]{1,0:T(8,128)(2,1)S(1)}, u32[]{:S(2)}, u32[]{:S(2)}) collective-permute-start(bf16[512,512]{1,0:T(8,128)(2,1)S(1)} %get-tuple-element.24), channel_id=1, source_target_pairs={{0,1},{1,0},{2,3},{3,2},{4,5},{5,4},{6,7},{7,6},{8,9},{9,8},{10,11... | collective-permute-start | bytes 1572872 | tf_op jit(solution)/shard_map/ppermute | solution.py:294
  5.5 11.7 %collective-permute-start.6 = (bf16[512,512]{1,0:T(8,128)(2,1)S(1)}, bf16[512,512]{1,0:T(8,128)(2,1)S(1)}, u32[]{:S(2)}, u32[]{:S(2)}) collective-permute-start(bf16[512,512]{1,0:T(8,128)(2,1)S(1)} %shard_map.40.refs_0_), channel_id=1, source_target_pairs={{0,2},{1,7},{8,10},{9,15},{16,18},{17,23},{24,26},{25,31},{32,34},... | collective-permute-start | bytes 1572872 | tf_op jit(solution)/shard_map/ppermute | solution.py:296
  10.1 18.3 %collective-permute-start.1 = (bf16[512,512]{1,0:T(8,128)(2,1)S(1)}, bf16[512,512]{1,0:T(8,128)(2,1)S(1)}, u32[]{:S(2)}, u32[]{:S(2)}) collective-permute-start(bf16[512,512]{1,0:T(8,128)(2,1)S(1)} %shard_map.38.refs_0_), channel_id=1, source_target_pairs={{0,2},{1,7},{8,10},{9,15},{16,18},{17,23},{24,26},{25,31},{32,34},... | collective-permute-start | bytes 1572872 | tf_op jit(solution)/shard_map/ppermute | solution.py:296
  11.4 17.7 %collective-permute-start.7 = (bf16[512,512]{1,0:T(8,128)(2,1)S(1)}, bf16[512,512]{1,0:T(8,128)(2,1)S(1)}, u32[]{:S(2)}, u32[]{:S(2)}) collective-permute-start(bf16[512,512]{1,0:T(8,128)(2,1)S(1)} %shard_map.40.refs_0_), channel_id=1, source_target_pairs={{0,6},{1,3},{8,14},{9,11},{16,22},{17,19},{24,30},{25,27},{32,38},... | collective-permute-start | bytes 1572872 | tf_op jit(solution)/shard_map/ppermute | solution.py:297
  17.2 11.9 %collective-permute-start.8 = (bf16[512,512]{1,0:T(8,128)(2,1)S(1)}, bf16[512,512]{1,0:T(8,128)(2,1)S(1)}, u32[]{:S(2)}, u32[]{:S(2)}) collective-permute-start(bf16[512,512]{1,0:T(8,128)(2,1)S(1)} %collective-permute-done.6.refs_1_), channel_id=1, source_target_pairs={{2,4},{7,5},{10,12},{15,13},{18,20},{23,21},{26,28},{31,29},{34,36... | collective-permute-start | bytes 1572872 | tf_op jit(solution)/shard_map/ppermute | solution.py:298
  17.8 16.4 %collective-permute-start.2 = (bf16[512,512]{1,0:T(8,128)(2,1)S(1)}, bf16[512,512]{1,0:T(8,128)(2,1)S(1)}, u32[]{:S(2)}, u32[]{:S(2)}) collective-permute-start(bf16[512,512]{1,0:T(8,128)(2,1)S(1)} %shard_map.38.refs_0_), channel_id=1, source_target_pairs={{0,6},{1,3},{8,14},{9,11},{16,22},{17,19},{24,30},{25,27},{32,38},... | collective-permute-start | bytes 1572872 | tf_op jit(solution)/shard_map/ppermute | solution.py:297
  28.4 5.8 %collective-permute-start.3 = (bf16[512,512]{1,0:T(8,128)(2,1)S(1)}, bf16[512,512]{1,0:T(8,128)(2,1)S(1)}, u32[]{:S(2)}, u32[]{:S(2)}) collective-permute-start(bf16[512,512]{1,0:T(8,128)(2,1)S(1)} %collective-permute-done.1.refs_1_), channel_id=1, source_target_pairs={{2,4},{7,5},{10,12},{15,13},{18,20},{23,21},{26,28},{31,29},{34,36... | collective-permute-start | bytes 1572872 | tf_op jit(solution)/shard_map/ppermute | solution.py:298
  29.1 5.8 %copy-start = (bf16[1024,2048]{1,0:T(8,128)(2,1)S(1)}, bf16[1024,2048]{1,0:T(8,128)(2,1)}, u32[]{:S(2)}) copy-start(bf16[1024,2048]{1,0:T(8,128)(2,1)} %density.1) | copy-start | bytes 12582916
  29.7 7.0 %collective-permute-start.9 = (bf16[512,512]{1,0:T(8,128)(2,1)S(1)}, bf16[512,512]{1,0:T(8,128)(2,1)S(1)}, u32[]{:S(2)}, u32[]{:S(2)}) collective-permute-start(bf16[512,512]{1,0:T(8,128)(2,1)S(1)} %shard_map.41.own_b), channel_id=1, source_target_pairs={{0,1},{1,0},{2,3},{3,2},{4,5},{5,4},{6,7},{7,6},{8,9},{9,8},{10,11... | collective-permute-start | bytes 1572872 | tf_op jit(solution)/shard_map/ppermute | solution.py:276
  34.8 2.0 %collective-permute-start.4 = (bf16[512,512]{1,0:T(8,128)(2,1)S(1)}, bf16[512,512]{1,0:T(8,128)(2,1)S(1)}, u32[]{:S(2)}, u32[]{:S(2)}) collective-permute-start(bf16[512,512]{1,0:T(8,128)(2,1)S(1)} %shard_map.39.own_a), channel_id=1, source_target_pairs={{0,1},{1,0},{2,3},{3,2},{4,5},{5,4},{6,7},{7,6},{8,9},{9,8},{10,11... | collective-permute-start | bytes 1572872 | tf_op jit(solution)/shard_map/ppermute | solution.py:276
  39.1 9.6 %collective-permute-start.12 = (s16[128,2176]{1,0:T(8,128)(2,1)S(1)}, s16[128,2176]{1,0:T(8,128)(2,1)S(1)}, u32[]{:S(2)}, u32[]{:S(2)}) collective-permute-start(s16[128,2176]{1,0:T(8,128)(2,1)S(1)} %get-tuple-element.28), channel_id=1, source_target_pairs={{0,32},{1,9},{2,34},{3,11},{4,36},{5,13},{6,38},{7,15},{8,40},{9,1... | collective-permute-start | bytes 1671176 | tf_op jit(solution)/shard_map/ppermute | solution.py:264
  40.7 12.0 %collective-permute-start.10 = (s16[128,2176]{1,0:T(8,128)(2,1)S(1)}, s16[128,2176]{1,0:T(8,128)(2,1)S(1)}, u32[]{:S(2)}, u32[]{:S(2)}) collective-permute-start(s16[128,2176]{1,0:T(8,128)(2,1)S(1)} %get-tuple-element.27), channel_id=1, source_target_pairs={{0,96},{1,25},{2,98},{3,27},{4,100},{5,29},{6,102},{7,31},{8,104},... | collective-permute-start | bytes 1671176 | tf_op jit(solution)/shard_map/ppermute | solution.py:264
  49.8 16.8 %collective-permute-start.13 = (s16[256,2176]{1,0:T(8,128)(2,1)S(1)}, s16[256,2176]{1,0:T(8,128)(2,1)S(1)}, u32[]{:S(2)}, u32[]{:S(2)}) collective-permute-start(s16[256,2176]{1,0:T(8,128)(2,1)S(1)} %shard_map.48), channel_id=1, source_target_pairs={{0,96},{1,25},{2,98},{3,27},{4,100},{5,29},{6,102},{7,31},{8,104},... | collective-permute-start | bytes 3342344 | tf_op jit(solution)/shard_map/ppermute | solution.py:264
  53.8 15.6 %collective-permute-start.11 = (s16[256,2176]{1,0:T(8,128)(2,1)S(1)}, s16[256,2176]{1,0:T(8,128)(2,1)S(1)}, u32[]{:S(2)}, u32[]{:S(2)}) collective-permute-start(s16[256,2176]{1,0:T(8,128)(2,1)S(1)} %shard_map.46), channel_id=1, source_target_pairs={{0,32},{1,9},{2,34},{3,11},{4,36},{5,13},{6,38},{7,15},{8,40},{9,1... | collective-permute-start | bytes 3342344 | tf_op jit(solution)/shard_map/ppermute | solution.py:264
  70.8 6.6 %collective-permute-start.14 = (s16[64,2176]{1,0:T(8,128)(2,1)S(1)}, s16[64,2176]{1,0:T(8,128)(2,1)S(1)}, u32[]{:S(2)}, u32[]{:S(2)}) collective-permute-start(s16[64,2176]{1,0:T(8,128)(2,1)S(1)} %get-tuple-element.30), channel_id=1, source_target_pairs={{0,8},{1,33},{2,10},{3,35},{4,12},{5,37},{6,14},{7,39},{8,0},{9,41... | collective-permute-start | bytes 835592 | tf_op jit(solution)/shard_map/ppermute | solution.py:264
  72.4 10.5 %collective-permute-start.15 = (s16[64,2176]{1,0:T(8,128)(2,1)S(1)}, s16[64,2176]{1,0:T(8,128)(2,1)S(1)}, u32[]{:S(2)}, u32[]{:S(2)}) collective-permute-start(s16[64,2176]{1,0:T(8,128)(2,1)S(1)} %get-tuple-element.31), channel_id=1, source_target_pairs={{0,16},{1,65},{2,18},{3,67},{4,20},{5,69},{6,22},{7,71},{8,24},{9,... | collective-permute-start | bytes 835592 | tf_op jit(solution)/shard_map/ppermute | solution.py:264
  75.3 10.5 %collective-permute-start.16 = (s16[64,2176]{1,0:T(8,128)(2,1)S(1)}, s16[64,2176]{1,0:T(8,128)(2,1)S(1)}, u32[]{:S(2)}, u32[]{:S(2)}) collective-permute-start(s16[64,2176]{1,0:T(8,128)(2,1)S(1)} %get-tuple-element.32), channel_id=1, source_target_pairs={{0,24},{1,97},{2,26},{3,99},{4,28},{5,101},{6,30},{7,103},{8,16},{... | collective-permute-start | bytes 835592 | tf_op jit(solution)/shard_map/ppermute | solution.py:264
  86.2 6.6 %collective-permute-start.17 = (s16[64,2176]{1,0:T(8,128)(2,1)S(1)}, s16[64,2176]{1,0:T(8,128)(2,1)S(1)}, u32[]{:S(2)}, u32[]{:S(2)}) collective-permute-start(s16[64,2176]{1,0:T(8,128)(2,1)S(1)} %shard_map.50.refs_0_), channel_id=1, source_target_pairs={{0,8},{1,33},{2,10},{3,35},{4,12},{5,37},{6,14},{7,39},{8,0},{9,41... | collective-permute-start | bytes 835592 | tf_op jit(solution)/shard_map/ppermute | solution.py:264
  86.3 9.3 %collective-permute-start.18 = (s16[64,2176]{1,0:T(8,128)(2,1)S(1)}, s16[64,2176]{1,0:T(8,128)(2,1)S(1)}, u32[]{:S(2)}, u32[]{:S(2)}) collective-permute-start(s16[64,2176]{1,0:T(8,128)(2,1)S(1)} %shard_map.50.refs_0_), channel_id=1, source_target_pairs={{0,16},{1,65},{2,18},{3,67},{4,20},{5,69},{6,22},{7,71},{8,24},{9,... | collective-permute-start | bytes 835592 | tf_op jit(solution)/shard_map/ppermute | solution.py:264
  87.9 12.0 %collective-permute-start.19 = (s16[64,2176]{1,0:T(8,128)(2,1)S(1)}, s16[64,2176]{1,0:T(8,128)(2,1)S(1)}, u32[]{:S(2)}, u32[]{:S(2)}) collective-permute-start(s16[64,2176]{1,0:T(8,128)(2,1)S(1)} %shard_map.50.refs_0_), channel_id=1, source_target_pairs={{0,24},{1,97},{2,26},{3,99},{4,28},{5,101},{6,30},{7,103},{8,16},{... | collective-permute-start | bytes 835592 | tf_op jit(solution)/shard_map/ppermute | solution.py:264
  100.0 16.8 %collective-permute-start.21 = (s16[256,2176]{1,0:T(8,128)(2,1)S(1)}, s16[256,2176]{1,0:T(8,128)(2,1)S(1)}, u32[]{:S(2)}, u32[]{:S(2)}) collective-permute-start(s16[256,2176]{1,0:T(8,128)(2,1)S(1)} %shard_map.51.refs_0_), channel_id=1, source_target_pairs={{0,96},{1,25},{2,98},{3,27},{4,100},{5,29},{6,102},{7,31},{8,104},... | collective-permute-start | bytes 3342344 | tf_op jit(solution)/shard_map/ppermute | solution.py:264
  100.1 17.4 %collective-permute-start.20 = (s16[256,2176]{1,0:T(8,128)(2,1)S(1)}, s16[256,2176]{1,0:T(8,128)(2,1)S(1)}, u32[]{:S(2)}, u32[]{:S(2)}) collective-permute-start(s16[256,2176]{1,0:T(8,128)(2,1)S(1)} %shard_map.51.refs_0_), channel_id=1, source_target_pairs={{0,32},{1,9},{2,34},{3,11},{4,36},{5,13},{6,38},{7,15},{8,40},{9,1... | collective-permute-start | bytes 3342344 | tf_op jit(solution)/shard_map/ppermute | solution.py:264
  117.4 9.6 %collective-permute-start.23 = (s16[128,2176]{1,0:T(8,128)(2,1)S(1)}, s16[128,2176]{1,0:T(8,128)(2,1)S(1)}, u32[]{:S(2)}, u32[]{:S(2)}) collective-permute-start(s16[128,2176]{1,0:T(8,128)(2,1)S(1)} %shard_map.53), channel_id=1, source_target_pairs={{0,32},{1,9},{2,34},{3,11},{4,36},{5,13},{6,38},{7,15},{8,40},{9,1... | collective-permute-start | bytes 1671176 | tf_op jit(solution)/shard_map/ppermute | solution.py:264
  118.1 10.8 %collective-permute-start.24 = (s16[128,2176]{1,0:T(8,128)(2,1)S(1)}, s16[128,2176]{1,0:T(8,128)(2,1)S(1)}, u32[]{:S(2)}, u32[]{:S(2)}) collective-permute-start(s16[128,2176]{1,0:T(8,128)(2,1)S(1)} %shard_map.54), channel_id=1, source_target_pairs={{0,96},{1,25},{2,98},{3,27},{4,100},{5,29},{6,102},{7,31},{8,104},... | collective-permute-start | bytes 1671176 | tf_op jit(solution)/shard_map/ppermute | solution.py:264
  123.8 9.8 %collective-permute-start.22 = (f32[256,1024]{1,0:T(8,128)S(1)}, f32[256,1024]{1,0:T(8,128)S(1)}, u32[]{:S(2)}, u32[]{:S(2)}) collective-permute-start(f32[256,1024]{1,0:T(8,128)S(1)} %get-tuple-element.34), channel_id=1, source_target_pairs={{0,1},{1,0},{2,3},{3,2},{4,5},{5,4},{6,7},{7,6},{8,9},{9,8},{10,11... | collective-permute-start | bytes 3145736 | tf_op jit(solution)/shard_map/ppermute | solution.py:276
  133.5 2.7 %collective-permute-start.25 = (f32[256,1024]{1,0:T(8,128)S(1)}, f32[256,1024]{1,0:T(8,128)S(1)}, u32[]{:S(2)}, u32[]{:S(2)}) collective-permute-start(f32[256,1024]{1,0:T(8,128)S(1)} %get-tuple-element.36), channel_id=1, source_target_pairs={{0,1},{1,0},{2,3},{3,2},{4,5},{5,4},{6,7},{7,6},{8,9},{9,8},{10,11... | collective-permute-start | bytes 3145736 | tf_op jit(solution)/shard_map/ppermute | solution.py:276
  137.5 11.7 %collective-permute-start.26 = (s16[128,1152]{1,0:T(8,128)(2,1)S(1)}, s16[128,1152]{1,0:T(8,128)(2,1)S(1)}, u32[]{:S(2)}, u32[]{:S(2)}) collective-permute-start(s16[128,1152]{1,0:T(8,128)(2,1)S(1)} %get-tuple-element.38), channel_id=1, source_target_pairs={{0,2},{1,3},{2,0},{3,1},{4,6},{5,7},{6,4},{7,5},{8,10},{9,11},{10,... | collective-permute-start | bytes 884744 | tf_op jit(solution)/shard_map/ppermute | solution.py:264
  141.8 19.4 %collective-permute-start.27 = (s16[128,1152]{1,0:T(8,128)(2,1)S(1)}, s16[128,1152]{1,0:T(8,128)(2,1)S(1)}, u32[]{:S(2)}, u32[]{:S(2)}) collective-permute-start(s16[128,1152]{1,0:T(8,128)(2,1)S(1)} %get-tuple-element.39), channel_id=1, source_target_pairs={{0,4},{1,5},{2,6},{3,7},{4,0},{5,1},{6,2},{7,3},{8,12},{9,13},{10,... | collective-permute-start | bytes 884744 | tf_op jit(solution)/shard_map/ppermute | solution.py:264
  147.6 16.3 %collective-permute-start.28 = (s16[128,1152]{1,0:T(8,128)(2,1)S(1)}, s16[128,1152]{1,0:T(8,128)(2,1)S(1)}, u32[]{:S(2)}, u32[]{:S(2)}) collective-permute-start(s16[128,1152]{1,0:T(8,128)(2,1)S(1)} %get-tuple-element.40), channel_id=1, source_target_pairs={{0,6},{1,7},{2,4},{3,5},{4,2},{5,3},{6,0},{7,1},{8,14},{9,15},{10,... | collective-permute-start | bytes 884744 | tf_op jit(solution)/shard_map/ppermute | solution.py:264

commit v5 on v4

--- a/solution.py
+++ b/solution.py
@@ -35,7 +35,7 @@
     subs = [second, second ^ 1, second ^ 2, second ^ 3]
     source = 0 if z == 0 else 1 if z == 1 + 2 * core else 3 if z == 2 else 2
     own_square = int(z * 2 + core == (x * 4 + y) // 2)
-    where = [turns(x, y).index(((z ^ flip) - z) % 4) for flip in range(4)]
+    where = [turns(x, y).index(q) for q in range(4)]
     return [*quarters, *chosen, *subs, *where, core, own_square, y % 2, source, odd] + [0] * 11
 
 
@@ -344,8 +344,8 @@
     coded = shape(128, SLAB + LANES, I16)
     own, *parts = call(deal_kernel, [shape(128, SLAB, F32)] + [coded] * 3, [s], *sums)
     came = []
-    for flip in (1, 2, 3):
-        came.append(send(parts[flip - 1], lambda x, y, z, core: (x, y, z ^ flip, core)))
+    for d in (1, 3, 2):
+        came.append(send(parts[d - 1], lambda x, y, z, core: (x, y, z + d, core)))
     return call(finish_kernel, shape(128, SLAB, F32), [], own, *came)
 
 

time: 166 us -> 163 us (0.982)
  waiting for transfers between devices: 88.7 us -> 84.5 us
    ppermute x17, waiting for transfers between devices: 71.2 us -> 67 us  [send(): return lax.ppermute(v, AXES, [(place(*d), place(*to(*d))) for d in DEVICES])]
  transfers between devices with their start and end apart: 29 -> 29, of which waited for: 21 -> 21; matrix products, arithmetic and copies ran while one was open for 0% -> 0% of each run, Pallas kernels for 13% -> 14%
where the time goes in v5:
time: 163 us; the launch traced here: 162 us
  waiting for transfers between devices  84.5 us (52%)
  starting transfers between devices  45.1 us (28%)
  Pallas kernels  29.7 us (18%)
  local copies, waits for them, and re-layouts  2.48 us (2%)
    ppermute x17, waiting for transfers between devices, send(): return lax.ppermute(v, AXES, [(place(*d), place(*to(*d))) for d in DEVICES])  67 us
    ppermute x17, starting transfers between devices, send(): return lax.ppermute(v, AXES, [(place(*d), place(*to(*d))) for d in DEVICES])  30.9 us
    pallas_call x21, Pallas kernels, call(): pl.pallas_call(kernel, out_shape=out, in_specs=[pl.BlockSpec(memory_space...  29.7 us
    ppermute x2, waiting for transfers between devices, spread_column(): one = lax.ppermute(half, axes, [(0, 2), (1, 7)])  12.8 us
    ppermute x2, starting transfers between devices, spread_column(): one = lax.ppermute(half, axes, [(0, 2), (1, 7)])  5.29 us
    ppermute x2, starting transfers between devices, spread_column(): two = lax.ppermute(half, axes, [(0, 6), (1, 3)])  3.51 us
    ppermute x4, starting transfers between devices, swap(): return lax.ppermute(v, 'core', [(0, 1), (1, 0)])  3.44 us
  transfers between devices with their start and end apart: 29, of which 21 were waited for; matrix products, arithmetic and copies ran while one was open for 0% of the time, Pallas kernels for 14%

profile of v5, /device:TPU:0, one launch (start us, length us, event | category | flops | bytes accessed | tf_op | source)
XLA Modules:
  0.0 162.2 jit_solution(5901250706142643090)
XLA Ops:
  0.0 1.8 %slice.3.density = bf16[1024,1024]{1,0:T(8,128)(2,1)S(1)} slice(bf16[1024,2048]{1,0:T(8,128)(2,1)} %density.1), slice={[0:1024], [0:1024]} | slice | bytes 4194304 | tf_op jit(solution)/shard_map/slice | solution.py:307
  1.8 1.1 shard_map.37
  5.5 4.0 %collective-permute-start.6 = (bf16[512,512]{1,0:T(8,128)(2,1)S(1)}, bf16[512,512]{1,0:T(8,128)(2,1)S(1)}, u32[]{:S(2)}, u32[]{:S(2)}) collective-permute-start(bf16[512,512]{1,0:T(8,128)(2,1)S(1)} %shard_map.40.refs_0_), channel_id=1, source_target_pairs={{0,2},{1,7},{8,10},{9,15},{16,18},{17,23},{24,26},{25,31},{32,34},... | collective-permute-start | bytes 1572872 | tf_op jit(solution)/shard_map/ppermute | solution.py:296
  10.1 1.3 collective-permute-start.1
  11.4 2.2 %collective-permute-start.7 = (bf16[512,512]{1,0:T(8,128)(2,1)S(1)}, bf16[512,512]{1,0:T(8,128)(2,1)S(1)}, u32[]{:S(2)}, u32[]{:S(2)}) collective-permute-start(bf16[512,512]{1,0:T(8,128)(2,1)S(1)} %shard_map.40.refs_0_), channel_id=1, source_target_pairs={{0,6},{1,3},{8,14},{9,11},{16,22},{17,19},{24,30},{25,27},{32,38},... | collective-permute-start | bytes 1572872 | tf_op jit(solution)/shard_map/ppermute | solution.py:297
  13.6 3.6 %collective-permute-done.6.refs_1_ = bf16[512,512]{1,0:T(8,128)(2,1)S(1)} collective-permute-done((bf16[512,512]{1,0:T(8,128)(2,1)S(1)}, bf16[512,512]{1,0:T(8,128)(2,1)S(1)}, u32[]{:S(2)}, u32[]{:S(2)}) %collective-permute-start.6) | collective-permute-done | bytes 524320 | tf_op jit(solution)/shard_map/ppermute | solution.py:296
  17.8 1.3 collective-permute-start.2
  19.2 9.2 %collective-permute-done.1.refs_1_ = bf16[512,512]{1,0:T(8,128)(2,1)S(1)} collective-permute-done((bf16[512,512]{1,0:T(8,128)(2,1)S(1)}, bf16[512,512]{1,0:T(8,128)(2,1)S(1)}, u32[]{:S(2)}, u32[]{:S(2)}) %collective-permute-start.1) | collective-permute-done | bytes 524320 | tf_op jit(solution)/shard_map/ppermute | solution.py:296
  29.7 3.2 %collective-permute-start.9 = (bf16[512,512]{1,0:T(8,128)(2,1)S(1)}, bf16[512,512]{1,0:T(8,128)(2,1)S(1)}, u32[]{:S(2)}, u32[]{:S(2)}) collective-permute-start(bf16[512,512]{1,0:T(8,128)(2,1)S(1)} %shard_map.41.own_b), channel_id=1, source_target_pairs={{0,1},{1,0},{2,3},{3,2},{4,5},{5,4},{6,7},{7,6},{8,9},{9,8},{10,11... | collective-permute-start | bytes 1572872 | tf_op jit(solution)/shard_map/ppermute | solution.py:276
  32.9 1.3 collective-permute-done.2.refs_2_
  34.9 1.8 %shard_map.42.masked.refs_3_.refs_5_ = bf16[1024,2048]{1,0:T(8,128)(2,1)S(1)} custom-call(s32[8,16]{1,0:T(8,128)S(1)} %copy-done.1, bf16[1024,2048]{1,0:T(8,128)(2,1)S(1)} %copy-done), custom_call_target="tpu_custom_call" | custom-call | flops 4194304 | bytes 4194304 | tf_op jit(solution)/shard_map/pallas_call | solution.py:51
  36.8 2.3 %shard_map.45 = (s16[128,2176]{1,0:T(8,128)(2,1)S(1)}, s16[128,2176]{1,0:T(8,128)(2,1)S(1)}) custom-call(s32[32]{0:T(128)S(1)} %dynamic-slice_bitcast_fusion.s, bf16[512,512]{1,0:T(8,128)(2,1)S(1)} %shard_map.39.own_a, bf16[512,512]{1,0:T(8,128)(2,1)S(1)} %collective-permute-done.4.other_a, bf16[512,512]{1,0:T(8,128)(2,1)S(1)} %shard_map.41.own_b, ...), custom_call_target="tpu_custom_call" | custom-call | flops 1073741824 | bytes 4194304 | tf_op jit(solution)/shard_map/pallas_call | solution.py:51
  39.1 1.6 collective-permute-start.12
  40.7 2.1 %collective-permute-start.10 = (s16[128,2176]{1,0:T(8,128)(2,1)S(1)}, s16[128,2176]{1,0:T(8,128)(2,1)S(1)}, u32[]{:S(2)}, u32[]{:S(2)}) collective-permute-start(s16[128,2176]{1,0:T(8,128)(2,1)S(1)} %get-tuple-element.27), channel_id=1, source_target_pairs={{0,96},{1,25},{2,98},{3,27},{4,100},{5,29},{6,102},{7,31},{8,104},... | collective-permute-start | bytes 1671176 | tf_op jit(solution)/shard_map/ppermute | solution.py:264
  42.8 1.9 %shard_map.47.mine = f32[256,2048]{1,0:T(8,128)S(1)} custom-call(s32[32]{0:T(128)S(1)} %dynamic-slice_bitcast_fusion.s, bf16[512,512]{1,0:T(8,128)(2,1)S(1)} %shard_map.39.own_a, bf16[512,512]{1,0:T(8,128)(2,1)S(1)} %collective-permute-done.4.other_a, bf16[512,512]{1,0:T(8,128)(2,1)S(1)} %shard_map.41.own_b, ...), custom_call_target="tpu_custom_call" | custom-call | flops 1073741824 | bytes 4194304 | tf_op jit(solution)/shard_map/pallas_call | solution.py:51
  44.7 1.9 %shard_map.44.mine = f32[256,2048]{1,0:T(8,128)S(1)} custom-call(s32[32]{0:T(128)S(1)} %dynamic-slice_bitcast_fusion.s, bf16[512,512]{1,0:T(8,128)(2,1)S(1)} %shard_map.39.own_a, bf16[512,512]{1,0:T(8,128)(2,1)S(1)} %collective-permute-done.4.other_a, bf16[512,512]{1,0:T(8,128)(2,1)S(1)} %shard_map.41.own_b, ...), custom_call_target="tpu_custom_call" | custom-call | flops 1073741824 | bytes 4194304 | tf_op jit(solution)/shard_map/pallas_call | solution.py:51
  46.6 2.1 %collective-permute-done.12.came = s16[128,2176]{1,0:T(8,128)(2,1)S(1)} collective-permute-done((s16[128,2176]{1,0:T(8,128)(2,1)S(1)}, s16[128,2176]{1,0:T(8,128)(2,1)S(1)}, u32[]{:S(2)}, u32[]{:S(2)}) %collective-permute-start.12) | collective-permute-done | bytes 557088 | tf_op jit(solution)/shard_map/ppermute | solution.py:264
  48.7 1.1 shard_map.48
  49.8 2.8 %collective-permute-start.13 = (s16[256,2176]{1,0:T(8,128)(2,1)S(1)}, s16[256,2176]{1,0:T(8,128)(2,1)S(1)}, u32[]{:S(2)}, u32[]{:S(2)}) collective-permute-start(s16[256,2176]{1,0:T(8,128)(2,1)S(1)} %shard_map.48), channel_id=1, source_target_pairs={{0,96},{1,25},{2,98},{3,27},{4,100},{5,29},{6,102},{7,31},{8,104},... | collective-permute-start | bytes 3342344 | tf_op jit(solution)/shard_map/ppermute | solution.py:264
  52.7 1.1 shard_map.46
  54.1 2.1 %shard_map.43.own = f32[256,2048]{1,0:T(8,128)S(1)} custom-call(s32[32]{0:T(128)S(1)} %dynamic-slice_bitcast_fusion.s, bf16[512,512]{1,0:T(8,128)(2,1)S(1)} %shard_map.39.own_a, bf16[512,512]{1,0:T(8,128)(2,1)S(1)} %collective-permute-done.4.other_a, bf16[512,512]{1,0:T(8,128)(2,1)S(1)} %shard_map.41.own_b, ...), custom_call_target="tpu_custom_call" | custom-call | flops 1073741824 | bytes 4194304 | tf_op jit(solution)/shard_map/pallas_call | solution.py:51
  56.2 10.5 %collective-permute-done.13.b = s16[256,2176]{1,0:T(8,128)(2,1)S(1)} collective-permute-done((s16[256,2176]{1,0:T(8,128)(2,1)S(1)}, s16[256,2176]{1,0:T(8,128)(2,1)S(1)}, u32[]{:S(2)}, u32[]{:S(2)}) %collective-permute-start.13) | collective-permute-done | bytes 1114144 | tf_op jit(solution)/shard_map/ppermute | solution.py:264
  66.6 2.7 %collective-permute-done.11.a = s16[256,2176]{1,0:T(8,128)(2,1)S(1)} collective-permute-done((s16[256,2176]{1,0:T(8,128)(2,1)S(1)}, s16[256,2176]{1,0:T(8,128)(2,1)S(1)}, u32[]{:S(2)}, u32[]{:S(2)}) %collective-permute-start.11) | collective-permute-done | bytes 1114144 | tf_op jit(solution)/shard_map/ppermute | solution.py:264
  69.4 1.4 shard_map.49
  70.8 1.7 %collective-permute-start.14 = (s16[64,2176]{1,0:T(8,128)(2,1)S(1)}, s16[64,2176]{1,0:T(8,128)(2,1)S(1)}, u32[]{:S(2)}, u32[]{:S(2)}) collective-permute-start(s16[64,2176]{1,0:T(8,128)(2,1)S(1)} %get-tuple-element.30), channel_id=1, source_target_pairs={{0,8},{1,33},{2,10},{3,35},{4,12},{5,37},{6,14},{7,39},{8,0},{9,41... | collective-permute-start | bytes 835592 | tf_op jit(solution)/shard_map/ppermute | solution.py:264
  72.4 2.9 %collective-permute-start.15 = (s16[64,2176]{1,0:T(8,128)(2,1)S(1)}, s16[64,2176]{1,0:T(8,128)(2,1)S(1)}, u32[]{:S(2)}, u32[]{:S(2)}) collective-permute-start(s16[64,2176]{1,0:T(8,128)(2,1)S(1)} %get-tuple-element.31), channel_id=1, source_target_pairs={{0,16},{1,65},{2,18},{3,67},{4,20},{5,69},{6,22},{7,71},{8,24},{9,... | collective-permute-start | bytes 835592 | tf_op jit(solution)/shard_map/ppermute | solution.py:264
  75.5 1.8 %collective-permute-done.14.a = s16[64,2176]{1,0:T(8,128)(2,1)S(1)} collective-permute-done((s16[64,2176]{1,0:T(8,128)(2,1)S(1)}, s16[64,2176]{1,0:T(8,128)(2,1)S(1)}, u32[]{:S(2)}, u32[]{:S(2)}) %collective-permute-start.14) | collective-permute-done | bytes 278560 | tf_op jit(solution)/shard_map/ppermute | solution.py:264
  77.4 5.5 %collective-permute-done.15.b = s16[64,2176]{1,0:T(8,128)(2,1)S(1)} collective-permute-done((s16[64,2176]{1,0:T(8,128)(2,1)S(1)}, s16[64,2176]{1,0:T(8,128)(2,1)S(1)}, u32[]{:S(2)}, u32[]{:S(2)}) %collective-permute-start.15) | collective-permute-done | bytes 278560 | tf_op jit(solution)/shard_map/ppermute | solution.py:264
  82.9 2.9 %collective-permute-done.16.c = s16[64,2176]{1,0:T(8,128)(2,1)S(1)} collective-permute-done((s16[64,2176]{1,0:T(8,128)(2,1)S(1)}, s16[64,2176]{1,0:T(8,128)(2,1)S(1)}, u32[]{:S(2)}, u32[]{:S(2)}) %collective-permute-start.16) | collective-permute-done | bytes 278560 | tf_op jit(solution)/shard_map/ppermute | solution.py:264
  86.3 1.7 %collective-permute-start.18 = (s16[64,2176]{1,0:T(8,128)(2,1)S(1)}, s16[64,2176]{1,0:T(8,128)(2,1)S(1)}, u32[]{:S(2)}, u32[]{:S(2)}) collective-permute-start(s16[64,2176]{1,0:T(8,128)(2,1)S(1)} %shard_map.50.refs_0_), channel_id=1, source_target_pairs={{0,16},{1,65},{2,18},{3,67},{4,20},{5,69},{6,22},{7,71},{8,24},{9,... | collective-permute-start | bytes 835592 | tf_op jit(solution)/shard_map/ppermute | solution.py:264
  87.9 3.0 %collective-permute-start.19 = (s16[64,2176]{1,0:T(8,128)(2,1)S(1)}, s16[64,2176]{1,0:T(8,128)(2,1)S(1)}, u32[]{:S(2)}, u32[]{:S(2)}) collective-permute-start(s16[64,2176]{1,0:T(8,128)(2,1)S(1)} %shard_map.50.refs_0_), channel_id=1, source_target_pairs={{0,24},{1,97},{2,26},{3,99},{4,28},{5,101},{6,30},{7,103},{8,16},{... | collective-permute-start | bytes 835592 | tf_op jit(solution)/shard_map/ppermute | solution.py:264
  91.0 1.8 %collective-permute-done.17.refs_1_ = s16[64,2176]{1,0:T(8,128)(2,1)S(1)} collective-permute-done((s16[64,2176]{1,0:T(8,128)(2,1)S(1)}, s16[64,2176]{1,0:T(8,128)(2,1)S(1)}, u32[]{:S(2)}, u32[]{:S(2)}) %collective-permute-start.17) | collective-permute-done | bytes 278560 | tf_op jit(solution)/shard_map/ppermute | solution.py:264
  92.8 2.7 %collective-permute-done.18.refs_2_ = s16[64,2176]{1,0:T(8,128)(2,1)S(1)} collective-permute-done((s16[64,2176]{1,0:T(8,128)(2,1)S(1)}, s16[64,2176]{1,0:T(8,128)(2,1)S(1)}, u32[]{:S(2)}, u32[]{:S(2)}) %collective-permute-start.18) | collective-permute-done | bytes 278560 | tf_op jit(solution)/shard_map/ppermute | solution.py:264
  95.5 4.4 %collective-permute-done.19.refs_3_ = s16[64,2176]{1,0:T(8,128)(2,1)S(1)} collective-permute-done((s16[64,2176]{1,0:T(8,128)(2,1)S(1)}, s16[64,2176]{1,0:T(8,128)(2,1)S(1)}, u32[]{:S(2)}, u32[]{:S(2)}) %collective-permute-start.19) | collective-permute-done | bytes 278560 | tf_op jit(solution)/shard_map/ppermute | solution.py:264
  101.1 15.7 %collective-permute-done.21.refs_2_.v = s16[256,2176]{1,0:T(8,128)(2,1)S(1)} collective-permute-done((s16[256,2176]{1,0:T(8,128)(2,1)S(1)}, s16[256,2176]{1,0:T(8,128)(2,1)S(1)}, u32[]{:S(2)}, u32[]{:S(2)}) %collective-permute-start.21) | collective-permute-done | bytes 1114144 | tf_op jit(solution)/shard_map/ppermute | solution.py:264
  118.1 1.4 collective-permute-start.24
  119.5 4.3 %shard_map.52 = (f32[256,1024]{1,0:T(8,128)S(1)}, f32[256,1024]{1,0:T(8,128)S(1)}) custom-call(s32[32]{0:T(128)S(1)} %dynamic-slice_bitcast_fusion.s, s16[256,2176]{1,0:T(8,128)(2,1)S(1)} %shard_map.51.refs_0_, s16[256,2176]{1,0:T(8,128)(2,1)S(1)} %collective-permute-done.20.refs_1_.v, s16[256,2176]{1,0:T(8,128)(2,1)S(1)} %collective-permute-done.21.refs_2_.v, ...), custom_call_target="tpu_custom_call" | custom-call | flops 2147483648 | bytes 4194304 | tf_op jit(solution)/shard_map/pallas_call | solution.py:51
  123.9 3.1 %collective-permute-done.23.refs_3_ = s16[128,2176]{1,0:T(8,128)(2,1)S(1)} collective-permute-done((s16[128,2176]{1,0:T(8,128)(2,1)S(1)}, s16[128,2176]{1,0:T(8,128)(2,1)S(1)}, u32[]{:S(2)}, u32[]{:S(2)}) %collective-permute-start.23) | collective-permute-done | bytes 557088 | tf_op jit(solution)/shard_map/ppermute | solution.py:264
  127.0 1.9 %collective-permute-done.24.refs_4_ = s16[128,2176]{1,0:T(8,128)(2,1)S(1)} collective-permute-done((s16[128,2176]{1,0:T(8,128)(2,1)S(1)}, s16[128,2176]{1,0:T(8,128)(2,1)S(1)}, u32[]{:S(2)}, u32[]{:S(2)}) %collective-permute-start.24) | collective-permute-done | bytes 557088 | tf_op jit(solution)/shard_map/ppermute | solution.py:264
  128.9 4.5 %shard_map.55 = (f32[256,1024]{1,0:T(8,128)S(1)}, f32[256,1024]{1,0:T(8,128)S(1)}) custom-call(s32[32]{0:T(128)S(1)} %dynamic-slice_bitcast_fusion.s, s16[256,2176]{1,0:T(8,128)(2,1)S(1)} %shard_map.51.refs_0_, s16[256,2176]{1,0:T(8,128)(2,1)S(1)} %collective-permute-done.20.refs_1_.v, s16[256,2176]{1,0:T(8,128)(2,1)S(1)} %collective-permute-done.21.refs_2_.v, ...), custom_call_target="tpu_custom_call" | custom-call | flops 2147483648 | bytes 4194304 | tf_op jit(solution)/shard_map/pallas_call | solution.py:51
  133.6 2.6 %collective-permute-done.25.came_b = f32[256,1024]{1,0:T(8,128)S(1)} collective-permute-done((f32[256,1024]{1,0:T(8,128)S(1)}, f32[256,1024]{1,0:T(8,128)S(1)}, u32[]{:S(2)}, u32[]{:S(2)}) %collective-permute-start.25) | collective-permute-done | bytes 1048608 | tf_op jit(solution)/shard_map/ppermute | solution.py:276
  136.2 1.3 shard_map.56
  137.5 4.3 %collective-permute-start.26 = (s16[128,1152]{1,0:T(8,128)(2,1)S(1)}, s16[128,1152]{1,0:T(8,128)(2,1)S(1)}, u32[]{:S(2)}, u32[]{:S(2)}) collective-permute-start(s16[128,1152]{1,0:T(8,128)(2,1)S(1)} %get-tuple-element.38), channel_id=1, source_target_pairs={{0,2},{1,3},{2,4},{3,5},{4,6},{5,7},{6,0},{7,1},{8,10},{9,11},{10,... | collective-permute-start | bytes 884744 | tf_op jit(solution)/shard_map/ppermute | solution.py:264
  141.8 4.1 %collective-permute-start.27 = (s16[128,1152]{1,0:T(8,128)(2,1)S(1)}, s16[128,1152]{1,0:T(8,128)(2,1)S(1)}, u32[]{:S(2)}, u32[]{:S(2)}) collective-permute-start(s16[128,1152]{1,0:T(8,128)(2,1)S(1)} %get-tuple-element.39), channel_id=1, source_target_pairs={{0,6},{1,7},{2,0},{3,1},{4,2},{5,3},{6,4},{7,5},{8,14},{9,15},{10,... | collective-permute-start | bytes 884744 | tf_op jit(solution)/shard_map/ppermute | solution.py:264
  145.9 3.6 %collective-permute-start.28 = (s16[128,1152]{1,0:T(8,128)(2,1)S(1)}, s16[128,1152]{1,0:T(8,128)(2,1)S(1)}, u32[]{:S(2)}, u32[]{:S(2)}) collective-permute-start(s16[128,1152]{1,0:T(8,128)(2,1)S(1)} %get-tuple-element.40), channel_id=1, source_target_pairs={{0,4},{1,5},{2,6},{3,7},{4,0},{5,1},{6,2},{7,3},{8,12},{9,13},{10,... | collective-permute-start | bytes 884744 | tf_op jit(solution)/shard_map/ppermute | solution.py:264
  149.5 3.7 %collective-permute-done.26.a = s16[128,1152]{1,0:T(8,128)(2,1)S(1)} collective-permute-done((s16[128,1152]{1,0:T(8,128)(2,1)S(1)}, s16[128,1152]{1,0:T(8,128)(2,1)S(1)}, u32[]{:S(2)}, u32[]{:S(2)}) %collective-permute-start.26) | collective-permute-done | bytes 294944 | tf_op jit(solution)/shard_map/ppermute | solution.py:264
  153.2 2.1 %collective-permute-done.27.b = s16[128,1152]{1,0:T(8,128)(2,1)S(1)} collective-permute-done((s16[128,1152]{1,0:T(8,128)(2,1)S(1)}, s16[128,1152]{1,0:T(8,128)(2,1)S(1)}, u32[]{:S(2)}, u32[]{:S(2)}) %collective-permute-start.27) | collective-permute-done | bytes 294944 | tf_op jit(solution)/shard_map/ppermute | solution.py:264
  155.3 5.8 %collective-permute-done.28.c = s16[128,1152]{1,0:T(8,128)(2,1)S(1)} collective-permute-done((s16[128,1152]{1,0:T(8,128)(2,1)S(1)}, s16[128,1152]{1,0:T(8,128)(2,1)S(1)}, u32[]{:S(2)}, u32[]{:S(2)}) %collective-permute-start.28) | collective-permute-done | bytes 294944 | tf_op jit(solution)/shard_map/ppermute | solution.py:264
  (37 shorter events, 10.5 us)
Async XLA Ops:
  0.0 1.8 %copy-start.1 = (s32[8,16]{1,0:T(8,128)S(1)}, s32[8,16]{1,0:T(8,128)}, u32[]{:S(2)}) copy-start(s32[8,16]{1,0:T(8,128)} %m.3) | copy-start | bytes 1540
  2.9 2.0 %collective-permute-start.5 = (bf16[512,512]{1,0:T(8,128)(2,1)S(1)}, bf16[512,512]{1,0:T(8,128)(2,1)S(1)}, u32[]{:S(2)}, u32[]{:S(2)}) collective-permute-start(bf16[512,512]{1,0:T(8,128)(2,1)S(1)} %get-tuple-element.26), channel_id=1, source_target_pairs={{0,1},{1,0},{2,3},{3,2},{4,5},{5,4},{6,7},{7,6},{8,9},{9,8},{10,11... | collective-permute-start | bytes 1572872 | tf_op jit(solution)/shard_map/ppermute | solution.py:294
  3.0 6.5 %collective-permute-start = (bf16[512,512]{1,0:T(8,128)(2,1)S(1)}, bf16[512,512]{1,0:T(8,128)(2,1)S(1)}, u32[]{:S(2)}, u32[]{:S(2)}) collective-permute-start(bf16[512,512]{1,0:T(8,128)(2,1)S(1)} %get-tuple-element.24), channel_id=1, source_target_pairs={{0,1},{1,0},{2,3},{3,2},{4,5},{5,4},{6,7},{7,6},{8,9},{9,8},{10,11... | collective-permute-start | bytes 1572872 | tf_op jit(solution)/shard_map/ppermute | solution.py:294
  5.5 11.7 %collective-permute-start.6 = (bf16[512,512]{1,0:T(8,128)(2,1)S(1)}, bf16[512,512]{1,0:T(8,128)(2,1)S(1)}, u32[]{:S(2)}, u32[]{:S(2)}) collective-permute-start(bf16[512,512]{1,0:T(8,128)(2,1)S(1)} %shard_map.40.refs_0_), channel_id=1, source_target_pairs={{0,2},{1,7},{8,10},{9,15},{16,18},{17,23},{24,26},{25,31},{32,34},... | collective-permute-start | bytes 1572872 | tf_op jit(solution)/shard_map/ppermute | solution.py:296
  10.1 18.3 %collective-permute-start.1 = (bf16[512,512]{1,0:T(8,128)(2,1)S(1)}, bf16[512,512]{1,0:T(8,128)(2,1)S(1)}, u32[]{:S(2)}, u32[]{:S(2)}) collective-permute-start(bf16[512,512]{1,0:T(8,128)(2,1)S(1)} %shard_map.38.refs_0_), channel_id=1, source_target_pairs={{0,2},{1,7},{8,10},{9,15},{16,18},{17,23},{24,26},{25,31},{32,34},... | collective-permute-start | bytes 1572872 | tf_op jit(solution)/shard_map/ppermute | solution.py:296
  11.4 17.7 %collective-permute-start.7 = (bf16[512,512]{1,0:T(8,128)(2,1)S(1)}, bf16[512,512]{1,0:T(8,128)(2,1)S(1)}, u32[]{:S(2)}, u32[]{:S(2)}) collective-permute-start(bf16[512,512]{1,0:T(8,128)(2,1)S(1)} %shard_map.40.refs_0_), channel_id=1, source_target_pairs={{0,6},{1,3},{8,14},{9,11},{16,22},{17,19},{24,30},{25,27},{32,38},... | collective-permute-start | bytes 1572872 | tf_op jit(solution)/shard_map/ppermute | solution.py:297
  17.2 11.9 %collective-permute-start.8 = (bf16[512,512]{1,0:T(8,128)(2,1)S(1)}, bf16[512,512]{1,0:T(8,128)(2,1)S(1)}, u32[]{:S(2)}, u32[]{:S(2)}) collective-permute-start(bf16[512,512]{1,0:T(8,128)(2,1)S(1)} %collective-permute-done.6.refs_1_), channel_id=1, source_target_pairs={{2,4},{7,5},{10,12},{15,13},{18,20},{23,21},{26,28},{31,29},{34,36... | collective-permute-start | bytes 1572872 | tf_op jit(solution)/shard_map/ppermute | solution.py:298
  17.8 16.4 %collective-permute-start.2 = (bf16[512,512]{1,0:T(8,128)(2,1)S(1)}, bf16[512,512]{1,0:T(8,128)(2,1)S(1)}, u32[]{:S(2)}, u32[]{:S(2)}) collective-permute-start(bf16[512,512]{1,0:T(8,128)(2,1)S(1)} %shard_map.38.refs_0_), channel_id=1, source_target_pairs={{0,6},{1,3},{8,14},{9,11},{16,22},{17,19},{24,30},{25,27},{32,38},... | collective-permute-start | bytes 1572872 | tf_op jit(solution)/shard_map/ppermute | solution.py:297
  28.4 5.8 %collective-permute-start.3 = (bf16[512,512]{1,0:T(8,128)(2,1)S(1)}, bf16[512,512]{1,0:T(8,128)(2,1)S(1)}, u32[]{:S(2)}, u32[]{:S(2)}) collective-permute-start(bf16[512,512]{1,0:T(8,128)(2,1)S(1)} %collective-permute-done.1.refs_1_), channel_id=1, source_target_pairs={{2,4},{7,5},{10,12},{15,13},{18,20},{23,21},{26,28},{31,29},{34,36... | collective-permute-start | bytes 1572872 | tf_op jit(solution)/shard_map/ppermute | solution.py:298
  29.1 5.8 %copy-start = (bf16[1024,2048]{1,0:T(8,128)(2,1)S(1)}, bf16[1024,2048]{1,0:T(8,128)(2,1)}, u32[]{:S(2)}) copy-start(bf16[1024,2048]{1,0:T(8,128)(2,1)} %density.1) | copy-start | bytes 12582916
  29.7 7.0 %collective-permute-start.9 = (bf16[512,512]{1,0:T(8,128)(2,1)S(1)}, bf16[512,512]{1,0:T(8,128)(2,1)S(1)}, u32[]{:S(2)}, u32[]{:S(2)}) collective-permute-start(bf16[512,512]{1,0:T(8,128)(2,1)S(1)} %shard_map.41.own_b), channel_id=1, source_target_pairs={{0,1},{1,0},{2,3},{3,2},{4,5},{5,4},{6,7},{7,6},{8,9},{9,8},{10,11... | collective-permute-start | bytes 1572872 | tf_op jit(solution)/shard_map/ppermute | solution.py:276
  34.8 2.0 %collective-permute-start.4 = (bf16[512,512]{1,0:T(8,128)(2,1)S(1)}, bf16[512,512]{1,0:T(8,128)(2,1)S(1)}, u32[]{:S(2)}, u32[]{:S(2)}) collective-permute-start(bf16[512,512]{1,0:T(8,128)(2,1)S(1)} %shard_map.39.own_a), channel_id=1, source_target_pairs={{0,1},{1,0},{2,3},{3,2},{4,5},{5,4},{6,7},{7,6},{8,9},{9,8},{10,11... | collective-permute-start | bytes 1572872 | tf_op jit(solution)/shard_map/ppermute | solution.py:276
  39.1 9.6 %collective-permute-start.12 = (s16[128,2176]{1,0:T(8,128)(2,1)S(1)}, s16[128,2176]{1,0:T(8,128)(2,1)S(1)}, u32[]{:S(2)}, u32[]{:S(2)}) collective-permute-start(s16[128,2176]{1,0:T(8,128)(2,1)S(1)} %get-tuple-element.28), channel_id=1, source_target_pairs={{0,32},{1,9},{2,34},{3,11},{4,36},{5,13},{6,38},{7,15},{8,40},{9,1... | collective-permute-start | bytes 1671176 | tf_op jit(solution)/shard_map/ppermute | solution.py:264
  40.7 12.0 %collective-permute-start.10 = (s16[128,2176]{1,0:T(8,128)(2,1)S(1)}, s16[128,2176]{1,0:T(8,128)(2,1)S(1)}, u32[]{:S(2)}, u32[]{:S(2)}) collective-permute-start(s16[128,2176]{1,0:T(8,128)(2,1)S(1)} %get-tuple-element.27), channel_id=1, source_target_pairs={{0,96},{1,25},{2,98},{3,27},{4,100},{5,29},{6,102},{7,31},{8,104},... | collective-permute-start | bytes 1671176 | tf_op jit(solution)/shard_map/ppermute | solution.py:264
  49.8 16.8 %collective-permute-start.13 = (s16[256,2176]{1,0:T(8,128)(2,1)S(1)}, s16[256,2176]{1,0:T(8,128)(2,1)S(1)}, u32[]{:S(2)}, u32[]{:S(2)}) collective-permute-start(s16[256,2176]{1,0:T(8,128)(2,1)S(1)} %shard_map.48), channel_id=1, source_target_pairs={{0,96},{1,25},{2,98},{3,27},{4,100},{5,29},{6,102},{7,31},{8,104},... | collective-permute-start | bytes 3342344 | tf_op jit(solution)/shard_map/ppermute | solution.py:264
  53.8 15.6 %collective-permute-start.11 = (s16[256,2176]{1,0:T(8,128)(2,1)S(1)}, s16[256,2176]{1,0:T(8,128)(2,1)S(1)}, u32[]{:S(2)}, u32[]{:S(2)}) collective-permute-start(s16[256,2176]{1,0:T(8,128)(2,1)S(1)} %shard_map.46), channel_id=1, source_target_pairs={{0,32},{1,9},{2,34},{3,11},{4,36},{5,13},{6,38},{7,15},{8,40},{9,1... | collective-permute-start | bytes 3342344 | tf_op jit(solution)/shard_map/ppermute | solution.py:264
  70.8 6.6 %collective-permute-start.14 = (s16[64,2176]{1,0:T(8,128)(2,1)S(1)}, s16[64,2176]{1,0:T(8,128)(2,1)S(1)}, u32[]{:S(2)}, u32[]{:S(2)}) collective-permute-start(s16[64,2176]{1,0:T(8,128)(2,1)S(1)} %get-tuple-element.30), channel_id=1, source_target_pairs={{0,8},{1,33},{2,10},{3,35},{4,12},{5,37},{6,14},{7,39},{8,0},{9,41... | collective-permute-start | bytes 835592 | tf_op jit(solution)/shard_map/ppermute | solution.py:264
  72.4 10.5 %collective-permute-start.15 = (s16[64,2176]{1,0:T(8,128)(2,1)S(1)}, s16[64,2176]{1,0:T(8,128)(2,1)S(1)}, u32[]{:S(2)}, u32[]{:S(2)}) collective-permute-start(s16[64,2176]{1,0:T(8,128)(2,1)S(1)} %get-tuple-element.31), channel_id=1, source_target_pairs={{0,16},{1,65},{2,18},{3,67},{4,20},{5,69},{6,22},{7,71},{8,24},{9,... | collective-permute-start | bytes 835592 | tf_op jit(solution)/shard_map/ppermute | solution.py:264
  75.3 10.5 %collective-permute-start.16 = (s16[64,2176]{1,0:T(8,128)(2,1)S(1)}, s16[64,2176]{1,0:T(8,128)(2,1)S(1)}, u32[]{:S(2)}, u32[]{:S(2)}) collective-permute-start(s16[64,2176]{1,0:T(8,128)(2,1)S(1)} %get-tuple-element.32), channel_id=1, source_target_pairs={{0,24},{1,97},{2,26},{3,99},{4,28},{5,101},{6,30},{7,103},{8,16},{... | collective-permute-start | bytes 835592 | tf_op jit(solution)/shard_map/ppermute | solution.py:264
  86.2 6.6 %collective-permute-start.17 = (s16[64,2176]{1,0:T(8,128)(2,1)S(1)}, s16[64,2176]{1,0:T(8,128)(2,1)S(1)}, u32[]{:S(2)}, u32[]{:S(2)}) collective-permute-start(s16[64,2176]{1,0:T(8,128)(2,1)S(1)} %shard_map.50.refs_0_), channel_id=1, source_target_pairs={{0,8},{1,33},{2,10},{3,35},{4,12},{5,37},{6,14},{7,39},{8,0},{9,41... | collective-permute-start | bytes 835592 | tf_op jit(solution)/shard_map/ppermute | solution.py:264
  86.3 9.3 %collective-permute-start.18 = (s16[64,2176]{1,0:T(8,128)(2,1)S(1)}, s16[64,2176]{1,0:T(8,128)(2,1)S(1)}, u32[]{:S(2)}, u32[]{:S(2)}) collective-permute-start(s16[64,2176]{1,0:T(8,128)(2,1)S(1)} %shard_map.50.refs_0_), channel_id=1, source_target_pairs={{0,16},{1,65},{2,18},{3,67},{4,20},{5,69},{6,22},{7,71},{8,24},{9,... | collective-permute-start | bytes 835592 | tf_op jit(solution)/shard_map/ppermute | solution.py:264
  87.9 12.0 %collective-permute-start.19 = (s16[64,2176]{1,0:T(8,128)(2,1)S(1)}, s16[64,2176]{1,0:T(8,128)(2,1)S(1)}, u32[]{:S(2)}, u32[]{:S(2)}) collective-permute-start(s16[64,2176]{1,0:T(8,128)(2,1)S(1)} %shard_map.50.refs_0_), channel_id=1, source_target_pairs={{0,24},{1,97},{2,26},{3,99},{4,28},{5,101},{6,30},{7,103},{8,16},{... | collective-permute-start | bytes 835592 | tf_op jit(solution)/shard_map/ppermute | solution.py:264
  100.0 16.8 %collective-permute-start.21 = (s16[256,2176]{1,0:T(8,128)(2,1)S(1)}, s16[256,2176]{1,0:T(8,128)(2,1)S(1)}, u32[]{:S(2)}, u32[]{:S(2)}) collective-permute-start(s16[256,2176]{1,0:T(8,128)(2,1)S(1)} %shard_map.51.refs_0_), channel_id=1, source_target_pairs={{0,96},{1,25},{2,98},{3,27},{4,100},{5,29},{6,102},{7,31},{8,104},... | collective-permute-start | bytes 3342344 | tf_op jit(solution)/shard_map/ppermute | solution.py:264
  100.1 17.4 %collective-permute-start.20 = (s16[256,2176]{1,0:T(8,128)(2,1)S(1)}, s16[256,2176]{1,0:T(8,128)(2,1)S(1)}, u32[]{:S(2)}, u32[]{:S(2)}) collective-permute-start(s16[256,2176]{1,0:T(8,128)(2,1)S(1)} %shard_map.51.refs_0_), channel_id=1, source_target_pairs={{0,32},{1,9},{2,34},{3,11},{4,36},{5,13},{6,38},{7,15},{8,40},{9,1... | collective-permute-start | bytes 3342344 | tf_op jit(solution)/shard_map/ppermute | solution.py:264
  117.4 9.6 %collective-permute-start.23 = (s16[128,2176]{1,0:T(8,128)(2,1)S(1)}, s16[128,2176]{1,0:T(8,128)(2,1)S(1)}, u32[]{:S(2)}, u32[]{:S(2)}) collective-permute-start(s16[128,2176]{1,0:T(8,128)(2,1)S(1)} %shard_map.53), channel_id=1, source_target_pairs={{0,32},{1,9},{2,34},{3,11},{4,36},{5,13},{6,38},{7,15},{8,40},{9,1... | collective-permute-start | bytes 1671176 | tf_op jit(solution)/shard_map/ppermute | solution.py:264
  118.1 10.8 %collective-permute-start.24 = (s16[128,2176]{1,0:T(8,128)(2,1)S(1)}, s16[128,2176]{1,0:T(8,128)(2,1)S(1)}, u32[]{:S(2)}, u32[]{:S(2)}) collective-permute-start(s16[128,2176]{1,0:T(8,128)(2,1)S(1)} %shard_map.54), channel_id=1, source_target_pairs={{0,96},{1,25},{2,98},{3,27},{4,100},{5,29},{6,102},{7,31},{8,104},... | collective-permute-start | bytes 1671176 | tf_op jit(solution)/shard_map/ppermute | solution.py:264
  123.8 9.8 %collective-permute-start.22 = (f32[256,1024]{1,0:T(8,128)S(1)}, f32[256,1024]{1,0:T(8,128)S(1)}, u32[]{:S(2)}, u32[]{:S(2)}) collective-permute-start(f32[256,1024]{1,0:T(8,128)S(1)} %get-tuple-element.34), channel_id=1, source_target_pairs={{0,1},{1,0},{2,3},{3,2},{4,5},{5,4},{6,7},{7,6},{8,9},{9,8},{10,11... | collective-permute-start | bytes 3145736 | tf_op jit(solution)/shard_map/ppermute | solution.py:276
  133.5 2.7 %collective-permute-start.25 = (f32[256,1024]{1,0:T(8,128)S(1)}, f32[256,1024]{1,0:T(8,128)S(1)}, u32[]{:S(2)}, u32[]{:S(2)}) collective-permute-start(f32[256,1024]{1,0:T(8,128)S(1)} %get-tuple-element.36), channel_id=1, source_target_pairs={{0,1},{1,0},{2,3},{3,2},{4,5},{5,4},{6,7},{7,6},{8,9},{9,8},{10,11... | collective-permute-start | bytes 3145736 | tf_op jit(solution)/shard_map/ppermute | solution.py:276
  137.5 15.7 %collective-permute-start.26 = (s16[128,1152]{1,0:T(8,128)(2,1)S(1)}, s16[128,1152]{1,0:T(8,128)(2,1)S(1)}, u32[]{:S(2)}, u32[]{:S(2)}) collective-permute-start(s16[128,1152]{1,0:T(8,128)(2,1)S(1)} %get-tuple-element.38), channel_id=1, source_target_pairs={{0,2},{1,3},{2,4},{3,5},{4,6},{5,7},{6,0},{7,1},{8,10},{9,11},{10,... | collective-permute-start | bytes 884744 | tf_op jit(solution)/shard_map/ppermute | solution.py:264
  141.8 13.5 %collective-permute-start.27 = (s16[128,1152]{1,0:T(8,128)(2,1)S(1)}, s16[128,1152]{1,0:T(8,128)(2,1)S(1)}, u32[]{:S(2)}, u32[]{:S(2)}) collective-permute-start(s16[128,1152]{1,0:T(8,128)(2,1)S(1)} %get-tuple-element.39), channel_id=1, source_target_pairs={{0,6},{1,7},{2,0},{3,1},{4,2},{5,3},{6,4},{7,5},{8,14},{9,15},{10,... | collective-permute-start | bytes 884744 | tf_op jit(solution)/shard_map/ppermute | solution.py:264
  145.9 15.2 %collective-permute-start.28 = (s16[128,1152]{1,0:T(8,128)(2,1)S(1)}, s16[128,1152]{1,0:T(8,128)(2,1)S(1)}, u32[]{:S(2)}, u32[]{:S(2)}) collective-permute-start(s16[128,1152]{1,0:T(8,128)(2,1)S(1)} %get-tuple-element.40), channel_id=1, source_target_pairs={{0,4},{1,5},{2,6},{3,7},{4,0},{5,1},{6,2},{7,3},{8,12},{9,13},{10,... | collective-permute-start | bytes 884744 | tf_op jit(solution)/shard_map/ppermute | solution.py:264
